TPU v7x, 32 devices: a whole 2x2x4 slice. The times are simulated.
32 devices in a mesh: dp: 2 (over core), sp: 16 (over z, y, x).
Axes of the slice: x: 2, y: 2, z: 4, core: 2. Of those that a mesh axis runs over, the one named last changes fastest.
Arguments:
- frames: bfloat16 [32, 256, 1152], P(('dp', 'sp')), may hold values from -6 to 6
- cotangent: bfloat16 [32, 256, 1152], P(('dp', 'sp')), may hold values from -6 to 6
- aspect: int32 [2], P('dp'), may hold values from 0 to 2
- table_index: int32 [2], P('dp'), may hold values from 0 to 3
- noise_level: int32 [2], P('dp'), may hold values from 0 to 999
- labels: int32 [2], P('dp'), may hold values from 0 to 100
- row_table: bfloat16 [4, 32, 1152], replicated, may hold values from -3 to 3
- column_table: bfloat16 [4, 32, 1152], replicated, may hold values from -3 to 3
- class_table: bfloat16 [101, 1152], replicated, may hold values from -6 to 6
- time_first: bfloat16 [256, 1152], replicated, may hold values from -0.5 to 0.5
- time_first_bias: bfloat16 [1152], replicated, may hold values from -1.75 to 1.75
- time_second: bfloat16 [1152, 1152], replicated, may hold values from -0.1875 to 0.1875
- time_second_bias: bfloat16 [1152], replicated, may hold values from -1.75 to 1.75
- modulate: bfloat16 [1152, 13824], P(None, 'sp'), may hold values from -0.1875 to 0.1875
- modulate_bias: bfloat16 [13824], P('sp'), may hold values from -1.75 to 1.75
- spatial_input: bfloat16 [1152, 3456], P('sp'), may hold values from -0.1875 to 0.1875
- spatial_input_bias: bfloat16 [2304], P('sp'), may hold values from -1.75 to 1.75
- spatial_output: bfloat16 [1152, 1152], P('sp'), may hold values from -2 to 2
- spatial_output_bias: bfloat16 [1152], P('sp'), may hold values from -1.75 to 1.75
- spatial_expand: bfloat16 [1152, 4608], P('sp'), may hold values from -0.1875 to 0.1875
- spatial_expand_bias: bfloat16 [4608], P('sp'), may hold values from -1.75 to 1.75
- spatial_reduce: bfloat16 [1152, 4608], P('sp'), may hold values from -0.09375 to 0.09375
- spatial_reduce_bias: bfloat16 [1152], P('sp'), may hold values from -1.75 to 1.75
- temporal_input: bfloat16 [1152, 3456], P('sp'), may hold values from -0.1875 to 0.1875
- temporal_input_bias: bfloat16 [2304], P('sp'), may hold values from -1.75 to 1.75
- temporal_output: bfloat16 [1152, 1152], P('sp'), may hold values from -0.75 to 0.75
- temporal_output_bias: bfloat16 [1152], P('sp'), may hold values from -1.75 to 1.75
- temporal_expand: bfloat16 [1152, 4608], P('sp'), may hold values from -0.1875 to 0.1875
- temporal_expand_bias: bfloat16 [4608], P('sp'), may hold values from -1.75 to 1.75
- temporal_reduce: bfloat16 [1152, 4608], P('sp'), may hold values from -0.09375 to 0.09375
- temporal_reduce_bias: bfloat16 [1152], P('sp'), may hold values from -3 to 3
Outputs:
- activations: bfloat16 [32, 256, 1152], P(('dp', 'sp'))
- input_grad: float32 [32, 256, 1152], P(('dp', 'sp'))
- row_table_grad: float32 [4, 32, 1152], P(None, None, 'sp')
- column_table_grad: float32 [4, 32, 1152], P(None, None, 'sp')
- class_table_grad: float32 [101, 1152], replicated
- time_first_grad: float32 [256, 1152], replicated
- time_first_bias_grad: float32 [1152], replicated
- time_second_grad: float32 [1152, 1152], replicated
- time_second_bias_grad: float32 [1152], replicated
- modulate_grad: float32 [1152, 13824], P(None, 'sp')
- modulate_bias_grad: float32 [13824], P('sp')
- spatial_input_grad: float32 [1152, 3456], P('sp')
- spatial_input_bias_grad: float32 [2304], P('sp')
- spatial_output_grad: float32 [1152, 1152], P('sp')
- spatial_output_bias_grad: float32 [1152], P('sp')
- spatial_expand_grad: float32 [1152, 4608], P('sp')
- spatial_expand_bias_grad: float32 [4608], P('sp')
- spatial_reduce_grad: float32 [1152, 4608], P('sp')
- spatial_reduce_bias_grad: float32 [1152], P('sp')
- temporal_input_grad: float32 [1152, 3456], P('sp')
- temporal_input_bias_grad: float32 [2304], P('sp')
- temporal_output_grad: float32 [1152, 1152], P('sp')
- temporal_output_bias_grad: float32 [1152], P('sp')
- temporal_expand_grad: float32 [1152, 4608], P('sp')
- temporal_expand_bias_grad: float32 [4608], P('sp')
- temporal_reduce_grad: float32 [1152, 4608], P('sp')
- temporal_reduce_bias_grad: float32 [1152], P('sp')
Inputs may be any that keep to these rules, and one draw needn't show every extreme that they name: `aspect`: 0: 16 rows of 16 patches; 1: 8 rows of 32; 2: 32 rows of 8.
All inputs are finite; a program needn't handle non-finite values.
Results may differ from a plain program's by a relative error of at most 0.023.
Values may be sent and summed in bfloat16 or wider, within the bound.
No kernel may reach another device: no remote copies, remote signals or barrier semaphores. Data moves between devices by JAX's collectives and lax.ppermute only.
A program may use at most 448 MiB of HBM per device.

v0:
```python
from functools import partial
import math

import jax
import jax.numpy as jnp
from jax import lax
from jax.sharding import PartitionSpec as P

HEADS = 16
HDIM = 72
FREQ = 256
SIDE = 16
FRAMES = 16


EPSILON = 1e-06
HIGHEST = lax.Precision.HIGHEST
SPACE_FORMS = ("bqhd,bkhd->bhqk", "bhqk,bkhd->bqhd", "bhqk,bqhd->bkhd")
TIME_FORMS = ("cqphd,ckphd->cphqk", "cphqk,ckphd->cqphd", "cphqk,cqphd->ckphd")


def layer_norm(values):
    center = values - jnp.mean(values, axis=-1, keepdims=True)
    inverse = lax.rsqrt(jnp.mean(center * center, axis=-1, keepdims=True) + EPSILON)
    return (center * inverse, inverse)


def norm_back(gradient, normed, inverse):
    mean_grad = jnp.mean(gradient, axis=-1, keepdims=True)
    mean_cross = jnp.mean(gradient * normed, axis=-1, keepdims=True)
    return inverse * (gradient - mean_grad - normed * mean_cross)


def split_heads(values):
    return values.reshape(values.shape[:-1] + (HEADS, HDIM))


def merge_heads(values):
    return values.reshape(values.shape[:-2] + (values.shape[-2] * values.shape[-1],))


def project(left_rows, weight):
    return jnp.dot(left_rows, weight, preferred_element_type=jnp.float32)


def project_rows(left_rows, weight):
    return lax.dot_general(
        left_rows,
        weight,
        (((left_rows.ndim - 1,), (1,)), ((), ())),
        preferred_element_type=jnp.float32,
    )


def contract_first(left_rows, right_rows, precision=None):
    return lax.dot_general(
        left_rows,
        right_rows,
        (((0,), (0,)), ((), ())),
        preferred_element_type=jnp.float32,
        precision=precision,
    )


def attend(query_rows, key_rows, value_rows, forms):
    scale = HDIM ** (-0.5)
    scores = (
        jnp.einsum(
            forms[0],
            split_heads(query_rows),
            split_heads(key_rows),
            preferred_element_type=jnp.float32,
        )
        * scale
    )
    row_max = jnp.max(scores, axis=-1, keepdims=True)
    exponent = jnp.exp(scores - row_max)
    row_total = jnp.sum(exponent, axis=-1, keepdims=True)
    attn_probs = (exponent / row_total).astype(jnp.bfloat16)
    mixed = jnp.einsum(
        forms[1], attn_probs, split_heads(value_rows), preferred_element_type=jnp.float32
    )
    return (merge_heads(mixed).astype(jnp.bfloat16), row_max + jnp.log(row_total))


def attend_back(query_rows, key_rows, value_rows, logsum, grad_out, forms):
    scale = HDIM ** (-0.5)
    query_heads = split_heads(query_rows)
    key_heads = split_heads(key_rows)
    grad_heads = split_heads(grad_out)
    scores = (
        jnp.einsum(forms[0], query_heads, key_heads, preferred_element_type=jnp.float32) * scale
    )
    attn_probs = jnp.exp(scores - logsum)
    grad_probs = jnp.einsum(
        forms[0], grad_heads, split_heads(value_rows), preferred_element_type=jnp.float32
    )
    inner = jnp.sum(attn_probs * grad_probs, axis=-1, keepdims=True)
    grad_scores = (attn_probs * (grad_probs - inner)).astype(jnp.bfloat16)
    grad_query = (
        jnp.einsum(forms[1], grad_scores, key_heads, preferred_element_type=jnp.float32) * scale
    )
    grad_key = (
        jnp.einsum(forms[2], grad_scores, query_heads, preferred_element_type=jnp.float32) * scale
    )
    grad_value = jnp.einsum(
        forms[2], attn_probs.astype(jnp.bfloat16), grad_heads, preferred_element_type=jnp.float32
    )
    return (merge_heads(grad_query), merge_heads(grad_key), merge_heads(grad_value))


def block_forward(inputs, modulation, weights, forms):
    w_input, input_bias, w_output, output_bias, w_expand, expand_bias, w_reduce, reduce_bias = (
        weights
    )
    width_model = inputs.shape[-1]
    shift_att, scale_att, gate_att, shift_mlp, scale_mlp, gate_mlp = jnp.split(
        modulation, 6, axis=-1
    )
    normed_att, inverse_att = layer_norm(inputs)
    attn_input = (normed_att * (1.0 + scale_att) + shift_att).astype(jnp.bfloat16)
    projected = project(attn_input, w_input)
    bias_qv = input_bias.astype(jnp.float32)
    query_rows = (projected[..., :width_model] + bias_qv[:width_model]).astype(jnp.bfloat16)
    key_rows = projected[..., width_model : 2 * width_model].astype(jnp.bfloat16)
    value_rows = (projected[..., 2 * width_model :] + bias_qv[width_model:]).astype(jnp.bfloat16)
    attended, logsum = attend(query_rows, key_rows, value_rows, forms)
    branch = project_rows(attended, w_output) + output_bias.astype(jnp.float32)
    hidden = inputs + gate_att * branch
    normed_mlp, inverse_mlp = layer_norm(hidden)
    mlp_input = (normed_mlp * (1.0 + scale_mlp) + shift_mlp).astype(jnp.bfloat16)
    expanded = project(mlp_input, w_expand) + expand_bias.astype(jnp.float32)
    activated = jax.nn.gelu(expanded, approximate=True).astype(jnp.bfloat16)
    reduced = project_rows(activated, w_reduce) + reduce_bias.astype(jnp.float32)
    output = hidden + gate_mlp * reduced
    kept = (
        normed_att,
        inverse_att,
        attn_input,
        query_rows,
        key_rows,
        value_rows,
        attended,
        logsum,
        branch,
        normed_mlp,
        inverse_mlp,
        mlp_input,
        expanded,
        activated,
        reduced,
    )
    return (output, kept)


def token_sum(values):
    return jnp.sum(values.astype(jnp.float32).reshape(-1, values.shape[-1]), axis=0)


def block_backward(gradient, kept, modulation, weights, forms, clip_sum):
    w_input, input_bias, w_output, output_bias, w_expand, expand_bias, w_reduce, reduce_bias = (
        weights
    )
    (
        normed_att,
        inverse_att,
        attn_input,
        query_rows,
        key_rows,
        value_rows,
        attended,
        logsum,
        branch,
        normed_mlp,
        inverse_mlp,
        mlp_input,
        expanded,
        activated,
        reduced,
    ) = kept
    shift_att, scale_att, gate_att, shift_mlp, scale_mlp, gate_mlp = jnp.split(
        modulation, 6, axis=-1
    )
    grad_gate_mlp = clip_sum(gradient * reduced)
    grad_reduced = (gradient * gate_mlp).astype(jnp.bfloat16)
    grad_activated = project(grad_reduced, w_reduce)
    gelu_back = jax.vjp(partial(jax.nn.gelu, approximate=True), expanded)[1]
    grad_expanded = gelu_back(grad_activated)[0].astype(jnp.bfloat16)
    grad_mlp_input = project_rows(grad_expanded, w_expand)
    grad_scale_mlp = clip_sum(grad_mlp_input * normed_mlp)
    grad_shift_mlp = clip_sum(grad_mlp_input)
    grad_hidden = gradient + norm_back(grad_mlp_input * (1.0 + scale_mlp), normed_mlp, inverse_mlp)
    grad_gate_att = clip_sum(grad_hidden * branch)
    grad_branch = (grad_hidden * gate_att).astype(jnp.bfloat16)
    grad_attended = project(grad_branch, w_output).astype(jnp.bfloat16)
    grad_query, grad_key, grad_value = attend_back(
        query_rows, key_rows, value_rows, logsum, grad_attended, forms
    )
    grad_query = grad_query.astype(jnp.bfloat16)
    grad_key = grad_key.astype(jnp.bfloat16)
    grad_value = grad_value.astype(jnp.bfloat16)
    grad_projected = jnp.concatenate([grad_query, grad_key, grad_value], axis=-1)
    grad_attn_input = project_rows(grad_projected, w_input)
    grad_scale_att = clip_sum(grad_attn_input * normed_att)
    grad_shift_att = clip_sum(grad_attn_input)
    grad_inputs = grad_hidden + norm_back(
        grad_attn_input * (1.0 + scale_att), normed_att, inverse_att
    )
    grad_mod = jnp.concatenate(
        [
            grad_shift_att,
            grad_scale_att,
            grad_gate_att,
            grad_shift_mlp,
            grad_scale_mlp,
            grad_gate_mlp,
        ],
        axis=-1,
    )
    bias_grads = (
        jnp.concatenate([token_sum(grad_query), token_sum(grad_value)]),
        token_sum(grad_branch),
        token_sum(grad_expanded),
        token_sum(grad_reduced),
    )
    terms = tuple(
        (
            values.reshape(-1, values.shape[-1])
            for values in (
                attn_input,
                grad_projected,
                grad_branch,
                attended,
                mlp_input,
                grad_expanded,
                grad_reduced,
                activated,
            )
        )
    )
    return (grad_inputs, grad_mod, bias_grads, terms)


def fetch_weights(
    w_input, input_bias, w_output, output_bias, w_expand, expand_bias, w_reduce, reduce_bias
):
    return (
        lax.all_gather(w_input, "sp", axis=0, tiled=True),
        lax.all_gather(input_bias, "sp", axis=0, tiled=True),
        lax.all_gather(w_output, "sp", axis=0, tiled=True),
        lax.all_gather(output_bias, "sp", axis=0, tiled=True),
        lax.all_gather(w_expand, "sp", axis=0, tiled=True),
        lax.all_gather(expand_bias, "sp", axis=0, tiled=True),
        lax.all_gather(w_reduce, "sp", axis=0, tiled=True),
        lax.all_gather(reduce_bias, "sp", axis=0, tiled=True),
    )


def term_pairs(terms):
    return ((terms[0], terms[1]), (terms[2], terms[3]), (terms[4], terms[5]), (terms[6], terms[7]))


def product_rows(pairs):
    parts = [contract_first(left_rows, right_rows) for left_rows, right_rows in pairs]
    return jnp.concatenate(parts, axis=1)


def split_products(summed, pairs):
    bounds = []
    offset = 0
    for left_rows, right_rows in pairs[:-1]:
        offset = offset + right_rows.shape[1]
        bounds.append(offset)
    return tuple(jnp.split(summed, bounds, axis=1))


def weight_grads(terms):
    pairs = term_pairs(terms)
    summed = lax.psum_scatter(product_rows(pairs), "sp", scatter_dimension=0, tiled=True)
    return split_products(summed, pairs)


def to_positions(values):
    return lax.all_to_all(values, "sp", split_axis=1, concat_axis=0, tiled=True)


def to_frames(values):
    return lax.all_to_all(values, "sp", split_axis=0, concat_axis=1, tiled=True)


def sum_spatial(values):
    return jnp.sum(values, axis=(0, 1))


def sum_temporal(values):
    return jnp.sum(values, axis=(1, 2))


def per_device(
    frames,
    cotangent,
    aspect,
    table_index,
    noise_level,
    labels,
    row_table,
    column_table,
    class_table,
    time_first,
    time_first_bias,
    time_second,
    time_second_bias,
    modulate,
    modulate_bias,
    spatial_input,
    spatial_input_bias,
    spatial_output,
    spatial_output_bias,
    spatial_expand,
    spatial_expand_bias,
    spatial_reduce,
    spatial_reduce_bias,
    temporal_input,
    temporal_input_bias,
    temporal_output,
    temporal_output_bias,
    temporal_expand,
    temporal_expand_bias,
    temporal_reduce,
    temporal_reduce_bias,
):
    device_rank = lax.axis_index("sp")
    frame_count, patches, width_model = frames.shape
    clips_here = aspect.shape[0]
    clip_here = device_rank * frame_count // FRAMES
    clip_pick = lax.iota(jnp.int32, clips_here) == clip_here
    half = FREQ // 2
    frequency = jnp.exp(-math.log(10000.0) * jnp.arange(half, dtype=jnp.float32) / half)
    angles = noise_level.astype(jnp.float32)[:, None] * frequency[None, :]
    embedding = jnp.concatenate([jnp.cos(angles), jnp.sin(angles)], axis=-1).astype(jnp.bfloat16)
    time_hidden = project(embedding, time_first) + time_first_bias.astype(jnp.float32)
    time_act = jax.nn.silu(time_hidden).astype(jnp.bfloat16)
    class_pick = (labels[:, None] == lax.iota(jnp.int32, class_table.shape[0])[None, :]).astype(
        jnp.bfloat16
    )
    condition = (
        project(time_act, time_second)
        + time_second_bias.astype(jnp.float32)
        + project(class_pick, class_table)
    )
    condition_act = jax.nn.silu(condition).astype(jnp.bfloat16)
    mod_cols = project(condition_act, modulate) + modulate_bias.astype(jnp.float32)
    modulation = lax.all_gather(mod_cols, "sp", axis=1, tiled=True)
    mod_here = jnp.sum(jnp.where(clip_pick[:, None], modulation, 0.0), axis=0)
    spatial_mod = mod_here[: 6 * width_model][None, None, :]
    temporal_mod = modulation[:, 6 * width_model :][:, None, None, :]
    aspect_here = jnp.sum(jnp.where(clip_pick, aspect, 0))
    table_here = jnp.sum(jnp.where(clip_pick, table_index, 0))
    row_width = jnp.where(aspect_here == 0, SIDE, jnp.where(aspect_here == 1, 2 * SIDE, SIDE // 2))
    patch_ids = lax.iota(jnp.int32, patches)
    grid_ids = lax.iota(jnp.int32, 2 * SIDE)
    row_pick = (patch_ids[:, None] // row_width == grid_ids[None, :]).astype(jnp.bfloat16)
    col_pick = (patch_ids[:, None] % row_width == grid_ids[None, :]).astype(jnp.bfloat16)
    row_chosen = lax.dynamic_index_in_dim(row_table, table_here, 0, keepdims=False)
    col_chosen = lax.dynamic_index_in_dim(column_table, table_here, 0, keepdims=False)
    positions = project(row_pick, row_chosen) + project(col_pick, col_chosen)
    block_input = frames.astype(jnp.float32) + positions[None]
    spatial_weights = fetch_weights(
        spatial_input,
        spatial_input_bias,
        spatial_output,
        spatial_output_bias,
        spatial_expand,
        spatial_expand_bias,
        spatial_reduce,
        spatial_reduce_bias,
    )
    spatial_out, spatial_kept = block_forward(
        block_input, spatial_mod, spatial_weights, SPACE_FORMS
    )
    between = to_positions(spatial_out.astype(jnp.bfloat16))
    local_patches = between.shape[1]
    between = between.reshape(clips_here, FRAMES, local_patches, width_model)
    temporal_weights = fetch_weights(
        temporal_input,
        temporal_input_bias,
        temporal_output,
        temporal_output_bias,
        temporal_expand,
        temporal_expand_bias,
        temporal_reduce,
        temporal_reduce_bias,
    )
    temporal_out, temporal_kept = block_forward(
        between.astype(jnp.float32), temporal_mod, temporal_weights, TIME_FORMS
    )
    activations = to_frames(
        temporal_out.astype(jnp.bfloat16).reshape(clips_here * FRAMES, local_patches, width_model)
    )
    grad_after = to_positions(cotangent).reshape(clips_here, FRAMES, local_patches, width_model)
    temporal_back = fetch_weights(
        temporal_input,
        temporal_input_bias,
        temporal_output,
        temporal_output_bias,
        temporal_expand,
        temporal_expand_bias,
        temporal_reduce,
        temporal_reduce_bias,
    )
    grad_between, temporal_dmod, temporal_bias, temporal_terms = block_backward(
        grad_after.astype(jnp.float32),
        temporal_kept,
        temporal_mod,
        temporal_back,
        TIME_FORMS,
        sum_temporal,
    )
    temporal_grads = weight_grads(temporal_terms)
    grad_frames = to_frames(
        grad_between.astype(jnp.bfloat16).reshape(clips_here * FRAMES, local_patches, width_model)
    )
    spatial_back = fetch_weights(
        spatial_input,
        spatial_input_bias,
        spatial_output,
        spatial_output_bias,
        spatial_expand,
        spatial_expand_bias,
        spatial_reduce,
        spatial_reduce_bias,
    )
    input_grad, spatial_dmod, spatial_bias, spatial_terms = block_backward(
        grad_frames.astype(jnp.float32),
        spatial_kept,
        spatial_mod,
        spatial_back,
        SPACE_FORMS,
        sum_spatial,
    )
    spatial_grads = weight_grads(spatial_terms)
    grad_positions = jnp.sum(input_grad, axis=0)
    table_pick = (lax.iota(jnp.int32, row_table.shape[0]) == table_here).astype(jnp.float32)
    row_part = contract_first(row_pick.astype(jnp.float32), grad_positions, HIGHEST)
    col_part = contract_first(col_pick.astype(jnp.float32), grad_positions, HIGHEST)
    row_grad = table_pick[:, None, None] * row_part[None]
    col_grad = table_pick[:, None, None] * col_part[None]
    grad_mod = jnp.concatenate(
        [jnp.where(clip_pick[:, None], spatial_dmod[None, :], 0.0), temporal_dmod], axis=-1
    )
    (
        mod_share,
        row_share_grad,
        col_share_grad,
        sib_qv,
        sib_out,
        sib_up,
        sib_down,
        tib_qv,
        tib_out,
        tib_up,
        tib_down,
    ) = (
        lax.psum_scatter(grad_mod, "sp", scatter_dimension=1, tiled=True),
        lax.psum_scatter(row_grad, "sp", scatter_dimension=2, tiled=True),
        lax.psum_scatter(col_grad, "sp", scatter_dimension=2, tiled=True),
        lax.psum_scatter(spatial_bias[0], "sp", scatter_dimension=0, tiled=True),
        lax.psum_scatter(spatial_bias[1], "sp", scatter_dimension=0, tiled=True),
        lax.psum_scatter(spatial_bias[2], "sp", scatter_dimension=0, tiled=True),
        lax.psum_scatter(spatial_bias[3], "sp", scatter_dimension=0, tiled=True),
        lax.psum_scatter(temporal_bias[0], "sp", scatter_dimension=0, tiled=True),
        lax.psum_scatter(temporal_bias[1], "sp", scatter_dimension=0, tiled=True),
        lax.psum_scatter(temporal_bias[2], "sp", scatter_dimension=0, tiled=True),
        lax.psum_scatter(temporal_bias[3], "sp", scatter_dimension=0, tiled=True),
    )
    mod_low = mod_share.astype(jnp.bfloat16)
    modulate_bias_grad = jnp.sum(mod_low.astype(jnp.float32), axis=0)
    modulate_grad = contract_first(condition_act, mod_low)
    condition_part = project_rows(mod_low, modulate)
    grad_condition_act = lax.psum(condition_part, "sp")
    silu_back = jax.vjp(jax.nn.silu, condition)[1]
    grad_condition = silu_back(grad_condition_act)[0]
    class_grad = contract_first(class_pick.astype(jnp.float32), grad_condition, HIGHEST)
    grad_time = grad_condition.astype(jnp.bfloat16)
    time_second_bias_grad = jnp.sum(grad_time.astype(jnp.float32), axis=0)
    time_second_grad = contract_first(time_act, grad_time)
    grad_time_act = project_rows(grad_time, time_second)
    time_silu_back = jax.vjp(jax.nn.silu, time_hidden)[1]
    grad_time_hidden = time_silu_back(grad_time_act)[0].astype(jnp.bfloat16)
    time_first_bias_grad = jnp.sum(grad_time_hidden.astype(jnp.float32), axis=0)
    time_first_grad = contract_first(embedding, grad_time_hidden)
    summed = (
        lax.psum(row_share_grad.astype(jnp.bfloat16), "dp").astype(jnp.float32),
        lax.psum(col_share_grad.astype(jnp.bfloat16), "dp").astype(jnp.float32),
        lax.psum(class_grad.astype(jnp.bfloat16), "dp").astype(jnp.float32),
        lax.psum(time_first_grad.astype(jnp.bfloat16), "dp").astype(jnp.float32),
        lax.psum(time_first_bias_grad.astype(jnp.bfloat16), "dp").astype(jnp.float32),
        lax.psum(time_second_grad.astype(jnp.bfloat16), "dp").astype(jnp.float32),
        lax.psum(time_second_bias_grad.astype(jnp.bfloat16), "dp").astype(jnp.float32),
        lax.psum(modulate_grad.astype(jnp.bfloat16), "dp").astype(jnp.float32),
        lax.psum(modulate_bias_grad.astype(jnp.bfloat16), "dp").astype(jnp.float32),
        lax.psum(spatial_grads[0].astype(jnp.bfloat16), "dp").astype(jnp.float32),
        lax.psum(sib_qv.astype(jnp.bfloat16), "dp").astype(jnp.float32),
        lax.psum(spatial_grads[1].astype(jnp.bfloat16), "dp").astype(jnp.float32),
        lax.psum(sib_out.astype(jnp.bfloat16), "dp").astype(jnp.float32),
        lax.psum(spatial_grads[2].astype(jnp.bfloat16), "dp").astype(jnp.float32),
        lax.psum(sib_up.astype(jnp.bfloat16), "dp").astype(jnp.float32),
        lax.psum(spatial_grads[3].astype(jnp.bfloat16), "dp").astype(jnp.float32),
        lax.psum(sib_down.astype(jnp.bfloat16), "dp").astype(jnp.float32),
        lax.psum(temporal_grads[0].astype(jnp.bfloat16), "dp").astype(jnp.float32),
        lax.psum(tib_qv.astype(jnp.bfloat16), "dp").astype(jnp.float32),
        lax.psum(temporal_grads[1].astype(jnp.bfloat16), "dp").astype(jnp.float32),
        lax.psum(tib_out.astype(jnp.bfloat16), "dp").astype(jnp.float32),
        lax.psum(temporal_grads[2].astype(jnp.bfloat16), "dp").astype(jnp.float32),
        lax.psum(tib_up.astype(jnp.bfloat16), "dp").astype(jnp.float32),
        lax.psum(temporal_grads[3].astype(jnp.bfloat16), "dp").astype(jnp.float32),
        lax.psum(tib_down.astype(jnp.bfloat16), "dp").astype(jnp.float32),
    )
    return (
        activations,
        input_grad,
        summed[0],
        summed[1],
        summed[2],
        summed[3],
        summed[4],
        summed[5],
        summed[6],
        summed[7],
        summed[8],
        summed[9],
        summed[10],
        summed[11],
        summed[12],
        summed[13],
        summed[14],
        summed[15],
        summed[16],
        summed[17],
        summed[18],
        summed[19],
        summed[20],
        summed[21],
        summed[22],
        summed[23],
        summed[24],
    )


def solution(mesh):
    in_specs = (
        P(("dp", "sp"), None, None),
        P(("dp", "sp"), None, None),
        P("dp"),
        P("dp"),
        P("dp"),
        P("dp"),
        P(),
        P(),
        P(),
        P(),
        P(),
        P(),
        P(),
        P(None, "sp"),
        P("sp"),
        P("sp", None),
        P("sp"),
        P("sp", None),
        P("sp"),
        P("sp", None),
        P("sp"),
        P("sp", None),
        P("sp"),
        P("sp", None),
        P("sp"),
        P("sp", None),
        P("sp"),
        P("sp", None),
        P("sp"),
        P("sp", None),
        P("sp"),
    )
    out_specs = (
        P(("dp", "sp"), None, None),
        P(("dp", "sp"), None, None),
        P(None, None, "sp"),
        P(None, None, "sp"),
        P(),
        P(),
        P(),
        P(),
        P(),
        P(None, "sp"),
        P("sp"),
        P("sp", None),
        P("sp"),
        P("sp", None),
        P("sp"),
        P("sp", None),
        P("sp"),
        P("sp", None),
        P("sp"),
        P("sp", None),
        P("sp"),
        P("sp", None),
        P("sp"),
        P("sp", None),
        P("sp"),
        P("sp", None),
        P("sp"),
    )
    return jax.shard_map(
        per_device, mesh=mesh, in_specs=in_specs, out_specs=out_specs, check_vma=False
    )
```

profile of v0, /device:TPU:0, one launch (start us, length us, event | category | flops | bytes accessed | tf_op | source)
XLA Modules:
  0.0 3170.3 jit_solution(17941326212723603053)
XLA Ops:
  21.3 8.3 all-to-all-start.2
  40.3 78.8 %all-reduce = f32[13824]{0:T(1024)S(1)} all-reduce(f32[13824]{0:T(1024)S(1)} %add_dynamic-update-slice_fusion), channel_id=2, replica_groups=mesh['dp'=2,'sp'=16] {'sp'}, use_global_device_ids=true, to_apply=%add | all-reduce | flops 13824 | bytes 110592
  128.1 72.6 %all-reduce.22 = (bf16[2304]{0:T(1024)(128)(2,1)S(1)}, bf16[1152]{0:T(1024)(128)(2,1)S(1)}, bf16[1152]{0:T(1024)(128)(2,1)S(1)}, bf16[4608]{0:T(1024)(128)(2,1)S...) all-reduce(bf16[2304]{0:T(1024)(128)(2,1)S(1)} %dynamic-update-slic, ...), channel_id=1, replica_groups=mesh['dp'=2,'sp'=16] {'sp'}, use_global_device_ids=true, to_apply=%add.1 | all-reduce | flops 18432 | bytes 73728
  229.8 102.3 %all-gather.14.cloned.1.call-done = bf16[1152,4608]{1,0:T(8,128)(2,1)} async-done(((bf16[72,4608]{1,0:T(8,128)(2,1)}), bf16[1152,4608]{1,0:T(8,128)(2,1)}) %all-gather.14.cloned.1.call-update) | async-done | bytes 10616848 | tf_op jit(solution)/shard_map/all_gather | solution.py:252
  332.2 9.8 convolution_add_fusion
  342.0 124.5 %all-gather.16.cloned.1.call-done = bf16[1152,4608]{1,0:T(8,128)(2,1)} async-done(((bf16[72,4608]{1,0:T(8,128)(2,1)}), bf16[1152,4608]{1,0:T(8,128)(2,1)}) %all-gather.16.cloned.1.call-update) | async-done | bytes 10616848 | tf_op jit(solution)/shard_map/all_gather | solution.py:254
  466.5 10.3 fusion.82
  492.8 18.1 all-to-all-done
  514.7 66.2 %all-gather.18.cloned.1.call-done = bf16[1152,3456]{1,0:T(8,128)(2,1)} async-done(((bf16[72,3456]{1,0:T(8,128)(2,1)}), bf16[1152,3456]{1,0:T(8,128)(2,1)}) %all-gather.18.cloned.1.call-update) | async-done | bytes 7962640 | tf_op jit(solution)/shard_map/all_gather | solution.py:248
  614.4 31.6 all-gather.20.cloned.1.call-done
  652.0 129.2 %all-gather.22.cloned.1.call-done = bf16[1152,4608]{1,0:T(8,128)(2,1)} async-done(((bf16[72,4608]{1,0:T(8,128)(2,1)}), bf16[1152,4608]{1,0:T(8,128)(2,1)}) %all-gather.22.cloned.1.call-update) | async-done | bytes 10616848 | tf_op jit(solution)/shard_map/all_gather | solution.py:252
  781.2 9.9 fusion.12
  791.1 124.6 %all-gather.24.cloned.1.call-done = bf16[1152,4608]{1,0:T(8,128)(2,1)} async-done(((bf16[72,4608]{1,0:T(8,128)(2,1)}), bf16[1152,4608]{1,0:T(8,128)(2,1)}) %all-gather.24.cloned.1.call-update) | async-done | bytes 10616848 | tf_op jit(solution)/shard_map/all_gather | solution.py:254
  915.7 9.6 convert_reduce_fusion
  925.3 9.8 multiply_reduce_fusion.5
  935.2 10.1 multiply_reduce_fusion.4
  964.9 9.0 convolution_bitcast_fusion.1
  1002.1 12.8 convolution_bitcast_fusion
  1014.9 7.8 convolution_bitcast_fusion.2
  1027.9 10.0 convert_reduce_fusion.1
  1037.9 8.2 fusion.67
  1071.6 42.3 %pad_maximum_fusion.1 = f32[1152,13824]{1,0:T(8,128)} fusion(f32[1152,4608]{1,0:T(8,128)} %convolution_bitcast_fusion, f32[1152,4608]{1,0:T(8,128)} %convolution_bitcast_fusion.1, f32[1152,1152]{1,0:T(8,128)} %convolution_bitcast_fusion.3, f32[1152,3456]{1,0:T(8,128)} %convolution_bitcast_fusion.2), kind=kLoop, calls=%fused_computation.1 | loop fusion | flops 47775744 | bytes 127401984 | tf_op jit(solution)/shard_map/concatenate | solution.py:265
  1119.7 8.1 fusion.96
  1127.9 9.0 fusion.150
  1136.9 9.1 fusion.145
  1146.0 43.0 %pad_maximum_fusion = f32[1152,13824]{1,0:T(8,128)} fusion(f32[1152,4608]{1,0:T(8,128)} %fusion.150, f32[1152,4608]{1,0:T(8,128)} %fusion.145, f32[1152,1152]{1,0:T(8,128)} %fusion.100, f32[1152,3456]{1,0:T(8,128)} %fusion.96), kind=kLoop, calls=%fused_computation | loop fusion | flops 47775744 | bytes 127401984 | tf_op jit(solution)/shard_map/concatenate | solution.py:265
  1195.6 28.9 reduce-scatter.12.cloned.1.call-done
  1227.7 114.3 %all-reduce.29 = (bf16[4,32,1152]{2,1,0:T(8,128)(2,1)}, bf16[4,32,1152]{2,1,0:T(8,128)(2,1)}, f32[1,1152]{1,0:T(1,128)S(1)}, bf16[2304]{0:T(1024)(128)(2,1)S(1)}...) all-reduce(f32[4,32,1152]{2,1,0:T(8,128)} %get-tuple-element.154, ...), channel_id=3, replica_groups=mesh['dp'=2,'sp'=16] {'sp'}, use_global_device_ids=true, to_apply=%region_22.23.clone | all-reduce | flops 314496 | bytes 1889280
  1348.1 822.6 %reduce-scatter.16.cloned.1.call-done = f32[72,13824]{1,0:T(8,128)} async-done(((f32[1152,13824]{1,0:T(8,128)}), f32[72,13824]{1,0:T(8,128)}) %reduce-scatter.16.cloned.1.call-update) | async-done | bytes 3981328
  2175.7 917.8 %reduce-scatter.14.cloned.1.call-done = f32[72,13824]{1,0:T(8,128)} async-done(((f32[1152,13824]{1,0:T(8,128)}), f32[72,13824]{1,0:T(8,128)}) %reduce-scatter.14.cloned.1.call-update) | async-done | bytes 3981328
  3105.8 14.5 all-to-all-done.1
  3133.9 9.5 all-reduce.28.cloned.1.call-done
  (539 shorter events, 264.0 us)
Async XLA Ops:
  7.2 198.6 %all-gather.10.cloned.1.call-start = ((), (), s32[]{:S(2)}) async-start(), calls=%async_computation.7 | async-start | bytes 8460288 | tf_op jit(solution)/shard_map/all_gather | solution.py:248
  8.0 216.2 %all-gather.12.cloned.1.call-start = ((), (), s32[]{:S(2)}) async-start(), calls=%async_computation.8 | async-start | bytes 2820096 | tf_op jit(solution)/shard_map/all_gather | solution.py:250
  8.7 323.5 %all-gather.14.cloned.1.call-start = ((), (), s32[]{:S(2)}) async-start(), calls=%async_computation.9 | async-start | bytes 11280384 | tf_op jit(solution)/shard_map/all_gather | solution.py:252
  9.4 457.1 %all-gather.16.cloned.1.call-start = ((), (), s32[]{:S(2)}) async-start(), calls=%async_computation.10 | async-start | bytes 11280384 | tf_op jit(solution)/shard_map/all_gather | solution.py:254
  10.0 570.9 %all-gather.18.cloned.1.call-start = ((), (), s32[]{:S(2)}) async-start(), calls=%async_computation.11 | async-start | bytes 8460288 | tf_op jit(solution)/shard_map/all_gather | solution.py:248
  10.6 635.3 %all-gather.20.cloned.1.call-start = ((), (), s32[]{:S(2)}) async-start(), calls=%async_computation.12 | async-start | bytes 2820096 | tf_op jit(solution)/shard_map/all_gather | solution.py:250
  11.2 770.0 %all-gather.22.cloned.1.call-start = ((), (), s32[]{:S(2)}) async-start(), calls=%async_computation.13 | async-start | bytes 11280384 | tf_op jit(solution)/shard_map/all_gather | solution.py:252
  11.9 903.8 %all-gather.24.cloned.1.call-start = ((), (), s32[]{:S(2)}) async-start(), calls=%async_computation.14 | async-start | bytes 11280384 | tf_op jit(solution)/shard_map/all_gather | solution.py:254
  21.3 182.2 %all-to-all-start.2 = ((bf16[16,2,9216]{2,1,0:T(2,128)(2,1)}), bf16[16,2,9216]{2,1,0:T(2,128)(2,1)S(1)}, u32[]{:S(2)}, u32[]{:S(2)}) async-start(bf16[16,2,9216]{2,1,0:T(2,128)(2,1)} %reshape.1302), calls=%async_computation.2 | async-start | bytes 1179648 | tf_op jit(solution)/shard_map/all_to_all | solution.py:284
  120.1 815.0 %copy-start.77 = (f32[1152]{0:T(1024)}, f32[1152]{0:T(1024)S(1)}, u32[]{:S(2)}) copy-start(f32[1152]{0:T(1024)S(1)} %get-tuple-element.43) | copy-start | bytes 13828
  124.1 88.7 %copy-start.68 = (f32[1152]{0:T(1024)}, f32[1152]{0:T(1024)S(1)}, u32[]{:S(2)}) copy-start(f32[1152]{0:T(1024)S(1)} %get-tuple-element.53) | copy-start | bytes 13828
  124.1 88.7 %copy-start.79 = (f32[1152]{0:T(1024)}, f32[1152]{0:T(1024)S(1)}, u32[]{:S(2)}) copy-start(f32[1152]{0:T(1024)S(1)} %get-tuple-element.52) | copy-start | bytes 13828
  124.1 100.1 %copy-start.81 = (f32[1152]{0:T(1024)}, f32[1152]{0:T(1024)S(1)}, u32[]{:S(2)}) copy-start(f32[1152]{0:T(1024)S(1)} %get-tuple-element.54) | copy-start | bytes 13828
  124.1 208.1 %copy-start.64 = (f32[1152]{0:T(1024)}, f32[1152]{0:T(1024)S(1)}, u32[]{:S(2)}) copy-start(f32[1152]{0:T(1024)S(1)} %get-tuple-element.51) | copy-start | bytes 13828
  124.1 208.1 %copy-start.72 = (f32[1152]{0:T(1024)}, f32[1152]{0:T(1024)S(1)}, u32[]{:S(2)}) copy-start(f32[1152]{0:T(1024)S(1)} %get-tuple-element.50) | copy-start | bytes 13828
  124.1 342.4 %copy-start.74 = (f32[1152]{0:T(1024)}, f32[1152]{0:T(1024)S(1)}, u32[]{:S(2)}) copy-start(f32[1152]{0:T(1024)S(1)} %get-tuple-element.49) | copy-start | bytes 13828
  228.5 113.5 %copy-start.86 = (f32[256]{0:T(256)}, f32[256]{0:T(256)S(1)}, u32[]{:S(2)}) copy-start(f32[256]{0:T(256)S(1)} %broadcast_multiply_fusion.12) | copy-start | bytes 3076
  229.8 112.2 %copy-start.97 = (f32[256]{0:T(256)}, f32[256]{0:T(256)S(1)}, u32[]{:S(2)}) copy-start(f32[256]{0:T(256)S(1)} %add_rsqrt_fusion.2) | copy-start | bytes 3076
  484.9 26.0 all-to-all-start
  514.6 72.3 %copy-start.107 = (f32[256]{0:T(256)}, f32[256]{0:T(256)S(1)}, u32[]{:S(2)}) copy-start(f32[256]{0:T(256)S(1)} %add_rsqrt_fusion.1) | copy-start | bytes 3076
  514.7 72.2 %copy-start.93 = (f32[16,16]{1,0:T(8,128)}, f32[16,16]{1,0:T(8,128)S(1)}, u32[]{:S(2)}) copy-start(f32[16,16]{1,0:T(8,128)S(1)} %rsqrt.39) | copy-start | bytes 3076
  998.2 27.9 all-to-all-start.3
  1002.0 222.5 %reduce-scatter.12.cloned.1.call-start = ((), (), s32[]{:S(2)}) async-start(), calls=%async_computation.15 | async-start | bytes 7520256
  1071.6 1099.1 %reduce-scatter.16.cloned.1.call-start = ((), (), s32[]{:S(2)}) async-start(), calls=%async_computation.17 | async-start | bytes 67682304
  1114.0 1979.5 %reduce-scatter.14.cloned.1.call-start = ((), (), s32[]{:S(2)}) async-start(), calls=%async_computation.16 | async-start | bytes 67682304
  1189.1 1954.3 %all-reduce.28.cloned.1.call-start = ((), (), s32[]{:S(2)}) async-start(), calls=%async_computation.18 | async-start | bytes 18911232 | tf_op jit(solution)/shard_map/psum | solution.py:495
  1194.0 33.6 %copy-start.99 = (f32[4608]{0:T(1024)S(1)}, f32[4608]{0:T(1024)}, u32[]{:S(2)}) copy-start(f32[4608]{0:T(1024)} %get-tuple-element.181) | copy-start | bytes 55300
  1194.0 33.6 %copy-start.100 = (f32[4608]{0:T(1024)S(1)}, f32[4608]{0:T(1024)}, u32[]{:S(2)}) copy-start(f32[4608]{0:T(1024)} %get-tuple-element.113) | copy-start | bytes 55300
  1227.6 115.2 %copy-start.84 = (f32[1152]{0:T(1024)S(1)}, f32[1152]{0:T(1024)}, u32[]{:S(2)}) copy-start(f32[1152]{0:T(1024)} %copy-done.83) | copy-start | bytes 13828
  1227.6 115.2 %copy-start.106 = (bf16[1152]{0:T(1024)(128)(2,1)S(1)}, bf16[1152]{0:T(1024)(128)(2,1)}, u32[]{:S(2)}) copy-start(bf16[1152]{0:T(1024)(128)(2,1)} %param.41) | copy-start | bytes 6916
  1227.7 116.1 %copy-start.122 = (f32[256]{0:T(256)S(1)}, f32[256]{0:T(256)}, u32[]{:S(2)}) copy-start(f32[256]{0:T(256)} %get-tuple-element.104) | copy-start | bytes 3076
  3098.5 21.8 all-to-all-start.1
  (126 other events, 779.3 us)
Sparse Core Ops, SparseCore 0:
  10.8 120.4 all-gather.9
  134.0 62.8 all-gather.11
  199.7 132.4 all-gather.13
  334.8 131.6 all-gather.15
  469.1 111.7 all-gather.17
  583.5 62.4 all-gather.19
  648.7 132.4 all-gather.21
  784.0 131.6 all-gather.23
  1071.7 152.7 reduce-scatter.11
  1230.3 940.3 reduce-scatter.15
  2177.8 915.6 reduce-scatter.13
  3099.7 43.6 all-reduce.27
where the time goes:
time: 3180 us; the launch traced here: 3170 us
  waiting for transfers between devices  2400 us (75%)
  blocking collectives  269 us (8%)
  matrix products  215 us (7%)
  other arithmetic  163 us (5%)
  local copies, waits for them, and re-layouts  83.2 us (3%)
    unnamed x15, waiting for transfers between devices  1770 us
    unnamed x3, blocking collectives  266 us
    all_gather x2, waiting for transfers between devices, fetch_weights(): lax.all_gather(w_reduce, 'sp', axis=0, tiled=True)  249 us
    all_gather x2, waiting for transfers between devices, fetch_weights(): lax.all_gather(w_expand, 'sp', axis=0, tiled=True)  232 us
    concatenate x2, other arithmetic, product_rows(): return jnp.concatenate(parts, axis=1)  85.4 us
    dot_general x10, matrix products, contract_first(): lax.dot_general(left_rows, right_rows, (((0,), (0,)), ((), ())), preferre...  66.4 us
    all_gather x2, waiting for transfers between devices, fetch_weights(): lax.all_gather(w_input, 'sp', axis=0, tiled=True)  66.2 us
    dot_general x14, matrix products, project(): return jnp.dot(left_rows, weight, preferred_element_type=jnp.float32)  65.5 us
  transfers between devices with their start and end apart: 16, of which 12 were waited for; matrix products, arithmetic and copies ran while one was open for 9% of the time, Pallas kernels for 0%

commit v1 on v0

v1 whole, which is shorter than its diff:
```python
from functools import partial
import math

import jax
import jax.numpy as jnp
from jax import lax
from jax.sharding import PartitionSpec as P

HEADS = 16
HDIM = 72
FREQ = 256
SIDE = 16
FRAMES = 16

EPSILON = 1e-06
HIGHEST = lax.Precision.HIGHEST
BF16 = jnp.bfloat16
F32 = jnp.float32


def layer_norm(values):
    center = values - jnp.mean(values, axis=-1, keepdims=True)
    inverse = lax.rsqrt(jnp.mean(center * center, axis=-1, keepdims=True) + EPSILON)
    return (center * inverse, inverse)


def norm_back(gradient, normed, inverse):
    mean_grad = jnp.mean(gradient, axis=-1, keepdims=True)
    mean_cross = jnp.mean(gradient * normed, axis=-1, keepdims=True)
    return inverse * (gradient - mean_grad - normed * mean_cross)


def project(left_rows, weight):
    return lax.dot_general(
        left_rows,
        weight,
        (((left_rows.ndim - 1,), (0,)), ((), ())),
        preferred_element_type=F32,
    )


def project_rows(left_rows, weight):
    return lax.dot_general(
        left_rows,
        weight,
        (((left_rows.ndim - 1,), (1,)), ((), ())),
        preferred_element_type=F32,
    )


def contract_first(left_rows, right_rows, precision=None):
    return lax.dot_general(
        left_rows,
        right_rows,
        (((0,), (0,)), ((), ())),
        preferred_element_type=F32,
        precision=precision,
    )


def flat(values):
    return values.reshape(-1, values.shape[-1])


def token_sum(values):
    return jnp.sum(flat(values).astype(F32), axis=0)


def flip(values, axis, size, bit):
    return lax.ppermute(values, axis, [(i, i ^ bit) for i in range(size)])


def bits_of(size):
    bits = []
    bit = 1
    while bit < size:
        bits.append(bit)
        bit = bit * 2
    assert bit == size
    return bits


def cube_gather(values, axis, size):
    rank = lax.axis_index(axis)
    held = values[None]
    for bit in bits_of(size):
        other = flip(held, axis, size, bit)
        upper = (rank & bit) != 0
        held = jnp.concatenate(
            [jnp.where(upper, other, held), jnp.where(upper, held, other)], axis=0
        )
    return held


def cube_sum(values, axis, size):
    for bit in bits_of(size):
        values = values + flip(values, axis, size, bit)
    return values


def cube_scatter(values, axis, size):
    rank = lax.axis_index(axis)
    for bit in reversed(bits_of(size)):
        upper = (rank & bit) != 0
        low, high = values[:bit], values[bit:]
        away = jnp.where(upper, low, high)
        kept = jnp.where(upper, high, low)
        values = kept + flip(away, axis, size, bit)
    return values[0]


def attention_scores(query, key, stride):
    scores = jnp.einsum("snhd,smhd->shnm", query, key, preferred_element_type=F32)
    scores = scores * HDIM ** (-0.5)
    if stride > 1:
        count = scores.shape[-1]
        row = lax.broadcasted_iota(jnp.int32, (count, count), 0) % stride
        col = lax.broadcasted_iota(jnp.int32, (count, count), 1) % stride
        scores = jnp.where(row == col, scores, -1e30)
    return scores


def attend(query, key, value, stride):
    scores = attention_scores(query, key, stride)
    row_max = jnp.max(scores, axis=-1, keepdims=True)
    exponent = jnp.exp(scores - row_max)
    row_total = jnp.sum(exponent, axis=-1, keepdims=True)
    probs = (exponent / row_total).astype(BF16)
    mixed = jnp.einsum("shnm,smhd->snhd", probs, value, preferred_element_type=F32)
    return (mixed.astype(BF16), row_max + jnp.log(row_total))


def attend_back(query, key, value, logsum, grad_out, stride):
    scale = HDIM ** (-0.5)
    probs = jnp.exp(attention_scores(query, key, stride) - logsum)
    grad_probs = jnp.einsum("snhd,smhd->shnm", grad_out, value, preferred_element_type=F32)
    inner = jnp.sum(probs * grad_probs, axis=-1, keepdims=True)
    grad_scores = (probs * (grad_probs - inner)).astype(BF16)
    grad_query = (
        jnp.einsum("shnm,smhd->snhd", grad_scores, key, preferred_element_type=F32) * scale
    )
    grad_key = (
        jnp.einsum("shnm,snhd->smhd", grad_scores, query, preferred_element_type=F32) * scale
    )
    grad_value = jnp.einsum(
        "shnm,snhd->smhd", probs.astype(BF16), grad_out, preferred_element_type=F32
    )
    return (grad_query.astype(BF16), grad_key.astype(BF16), grad_value.astype(BF16))


class Layout:
    def __init__(self, mesh):
        self.cores = mesh.shape["dp"]
        self.chips = mesh.shape["sp"]
        self.heads = HEADS // self.cores


def core_total(values, lay):
    total = values.astype(BF16).astype(F32)
    for bit in bits_of(lay.cores):
        total = total + flip(total.astype(BF16), "dp", lay.cores, bit).astype(F32)
    return total


def core_part(values, axis, lay):
    share = values.shape[axis] // lay.cores
    return lax.dynamic_slice_in_dim(values, lax.axis_index("dp") * share, share, axis)


def heads_of(values, sequences, lay):
    return values.reshape(sequences, -1, lay.heads, HDIM)


def block_forward(inputs, modulation, weights, biases, stride, lay):
    w_input, w_output, w_expand, w_reduce = weights
    query_bias, value_bias, output_bias, expand_bias, reduce_bias = biases
    groups, count, width = inputs.shape
    share = width // lay.cores
    shift_att, scale_att, gate_att, shift_mlp, scale_mlp, gate_mlp = jnp.split(
        modulation[:, None, :], 6, axis=-1
    )
    normed_att, inverse_att = layer_norm(inputs)
    attn_input = (normed_att * (1.0 + scale_att) + shift_att).astype(BF16)
    projected = project(attn_input, w_input)
    query = heads_of((projected[..., :share] + query_bias).astype(BF16), groups, lay)
    key = heads_of(projected[..., share : 2 * share].astype(BF16), groups, lay)
    value = heads_of((projected[..., 2 * share :] + value_bias).astype(BF16), groups, lay)
    mixed, logsum = attend(query, key, value, stride)
    attended = mixed.reshape(groups, count, share)
    branch = core_total(project_rows(attended, w_output), lay) + output_bias
    hidden = inputs + gate_att * branch
    normed_mlp, inverse_mlp = layer_norm(hidden)
    mlp_input = (normed_mlp * (1.0 + scale_mlp) + shift_mlp).astype(BF16)
    expanded = project(mlp_input, w_expand) + expand_bias
    activated = jax.nn.gelu(expanded, approximate=True).astype(BF16)
    reduced = core_total(project_rows(activated, w_reduce), lay) + reduce_bias
    output = hidden + gate_mlp * reduced
    kept = (
        normed_att,
        inverse_att,
        attn_input,
        query,
        key,
        value,
        attended,
        logsum,
        branch,
        normed_mlp,
        inverse_mlp,
        mlp_input,
        expanded,
        activated,
        reduced,
    )
    return (output, kept)


def block_backward(gradient, kept, modulation, weights, stride, lay):
    w_input, w_output, w_expand, w_reduce = weights
    (
        normed_att,
        inverse_att,
        attn_input,
        query,
        key,
        value,
        attended,
        logsum,
        branch,
        normed_mlp,
        inverse_mlp,
        mlp_input,
        expanded,
        activated,
        reduced,
    ) = kept
    groups, count, width = gradient.shape
    share = width // lay.cores
    shift_att, scale_att, gate_att, shift_mlp, scale_mlp, gate_mlp = jnp.split(
        modulation[:, None, :], 6, axis=-1
    )
    grad_gate_mlp = jnp.sum(gradient * reduced, axis=1)
    grad_reduced = (gradient * gate_mlp).astype(BF16)
    reduce_grad = contract_first(flat(grad_reduced), flat(activated)).astype(BF16)
    grad_activated = project(grad_reduced, w_reduce)
    gelu_back = jax.vjp(partial(jax.nn.gelu, approximate=True), expanded)[1]
    grad_expanded = gelu_back(grad_activated)[0].astype(BF16)
    expand_grad = contract_first(flat(mlp_input), flat(grad_expanded)).astype(BF16)
    grad_mlp_input = core_total(project_rows(grad_expanded, w_expand), lay)
    grad_scale_mlp = jnp.sum(grad_mlp_input * normed_mlp, axis=1)
    grad_shift_mlp = jnp.sum(grad_mlp_input, axis=1)
    grad_hidden = gradient + norm_back(grad_mlp_input * (1.0 + scale_mlp), normed_mlp, inverse_mlp)
    grad_gate_att = jnp.sum(grad_hidden * branch, axis=1)
    grad_branch = (grad_hidden * gate_att).astype(BF16)
    output_grad = contract_first(flat(grad_branch), flat(attended)).astype(BF16)
    grad_attended = project(grad_branch, w_output).astype(BF16)
    grad_query, grad_key, grad_value = attend_back(
        query, key, value, logsum, heads_of(grad_attended, groups, lay), stride
    )
    grad_query = grad_query.reshape(groups, count, share)
    grad_key = grad_key.reshape(groups, count, share)
    grad_value = grad_value.reshape(groups, count, share)
    grad_projected = jnp.concatenate([grad_query, grad_key, grad_value], axis=-1)
    input_grad = contract_first(flat(attn_input), flat(grad_projected)).astype(BF16)
    grad_attn_input = core_total(project_rows(grad_projected, w_input), lay)
    grad_scale_att = jnp.sum(grad_attn_input * normed_att, axis=1)
    grad_shift_att = jnp.sum(grad_attn_input, axis=1)
    grad_inputs = grad_hidden + norm_back(
        grad_attn_input * (1.0 + scale_att), normed_att, inverse_att
    )
    grad_mod = jnp.concatenate(
        [
            grad_shift_att,
            grad_scale_att,
            grad_gate_att,
            grad_shift_mlp,
            grad_scale_mlp,
            grad_gate_mlp,
        ],
        axis=-1,
    )
    split_biases = (token_sum(grad_query), token_sum(grad_value), token_sum(grad_expanded))
    whole_biases = (token_sum(grad_branch), token_sum(grad_reduced))
    return (
        grad_inputs,
        grad_mod,
        split_biases,
        whole_biases,
        (input_grad, output_grad, expand_grad, reduce_grad),
    )


def shard_parts(w_input, w_output, w_expand, w_reduce, lay):
    rows = w_input.shape[0]
    attention = core_part(w_input.reshape(rows, 3, -1), 2, lay).reshape(rows, -1)
    return (
        attention,
        core_part(w_output, 1, lay),
        core_part(w_expand, 1, lay),
        core_part(w_reduce, 1, lay),
    )


def split_columns(values, widths):
    bounds = []
    offset = 0
    for width in widths[:-1]:
        offset = offset + width
        bounds.append(offset)
    return jnp.split(values, bounds, axis=-1)


def fetch_weights(w_input, w_output, w_expand, w_reduce, lay):
    parts = shard_parts(w_input, w_output, w_expand, w_reduce, lay)
    joined = jnp.concatenate(parts, axis=1)
    whole = lax.all_gather(joined, "sp", axis=0, tiled=True)
    return split_columns(whole, [part.shape[1] for part in parts])


def reduce_weights(grads, lay):
    joined = jnp.concatenate(grads, axis=1)
    summed = lax.psum_scatter(joined, "sp", scatter_dimension=0, tiled=True)
    return split_columns(summed, [grad.shape[1] for grad in grads])


def join_columns(parts, lay):
    g_input, g_output, g_expand, g_reduce = [
        cube_gather(part.astype(BF16), "dp", lay.cores).astype(F32) for part in parts
    ]
    rows = g_output.shape[1]
    thirds = g_input.reshape(lay.cores, rows, 3, -1)
    return (
        jnp.transpose(thirds, (1, 2, 0, 3)).reshape(rows, -1),
        jnp.transpose(g_output, (1, 0, 2)).reshape(rows, -1),
        jnp.transpose(g_expand, (1, 0, 2)).reshape(rows, -1),
        jnp.transpose(g_reduce, (1, 0, 2)).reshape(rows, -1),
    )


def to_positions(values, clips, lay):
    moved = lax.all_to_all(values, "sp", split_axis=1, concat_axis=0, tiled=True)
    moved = moved.reshape(clips, -1, values.shape[-1])
    return cube_gather(moved, "dp", lay.cores).reshape(-1, moved.shape[1], moved.shape[2])


def own_group(values, lay):
    share = values.shape[0] // lay.cores
    return lax.dynamic_slice_in_dim(values, lax.axis_index("dp") * share, share, 0)


def to_frames(values, frames_here, lay):
    own = own_group(values, lay)
    own = own.reshape(frames_here * lay.chips, -1, values.shape[-1])
    return lax.all_to_all(own, "sp", split_axis=0, concat_axis=1, tiled=True)


def place_split(values, lay):
    whole = jnp.zeros((lay.cores,) + values.shape, values.dtype)
    whole = lax.dynamic_update_index_in_dim(whole, values, lax.axis_index("dp"), 0)
    return whole.reshape(-1)


def per_device(
    lay,
    frames,
    cotangent,
    aspect,
    table_index,
    noise_level,
    labels,
    row_table,
    column_table,
    class_table,
    time_first,
    time_first_bias,
    time_second,
    time_second_bias,
    modulate,
    modulate_bias,
    spatial_input,
    spatial_input_bias,
    spatial_output,
    spatial_output_bias,
    spatial_expand,
    spatial_expand_bias,
    spatial_reduce,
    spatial_reduce_bias,
    temporal_input,
    temporal_input_bias,
    temporal_output,
    temporal_output_bias,
    temporal_expand,
    temporal_expand_bias,
    temporal_reduce,
    temporal_reduce_bias,
):
    cores, chips = lay.cores, lay.chips
    chip = lax.axis_index("sp")
    core = lax.axis_index("dp")
    frame_count, patches, width = frames.shape
    clips_here = aspect.shape[0]
    clips = cores * clips_here
    clip_here = chip * frame_count // FRAMES

    spatial_weights = fetch_weights(
        spatial_input, spatial_output, spatial_expand, spatial_reduce, lay
    )
    temporal_weights = fetch_weights(
        temporal_input, temporal_output, temporal_expand, temporal_reduce, lay
    )

    facts = cube_gather(jnp.stack([aspect, table_index, noise_level, labels]), "dp", cores)
    group_aspect, group_table = (
        lax.dynamic_index_in_dim(facts[:, k], clip_here, 1, keepdims=False) for k in (0, 1)
    )
    all_levels = facts[:, 2].reshape(clips)
    all_labels = facts[:, 3].reshape(clips)
    group_clips = jnp.arange(cores) * clips_here + clip_here

    half = FREQ // 2
    frequency = jnp.exp(-math.log(10000.0) * jnp.arange(half, dtype=F32) / half)
    angles = all_levels.astype(F32)[:, None] * frequency[None, :]
    embedding = jnp.concatenate([jnp.cos(angles), jnp.sin(angles)], axis=-1).astype(BF16)
    time_hidden = project(embedding, time_first) + time_first_bias.astype(F32)
    time_act = jax.nn.silu(time_hidden).astype(BF16)
    class_pick = (all_labels[:, None] == lax.iota(jnp.int32, class_table.shape[0])[None, :]).astype(
        BF16
    )
    condition = (
        project(time_act, time_second)
        + time_second_bias.astype(F32)
        + project(class_pick, class_table)
    )
    condition_act = jax.nn.silu(condition).astype(BF16)
    mod_cols = project(condition_act, modulate) + modulate_bias.astype(F32)

    bias_shards = (
        spatial_input_bias,
        spatial_output_bias,
        spatial_expand_bias,
        spatial_reduce_bias,
        temporal_input_bias,
        temporal_output_bias,
        temporal_expand_bias,
        temporal_reduce_bias,
    )
    bias_sizes = [shard.shape[0] for shard in bias_shards]
    small = jnp.concatenate([mod_cols.reshape(-1)] + [shard.astype(F32) for shard in bias_shards])
    gathered = cube_gather(small, "sp", chips)
    mod_size = mod_cols.shape[1]
    pieces = split_columns(gathered, [clips * mod_size] + bias_sizes)
    modulation = jnp.transpose(pieces[0].reshape(chips, clips, mod_size), (1, 0, 2)).reshape(
        clips, chips * mod_size
    )
    whole_biases = [piece.reshape(-1) for piece in pieces[1:]]

    def block_biases(parts):
        query_bias, value_bias = jnp.split(parts[0], 2)
        return (
            core_part(query_bias, 0, lay),
            core_part(value_bias, 0, lay),
            parts[1],
            core_part(parts[2], 0, lay),
            parts[3],
        )

    spatial_biases = block_biases(whole_biases[:4])
    temporal_biases = block_biases(whole_biases[4:])
    clip_pick = (group_clips[:, None] == jnp.arange(clips)[None, :]).astype(F32)
    spatial_mod = jnp.sum(
        clip_pick[:, :, None] * modulation[None, :, : 6 * width], axis=1
    )
    temporal_mod = modulation[:, 6 * width :]

    row_width = jnp.where(
        group_aspect == 0, SIDE, jnp.where(group_aspect == 1, 2 * SIDE, SIDE // 2)
    )[:, None, None]
    patch_ids = lax.iota(jnp.int32, patches)[None, :, None]
    grid_ids = lax.iota(jnp.int32, 2 * SIDE)[None, None, :]
    row_pick = (patch_ids // row_width == grid_ids).astype(BF16)
    col_pick = (patch_ids % row_width == grid_ids).astype(BF16)
    row_chosen = jnp.take(row_table, group_table, axis=0)
    col_chosen = jnp.take(column_table, group_table, axis=0)
    positions = jnp.einsum(
        "gpr,grd->gpd", row_pick, row_chosen, preferred_element_type=F32
    ) + jnp.einsum("gpr,grd->gpd", col_pick, col_chosen, preferred_element_type=F32)
    all_frames = cube_gather(frames, "dp", cores).astype(F32)
    block_input = (all_frames + positions[:, None]).reshape(-1, patches, width)
    frame_mod = jnp.repeat(spatial_mod, frame_count, axis=0)

    spatial_out, spatial_kept = block_forward(
        block_input, frame_mod, spatial_weights, spatial_biases, 1, lay
    )
    own_out = own_group(spatial_out.astype(BF16), lay)
    between = to_positions(own_out, clips_here, lay)
    local_patches = patches // chips
    temporal_out, temporal_kept = block_forward(
        between.astype(F32), temporal_mod, temporal_weights, temporal_biases, local_patches, lay
    )
    activations = to_frames(temporal_out.astype(BF16), frame_count, lay)
    grad_after = to_positions(cotangent, clips_here, lay)
    grad_between, temporal_dmod, temporal_split, temporal_whole, temporal_grads = block_backward(
        grad_after.astype(F32), temporal_kept, temporal_mod, temporal_weights, local_patches, lay
    )
    temporal_sums = reduce_weights(temporal_grads, lay)
    own_grad = to_frames(grad_between.astype(BF16), frame_count, lay)
    grad_frames = cube_gather(own_grad, "dp", cores).reshape(-1, patches, width)
    input_grad_all, frame_dmod, spatial_split, spatial_whole, spatial_grads = block_backward(
        grad_frames.astype(F32), spatial_kept, frame_mod, spatial_weights, 1, lay
    )
    spatial_sums = reduce_weights(spatial_grads, lay)
    input_grad = own_group(input_grad_all, lay)

    grad_positions = jnp.sum(input_grad, axis=0)
    own_rows = lax.dynamic_index_in_dim(row_pick, core, 0, keepdims=False).astype(F32)
    own_cols = lax.dynamic_index_in_dim(col_pick, core, 0, keepdims=False).astype(F32)
    table_part = contract_first(
        jnp.concatenate([own_rows, own_cols], axis=1), grad_positions, HIGHEST
    )
    here = (lax.iota(jnp.int32, clips_here) == clip_here).astype(F32)
    table_part = here[:, None, None] * table_part[None]

    spatial_dmod = jnp.sum(frame_dmod.reshape(cores, frame_count, -1), axis=1)
    spatial_dmod = jnp.sum(clip_pick[:, :, None] * spatial_dmod[:, None, :], axis=0)
    grad_mod = jnp.concatenate([spatial_dmod, temporal_dmod], axis=-1)

    def by_chip(values):
        parts = values.reshape(-1, chips, values.shape[-1] // chips)
        return jnp.transpose(parts, (1, 0, 2)).reshape(chips, -1)

    def bias_rows(split, whole):
        query_sum, value_sum, expand_sum = [place_split(part, lay) for part in split]
        output_sum, reduce_sum = whole
        return (
            by_chip(jnp.concatenate([query_sum, value_sum])),
            by_chip(expand_sum),
            by_chip(output_sum),
            by_chip(reduce_sum),
        )

    spatial_rows = bias_rows(spatial_split, spatial_whole)
    temporal_rows = bias_rows(temporal_split, temporal_whole)
    rows = (
        by_chip(table_part.reshape(-1, width)),
        spatial_rows[0],
        spatial_rows[1],
        temporal_rows[0],
        temporal_rows[1],
        by_chip(grad_mod),
        spatial_rows[2],
        spatial_rows[3],
        temporal_rows[2],
        temporal_rows[3],
    )
    summed = cube_scatter(jnp.concatenate(rows, axis=1), "sp", chips)
    sums = split_columns(summed, [row.shape[1] for row in rows])

    mod_low = sums[5].reshape(clips, -1).astype(BF16)
    modulate_bias_grad = jnp.sum(mod_low.astype(F32), axis=0)
    modulate_grad = contract_first(condition_act, mod_low)
    condition_part = project_rows(mod_low, modulate)

    table_sum = sums[0].reshape(clips_here, -1)
    table_pick = (lax.iota(jnp.int32, row_table.shape[0])[:, None] == table_index[None, :]).astype(
        F32
    )
    table_placed = jnp.sum(table_pick[:, :, None] * table_sum[None], axis=1)
    exchanged = jnp.concatenate([table_placed.reshape(-1)] + [sums[k] for k in (1, 2, 3, 4)])
    exchanged = cube_sum(exchanged, "dp", cores)
    tables, s_input_bias, s_expand_bias, t_input_bias, t_expand_bias = split_columns(
        exchanged, [table_placed.size] + [sums[k].shape[0] for k in (1, 2, 3, 4)]
    )
    tables = tables.reshape(row_table.shape[0], 2, 2 * SIDE, -1)

    grad_condition_act = cube_sum(condition_part, "sp", chips)
    silu_back = jax.vjp(jax.nn.silu, condition)[1]
    grad_condition = silu_back(grad_condition_act)[0]
    class_grad = contract_first(class_pick.astype(F32), grad_condition, HIGHEST)
    grad_time = grad_condition.astype(BF16)
    time_second_bias_grad = jnp.sum(grad_time.astype(F32), axis=0)
    time_second_grad = contract_first(time_act, grad_time)
    grad_time_act = project_rows(grad_time, time_second)
    time_silu_back = jax.vjp(jax.nn.silu, time_hidden)[1]
    grad_time_hidden = time_silu_back(grad_time_act)[0].astype(BF16)
    time_first_bias_grad = jnp.sum(grad_time_hidden.astype(F32), axis=0)
    time_first_grad = contract_first(embedding, grad_time_hidden)

    s_input, s_output, s_expand, s_reduce = join_columns(spatial_sums, lay)
    t_input, t_output, t_expand, t_reduce = join_columns(temporal_sums, lay)
    return (
        activations,
        input_grad,
        tables[:, 0],
        tables[:, 1],
        class_grad,
        time_first_grad,
        time_first_bias_grad,
        time_second_grad,
        time_second_bias_grad,
        modulate_grad,
        modulate_bias_grad,
        s_input,
        s_input_bias,
        s_output,
        sums[6],
        s_expand,
        s_expand_bias,
        s_reduce,
        sums[7],
        t_input,
        t_input_bias,
        t_output,
        sums[8],
        t_expand,
        t_expand_bias,
        t_reduce,
        sums[9],
    )


def solution(mesh):
    in_specs = (
        P(("dp", "sp"), None, None),
        P(("dp", "sp"), None, None),
        P("dp"),
        P("dp"),
        P("dp"),
        P("dp"),
        P(),
        P(),
        P(),
        P(),
        P(),
        P(),
        P(),
        P(None, "sp"),
        P("sp"),
        P("sp", None),
        P("sp"),
        P("sp", None),
        P("sp"),
        P("sp", None),
        P("sp"),
        P("sp", None),
        P("sp"),
        P("sp", None),
        P("sp"),
        P("sp", None),
        P("sp"),
        P("sp", None),
        P("sp"),
        P("sp", None),
        P("sp"),
    )
    out_specs = (
        P(("dp", "sp"), None, None),
        P(("dp", "sp"), None, None),
        P(None, None, "sp"),
        P(None, None, "sp"),
        P(),
        P(),
        P(),
        P(),
        P(),
        P(None, "sp"),
        P("sp"),
        P("sp", None),
        P("sp"),
        P("sp", None),
        P("sp"),
        P("sp", None),
        P("sp"),
        P("sp", None),
        P("sp"),
        P("sp", None),
        P("sp"),
        P("sp", None),
        P("sp"),
        P("sp", None),
        P("sp"),
        P("sp", None),
        P("sp"),
    )
    return jax.shard_map(
        partial(per_device, Layout(mesh)), mesh=mesh, in_specs=in_specs, out_specs=out_specs, check_vma=False
    )
```

time: 3180 us -> 1100 us (0.35)
  waiting for transfers between devices: 2400 us -> 577 us
  blocking collectives: 269 us -> 36.9 us
  local copies, waits for them, and re-layouts: 83.2 us -> 180 us
  other arithmetic: 163 us -> 79.7 us
  matrix products: 215 us -> 157 us
    unnamed x15 -> x4, waiting for transfers between devices: 1770 us -> 0.07 us
    all_gather x8 -> x2, waiting for transfers between devices: 578 us -> 215 us  [fetch_weights(): whole = lax.all_gather(joined, 'sp', axis=0, tiled=True)]
    unnamed x3 -> x0, blocking collectives: 266 us -> none
    reduce_scatter x0 -> x2, waiting for transfers between devices: none -> 254 us  [reduce_weights(): summed = lax.psum_scatter(joined, 'sp', scatter_dimension=0, tiled=True)]
    concatenate x4 -> x10, other arithmetic: 85.4 us -> 2.77 us  [the longest x8 2.75 us: cube_gather(): jnp.concatenate([jnp.where(upper, other, held), jnp.where(upper, held, ot...]
    ppermute x0 -> x34, waiting for transfers between devices: none -> 65.1 us  [flip(): return lax.ppermute(values, axis, [(i, i ^ bit) for i in range(size)])]
    concatenate x2 -> x16, local copies, waits for them, and re-layouts: 0.02 us -> 64.3 us  [the longest x2 51 us: reduce_weights(): joined = jnp.concatenate(grads, axis=1)]
    all_to_all x0 -> x1, blocking collectives: none -> 36.9 us  [to_frames(): return lax.all_to_all(own, 'sp', split_axis=0, concat_axis=1, tiled=True)]
  transfers between devices with their start and end apart: 16 -> 41, of which waited for: 12 -> 22; matrix products, arithmetic and copies ran while one was open for 9% -> 29% of each run, Pallas kernels for 0% -> 0%
where the time goes in v1:
time: 1100 us; the launch traced here: 1090 us
  waiting for transfers between devices  577 us (52%)
  local copies, waits for them, and re-layouts  180 us (16%)
  matrix products  157 us (14%)
  other arithmetic  79.7 us (7%)
  starting transfers between devices  40.2 us (4%)
  blocking collectives  36.9 us (3%)
  between operations  18.7 us (2%)
    reduce_scatter x2, waiting for transfers between devices, reduce_weights(): summed = lax.psum_scatter(joined, 'sp', scatter_dimension=0, tiled=True)  254 us
    all_gather x2, waiting for transfers between devices, fetch_weights(): whole = lax.all_gather(joined, 'sp', axis=0, tiled=True)  215 us
    ppermute x34, waiting for transfers between devices, flip(): return lax.ppermute(values, axis, [(i, i ^ bit) for i in range(size)])  65.1 us
    concatenate x2, local copies, waits for them, and re-layouts, reduce_weights(): joined = jnp.concatenate(grads, axis=1)  51 us
    dot_general x10, matrix products, project_rows(): lax.dot_general(left_rows, weight, (((left_rows.ndim - 1,), (1,)), ((), (...  48.5 us
    dot_general x12, matrix products, project(): lax.dot_general(left_rows, weight, (((left_rows.ndim - 1,), (0,)), ((), (...  46.3 us
    dot_general x13, matrix products, contract_first(): lax.dot_general(left_rows, right_rows, (((0,), (0,)), ((), ())), preferre...  45.6 us
    all_to_all x1, blocking collectives, to_frames(): return lax.all_to_all(own, 'sp', split_axis=0, concat_axis=1, tiled=True)  36.9 us
  transfers between devices with their start and end apart: 41, of which 22 were waited for; matrix products, arithmetic and copies ran while one was open for 29% of the time, Pallas kernels for 0%

profile of v1, /device:TPU:0, one launch (start us, length us, event | category | flops | bytes accessed | tf_op | source)
XLA Modules:
  0.0 1090.2 jit_solution(5648749638575496219)
XLA Ops:
  75.3 129.0 %all-gather.3.cloned.1.call-done = bf16[1152,6912]{1,0:T(8,128)(2,1)} async-done(((bf16[72,6912]{1,0:T(8,128)(2,1)}), bf16[1152,6912]{1,0:T(8,128)(2,1)}) %all-gather.3.cloned.1.call-update) | async-done | bytes 15925264 | tf_op jit(solution)/shard_map/all_gather | solution.py:316
  204.4 5.4 fusion.28
  226.3 5.9 convolution_add_fusion.1
  232.3 9.3 fusion.35
  251.4 5.2 reduce.33
  264.1 6.0 reduce.34
  272.6 13.5 %all-to-all-done = bf16[16,2,9216]{2,1,0:T(2,128)(2,1)S(1)} async-done(((bf16[16,2,9216]{2,1,0:T(2,128)(2,1)}), bf16[16,2,9216]{2,1,0:T(2,128)(2,1)S(1)}, u32[]{:S(2)}, u32[]{:S(2)}) %all-to-all-start) | async-done | bytes 589856 | tf_op jit(solution)/shard_map/all_to_all | solution.py:341
  286.9 11.8 %all-to-all-start.2 = ((bf16[16,2,9216]{2,1,0:T(2,128)(2,1)}), bf16[16,2,9216]{2,1,0:T(2,128)(2,1)S(1)}, u32[]{:S(2)}, u32[]{:S(2)}) async-start(bf16[16,2,9216]{2,1,0:T(2,128)(2,1)} %reshape.802), calls=%async_computation.2 | async-start | bytes 1179648 | tf_op jit(solution)/shard_map/all_to_all | solution.py:341
  305.6 10.8 all-to-all-done.2
  323.4 85.8 %all-gather.5.cloned.1.call-done = bf16[1152,6912]{1,0:T(8,128)(2,1)} async-done(((bf16[72,6912]{1,0:T(8,128)(2,1)}), bf16[1152,6912]{1,0:T(8,128)(2,1)}) %all-gather.5.cloned.1.call-update) | async-done | bytes 15925264 | tf_op jit(solution)/shard_map/all_gather | solution.py:316
  428.8 6.4 convolution_add_fusion
  435.2 6.6 fusion.33
  442.0 7.1 convert_reduce_fusion
  449.1 5.7 fusion.34
  455.3 5.3 fusion.3
  460.7 5.6 fusion.2
  485.8 6.2 fusion.5
  492.0 6.5 copy.367
  498.5 25.4 %concatenate.161 = bf16[1152,6912]{1,0:T(8,128)(2,1)} concatenate(bf16[1152,1728]{1,0:T(8,128)(2,1)} %copy.367, bf16[1152,576]{1,0:T(8,128)(2,1)} %copy.368, bf16[1152,2304]{1,0:T(8,128)(2,1)} %fusion.2, bf16[1152,2304]{1,0:T(8,128)(2,1)} %fusion.3), dimensions={1} | concatenate | bytes 31850496 | tf_op jit(solution)/shard_map/concatenate | solution.py:321
  524.0 5.5 fusion.31
  534.1 36.9 %all_to_all.19 = bf16[16,16,1152]{2,1,0:T(8,128)(2,1)S(1)} all-to-all(bf16[16,16,1152]{2,1,0:T(8,128)(2,1)S(1)} %bitcast.435), channel_id=1, replica_groups=mesh['dp'=2,'sp'=16] {'sp'}, dimensions={0} | all-to-all | bytes 1179648 | tf_op jit(solution)/shard_map/all_to_all | solution.py:354
  573.2 7.0 convert_reduce_fusion.1
  583.7 5.5 fusion
  589.2 5.4 fusion.1
  619.1 6.5 copy.358
  625.6 25.7 %concatenate.154 = bf16[1152,6912]{1,0:T(8,128)(2,1)} concatenate(bf16[1152,1728]{1,0:T(8,128)(2,1)} %copy.358, bf16[1152,576]{1,0:T(8,128)(2,1)} %copy.359, bf16[1152,2304]{1,0:T(8,128)(2,1)} %fusion, bf16[1152,2304]{1,0:T(8,128)(2,1)} %fusion.1), dimensions={1} | concatenate | bytes 31850496 | tf_op jit(solution)/shard_map/concatenate | solution.py:321
  652.0 6.3 fusion.32
  682.1 27.3 %collective-permute-done.17 = f32[8,7488]{1,0:T(8,128)S(1)} collective-permute-done((f32[8,7488]{1,0:T(8,128)S(1)}, f32[8,7488]{1,0:T(8,128)S(1)}, u32[]{:S(2)}, u32[]{:S(2)}) %collective-permute-start.17) | collective-permute-done | bytes 239648 | tf_op jit(solution)/shard_map/ppermute | solution.py:70
  709.6 15.3 %collective-permute-done.18 = f32[4,7488]{1,0:T(4,128)S(1)} collective-permute-done((f32[4,7488]{1,0:T(4,128)S(1)}, f32[4,7488]{1,0:T(4,128)S(1)}, u32[]{:S(2)}, u32[]{:S(2)}) %collective-permute-start.18) | collective-permute-done | bytes 119840 | tf_op jit(solution)/shard_map/ppermute | solution.py:70
  733.4 18.7 %all-to-all-done.1 = bf16[16,16,1152]{2,1,0:T(8,128)(2,1)S(1)} async-done(((bf16[16,16,1152]{2,1,0:T(8,128)(2,1)}), bf16[16,16,1152]{2,1,0:T(8,128)(2,1)S(1)}, u32[]{:S(2)}, u32[]{:S(2)}) %all-to-all-start.1) | async-done | bytes 589856 | tf_op jit(solution)/shard_map/all_to_all | solution.py:354
  780.4 20.6 %reduce-scatter.5.cloned.1.call-done = bf16[72,6912]{1,0:T(8,128)(2,1)} async-done(((bf16[1152,6912]{1,0:T(8,128)(2,1)}), bf16[72,6912]{1,0:T(8,128)(2,1)}) %reduce-scatter.5.cloned.1.call-update) | async-done | bytes 995344 | tf_op jit(solution)/shard_map/reduce_scatter | solution.py:322
  824.9 233.8 %reduce-scatter.3.cloned.1.call-done = bf16[72,6912]{1,0:T(8,128)(2,1)} async-done(((bf16[1152,6912]{1,0:T(8,128)(2,1)}), bf16[72,6912]{1,0:T(8,128)(2,1)}) %reduce-scatter.3.cloned.1.call-update) | async-done | bytes 995344 | tf_op jit(solution)/shard_map/reduce_scatter | solution.py:322
  (584 shorter events, 299.5 us)
Async XLA Ops:
  7.2 197.2 %all-gather.3.cloned.1.call-start = ((), (), s32[]{:S(2)}) async-start(), calls=%async_computation.6 | async-start | bytes 16920576 | tf_op jit(solution)/shard_map/all_gather | solution.py:316
  16.9 392.4 %all-gather.5.cloned.1.call-start = ((), (), s32[]{:S(2)}) async-start(), calls=%async_computation.7 | async-start | bytes 16920576 | tf_op jit(solution)/shard_map/all_gather | solution.py:316
  30.9 38.6 %collective-permute-start = (bf16[1,1,256,1152]{3,2,1,0:T(8,128)(2,1)S(1)}, bf16[1,1,256,1152]{3,2,1,0:T(8,128)(2,1)}, u32[]{:S(2)}, u32[]{:S(2)}) collective-permute-start(bf16[1,1,256,1152]{3,2,1,0:T(8,128)(2,1)S(1)} %bitcast.442), channel_id=1, source_target_pairs={{0,16},{16,0},{1,17},{17,1},{2,18},{18,2},{3,19},{19,3},{4,20},{20... | collective-permute-start | bytes 1769480 | tf_op jit(solution)/shard_map/ppermute | solution.py:70
  37.1 4.6 collective-permute-start.2
  45.8 7.8 collective-permute-start.4
  55.0 6.7 collective-permute-start.5
  257.5 28.6 %all-to-all-start = ((bf16[16,2,9216]{2,1,0:T(2,128)(2,1)}), bf16[16,2,9216]{2,1,0:T(2,128)(2,1)S(1)}, u32[]{:S(2)}, u32[]{:S(2)}) async-start(bf16[16,2,9216]{2,1,0:T(2,128)(2,1)} %reshape.800), calls=%async_computation | async-start | bytes 1179648 | tf_op jit(solution)/shard_map/all_to_all | solution.py:341
  286.9 29.5 %all-to-all-start.2 = ((bf16[16,2,9216]{2,1,0:T(2,128)(2,1)}), bf16[16,2,9216]{2,1,0:T(2,128)(2,1)S(1)}, u32[]{:S(2)}, u32[]{:S(2)}) async-start(bf16[16,2,9216]{2,1,0:T(2,128)(2,1)} %reshape.802), calls=%async_computation.2 | async-start | bytes 1179648 | tf_op jit(solution)/shard_map/all_to_all | solution.py:341
  298.7 502.2 %reduce-scatter.5.cloned.1.call-start = ((), (), s32[]{:S(2)}) async-start(), calls=%async_computation.9 | async-start | bytes 16920576 | tf_op jit(solution)/shard_map/reduce_scatter | solution.py:322
  304.4 16.5 %collective-permute-start.8 = (bf16[1,1,256,1152]{3,2,0,1:T(8,128)(2,1)}, bf16[1,1,256,1152]{3,2,0,1:T(8,128)(2,1)}, u32[]{:S(2)}, u32[]{:S(2)}) collective-permute-start(bf16[1,1,256,1152]{3,2,0,1:T(8,128)(2,1)} %bitcast.401), channel_id=1, source_target_pairs={{0,16},{16,0},{1,17},{17,1},{2,18},{18,2},{3,19},{19,3},{4,20},{20... | collective-permute-start | bytes 1769480 | tf_op jit(solution)/shard_map/ppermute | solution.py:70
  320.9 102.0 %collective-permute-start.11 = (bf16[1,1,256,1152]{3,2,0,1:T(8,128)(2,1)}, bf16[1,1,256,1152]{3,2,0,1:T(8,128)(2,1)}, u32[]{:S(2)}, u32[]{:S(2)}) collective-permute-start(bf16[1,1,256,1152]{3,2,0,1:T(8,128)(2,1)} %bitcast.400), channel_id=1, source_target_pairs={{0,16},{16,0},{1,17},{17,1},{2,18},{18,2},{3,19},{19,3},{4,20},{20... | collective-permute-start | bytes 1769480 | tf_op jit(solution)/shard_map/ppermute | solution.py:70
  441.8 25.7 %collective-permute-start.10 = (bf16[2,256,1152]{2,1,0:T(8,128)(2,1)S(1)}, bf16[2,256,1152]{2,1,0:T(8,128)(2,1)S(1)}, u32[]{:S(2)}, u32[]{:S(2)}) collective-permute-start(bf16[2,256,1152]{2,1,0:T(8,128)(2,1)S(1)} %fusion.33), channel_id=1, source_target_pairs={{0,16},{16,0},{1,17},{17,1},{2,18},{18,2},{3,19},{19,3},{4,20},{20... | collective-permute-start | bytes 3538952 | tf_op jit(solution)/shard_map/ppermute | solution.py:70
  454.9 11.4 %collective-permute-start.12 = (bf16[2,256,1152]{2,1,0:T(8,128)(2,1)S(1)}, bf16[2,256,1152]{2,1,0:T(8,128)(2,1)S(1)}, u32[]{:S(2)}, u32[]{:S(2)}) collective-permute-start(bf16[2,256,1152]{2,1,0:T(8,128)(2,1)S(1)} %fusion.34), channel_id=1, source_target_pairs={{0,16},{16,0},{1,17},{17,1},{2,18},{18,2},{3,19},{19,3},{4,20},{20... | collective-permute-start | bytes 3538952 | tf_op jit(solution)/shard_map/ppermute | solution.py:70
  523.9 534.8 %reduce-scatter.3.cloned.1.call-start = ((), (), s32[]{:S(2)}) async-start(), calls=%async_computation.8 | async-start | bytes 16920576 | tf_op jit(solution)/shard_map/reduce_scatter | solution.py:322
  583.5 11.1 %collective-permute-start.15 = (bf16[2,256,1152]{2,1,0:T(8,128)(2,1)S(1)}, bf16[2,256,1152]{2,1,0:T(8,128)(2,1)S(1)}, u32[]{:S(2)}, u32[]{:S(2)}) collective-permute-start(bf16[2,256,1152]{2,1,0:T(8,128)(2,1)S(1)} %fusion.36), channel_id=1, source_target_pairs={{0,16},{16,0},{1,17},{17,1},{2,18},{18,2},{3,19},{19,3},{4,20},{20... | collective-permute-start | bytes 3538952 | tf_op jit(solution)/shard_map/ppermute | solution.py:70
  658.3 10.3 collective-permute-start.16
  681.8 27.6 %collective-permute-start.17 = (f32[8,7488]{1,0:T(8,128)S(1)}, f32[8,7488]{1,0:T(8,128)S(1)}, u32[]{:S(2)}, u32[]{:S(2)}) collective-permute-start(f32[8,7488]{1,0:T(8,128)S(1)} %slice_select_fusion), channel_id=1, source_target_pairs={{0,8},{1,9},{2,10},{3,11},{4,12},{5,13},{6,14},{7,15},{8,0},{9,1},... | collective-permute-start | bytes 718856 | tf_op jit(solution)/shard_map/ppermute | solution.py:70
  709.5 15.4 %collective-permute-start.18 = (f32[4,7488]{1,0:T(4,128)S(1)}, f32[4,7488]{1,0:T(4,128)S(1)}, u32[]{:S(2)}, u32[]{:S(2)}) collective-permute-start(f32[4,7488]{1,0:T(4,128)S(1)} %slice_select_fusion.1), channel_id=1, source_target_pairs={{0,4},{1,5},{2,6},{3,7},{4,0},{5,1},{6,2},{7,3},{8,12},{9,13},{10,... | collective-permute-start | bytes 359432 | tf_op jit(solution)/shard_map/ppermute | solution.py:70
  725.0 6.3 collective-permute-start.19
  727.4 24.7 %all-to-all-start.1 = ((bf16[16,16,1152]{2,1,0:T(8,128)(2,1)}), bf16[16,16,1152]{2,1,0:T(8,128)(2,1)S(1)}, u32[]{:S(2)}, u32[]{:S(2)}) async-start(bf16[16,16,1152]{2,1,0:T(8,128)(2,1)} %bitcast.441), calls=%async_computation.1 | async-start | bytes 1179648 | tf_op jit(solution)/shard_map/all_to_all | solution.py:354
  731.4 20.7 %collective-permute-start.20 = (f32[1,7488]{1,0:T(1,128)S(1)}, f32[1,7488]{1,0:T(1,128)S(1)}, u32[]{:S(2)}, u32[]{:S(2)}) collective-permute-start(f32[1,7488]{1,0:T(1,128)S(1)} %broadcast_select_fusion.23), channel_id=1, source_target_pairs={{0,1},{1,0},{2,3},{3,2},{4,5},{5,4},{6,7},{7,6},{8,9},{9,8},{10,11... | collective-permute-start | bytes 89864 | tf_op jit(solution)/shard_map/ppermute | solution.py:70
  761.7 3.9 collective-permute-start.24
  765.6 4.6 collective-permute-start.25
  768.0 10.2 collective-permute-start.21
  801.9 4.1 collective-permute-start.31
  803.0 7.0 collective-permute-start.30
  805.5 15.5 %collective-permute-start.33 = (bf16[1,72,2304]{2,1,0:T(8,128)(2,1)}, bf16[1,72,2304]{2,1,0:T(8,128)(2,1)}, u32[]{:S(2)}, u32[]{:S(2)}) collective-permute-start(bf16[1,72,2304]{2,1,0:T(8,128)(2,1)} %get-tuple-element.107), channel_id=1, source_target_pairs={{0,16},{16,0},{1,17},{17,1},{2,18},{18,2},{3,19},{19,3},{4,20},{20... | collective-permute-start | bytes 995336 | tf_op jit(solution)/shard_map/ppermute | solution.py:70
  805.5 15.5 %collective-permute-start.32 = (bf16[1,72,2304]{2,1,0:T(8,128)(2,1)}, bf16[1,72,2304]{2,1,0:T(8,128)(2,1)}, u32[]{:S(2)}, u32[]{:S(2)}) collective-permute-start(bf16[1,72,2304]{2,1,0:T(8,128)(2,1)} %get-tuple-element.108), channel_id=1, source_target_pairs={{0,16},{16,0},{1,17},{17,1},{2,18},{18,2},{3,19},{19,3},{4,20},{20... | collective-permute-start | bytes 995336 | tf_op jit(solution)/shard_map/ppermute | solution.py:70
  1059.7 4.1 collective-permute-start.27
  1060.7 7.0 collective-permute-start.26
  1063.3 15.5 %collective-permute-start.29 = (bf16[1,72,2304]{2,1,0:T(8,128)(2,1)}, bf16[1,72,2304]{2,1,0:T(8,128)(2,1)}, u32[]{:S(2)}, u32[]{:S(2)}) collective-permute-start(bf16[1,72,2304]{2,1,0:T(8,128)(2,1)} %get-tuple-element.111), channel_id=1, source_target_pairs={{0,16},{16,0},{1,17},{17,1},{2,18},{18,2},{3,19},{19,3},{4,20},{20... | collective-permute-start | bytes 995336 | tf_op jit(solution)/shard_map/ppermute | solution.py:70
  1063.3 15.5 %collective-permute-start.28 = (bf16[1,72,2304]{2,1,0:T(8,128)(2,1)}, bf16[1,72,2304]{2,1,0:T(8,128)(2,1)}, u32[]{:S(2)}, u32[]{:S(2)}) collective-permute-start(bf16[1,72,2304]{2,1,0:T(8,128)(2,1)} %get-tuple-element.112), channel_id=1, source_target_pairs={{0,16},{16,0},{1,17},{17,1},{2,18},{18,2},{3,19},{19,3},{4,20},{20... | collective-permute-start | bytes 995336 | tf_op jit(solution)/shard_map/ppermute | solution.py:70
  (112 other events, 1469.8 us)
Sparse Core Ops, SparseCore 0:
  17.0 187.3 all-gather.2
  207.8 201.4 all-gather.4
  524.0 276.8 reduce-scatter.4
  806.6 252.0 reduce-scatter.2

commit v2 on v1

--- a/solution.py
+++ b/solution.py
@@ -4,6 +4,8 @@
 import jax
 import jax.numpy as jnp
 from jax import lax
+from jax.experimental import pallas as pl
+from jax.experimental.pallas import tpu as pltpu
 from jax.sharding import PartitionSpec as P
 
 HEADS = 16
@@ -107,6 +109,139 @@
         kept = jnp.where(upper, high, low)
         values = kept + flip(away, axis, size, bit)
     return values[0]
+
+
+def tie(values, others):
+    values = list(values)
+    return lax.optimization_barrier(tuple(values) + tuple(others))[: len(values)]
+
+
+def pick(values, axis, index):
+    return lax.dynamic_index_in_dim(values, index, axis, keepdims=False)
+
+
+def add_low(left, right):
+    return (left.astype(F32) + right.astype(F32)).astype(BF16)
+
+
+def hop(values, lay, bit):
+    return flip(values, "sp", lay.chips, bit)
+
+
+def turn(values, lay, offset):
+    count = lay.chips
+    return lax.ppermute(values, "sp", [(i, (i + 4 * offset) % count) for i in range(count)])
+
+
+def put_kernel(depth, cut, held_ref, x_ref, y_ref, low_ref, high_ref, out_ref):
+    chip = lax.axis_index("sp")
+    z, y, x = chip // 4, lax.rem(chip // 2, 2), lax.rem(chip, 2)
+    for k in range(depth):
+        layer = lax.rem(z + depth - k, depth)
+        out_ref[layer, y, x] = held_ref[k]
+        out_ref[layer, y, 1 - x] = x_ref[k]
+        out_ref[layer, 1 - y, x] = y_ref[k]
+        out_ref[layer, 1 - y, 1 - x, :, :cut] = low_ref[k]
+        out_ref[layer, 1 - y, 1 - x, :, cut:] = high_ref[k]
+
+
+def put_rows(arrays, cut):
+    depth, rows, columns = arrays[0].shape
+    whole = pl.pallas_call(
+        partial(put_kernel, depth, cut),
+        out_shape=jax.ShapeDtypeStruct((depth, 2, 2, rows, columns), BF16),
+        in_specs=[pl.BlockSpec(memory_space=pltpu.VMEM)] * 5,
+        out_specs=pl.BlockSpec(memory_space=pltpu.VMEM),
+        compiler_params=pltpu.CompilerParams(vmem_limit_bytes=24 << 20),
+        cost_estimate=pl.CostEstimate(
+            flops=0, transcendentals=0, bytes_accessed=16 * depth * rows * columns
+        ),
+        name="put_rows",
+    )(*arrays)
+    return whole.reshape(depth * 4 * rows, columns)
+
+
+def cut_of(columns):
+    return columns // 256 * 128
+
+
+class Gather:
+    def __init__(self, lay):
+        self.lay = lay
+        self.layers = []
+        self.sides = []
+        self.corners = []
+
+    def chunk(self, shard):
+        lay = self.lay
+        cut = cut_of(shard.shape[1])
+        after = (self.layers[-1] if self.layers else []) + (
+            self.corners[-2] if len(self.corners) > 1 else []
+        )
+        if after:
+            (shard,) = tie([shard], after)
+        layers = [turn(shard, lay, k) for k in range(1, lay.chips // 4)]
+        held = jnp.stack([shard] + layers)
+        if self.sides:
+            (held,) = tie([held], self.sides[-1])
+        along_x, along_y = hop(held, lay, 1), hop(held, lay, 2)
+        low = hop(along_x[:, :, :cut], lay, 2)
+        high = hop(along_y[:, :, cut:], lay, 1)
+        self.layers.append(layers)
+        self.sides.append([along_x, along_y])
+        self.corners.append([low, high])
+        return put_rows([held, along_x, along_y, low, high], cut)
+
+
+class Scatter:
+    def __init__(self, lay):
+        self.lay = lay
+        self.layers = []
+        self.sides = []
+        self.corners = []
+
+    def chunk(self, grad):
+        lay = self.lay
+        depth = lay.chips // 4
+        chip = lax.axis_index("sp")
+        z, y, x = chip // 4, (chip // 2) % 2, chip % 2
+        cut = cut_of(grad.shape[1])
+        grid = grad.reshape(depth, 2, 2, -1, grad.shape[1])
+
+        def at(row, column):
+            return pick(pick(grid, 1, row), 1, column)
+
+        corner = at(1 - y, 1 - x)
+        low, high = corner[..., :cut], corner[..., cut:]
+        after = (self.corners[-1] if self.corners else []) + (
+            self.sides[-2] if len(self.sides) > 1 else []
+        )
+        if after:
+            low, high = tie([low, high], after)
+        low_got, high_got = hop(low, lay, 2), hop(high, lay, 1)
+        side_x, side_y = at(y, 1 - x), at(1 - y, x)
+        send_x = jnp.concatenate([add_low(side_x[..., :cut], low_got), side_x[..., cut:]], axis=-1)
+        send_y = jnp.concatenate([side_y[..., :cut], add_low(side_y[..., cut:], high_got)], axis=-1)
+        if len(self.layers) > 1:
+            send_x, send_y = tie([send_x, send_y], self.layers[-2])
+        got_x, got_y = hop(send_x, lay, 1), hop(send_y, lay, 2)
+        own = at(y, x)
+
+        def part(layer):
+            return (
+                pick(own, 0, layer).astype(F32)
+                + pick(got_x, 0, layer).astype(F32)
+                + pick(got_y, 0, layer).astype(F32)
+            )
+
+        layers = [turn(part((z + k) % depth).astype(BF16), lay, k) for k in range(1, depth)]
+        total = part(z)
+        for got in layers:
+            total = total + got.astype(F32)
+        self.layers.append(layers)
+        self.sides.append([got_x, got_y])
+        self.corners.append([low_got, high_got])
+        return total
 
 
 def attention_scores(query, key, stride):
@@ -252,7 +387,6 @@
     grad_hidden = gradient + norm_back(grad_mlp_input * (1.0 + scale_mlp), normed_mlp, inverse_mlp)
     grad_gate_att = jnp.sum(grad_hidden * branch, axis=1)
     grad_branch = (grad_hidden * gate_att).astype(BF16)
-    output_grad = contract_first(flat(grad_branch), flat(attended)).astype(BF16)
     grad_attended = project(grad_branch, w_output).astype(BF16)
     grad_query, grad_key, grad_value = attend_back(
         query, key, value, logsum, heads_of(grad_attended, groups, lay), stride
@@ -261,7 +395,15 @@
     grad_key = grad_key.reshape(groups, count, share)
     grad_value = grad_value.reshape(groups, count, share)
     grad_projected = jnp.concatenate([grad_query, grad_key, grad_value], axis=-1)
-    input_grad = contract_first(flat(attn_input), flat(grad_projected)).astype(BF16)
+    left = jnp.concatenate([flat(attn_input), flat(grad_branch)], axis=0)
+    right = jnp.concatenate(
+        [
+            jnp.pad(flat(grad_projected), ((0, 0), (0, share))),
+            jnp.pad(flat(attended), ((0, 0), (3 * share, 0))),
+        ],
+        axis=0,
+    )
+    attention_grad = contract_first(left, right).astype(BF16)
     grad_attn_input = core_total(project_rows(grad_projected, w_input), lay)
     grad_scale_att = jnp.sum(grad_attn_input * normed_att, axis=1)
     grad_shift_att = jnp.sum(grad_attn_input, axis=1)
@@ -286,7 +428,7 @@
         grad_mod,
         split_biases,
         whole_biases,
-        (input_grad, output_grad, expand_grad, reduce_grad),
+        (attention_grad, expand_grad, reduce_grad),
     )
 
 
@@ -310,17 +452,39 @@
     return jnp.split(values, bounds, axis=-1)
 
 
-def fetch_weights(w_input, w_output, w_expand, w_reduce, lay):
+def fetch_weights(gather, w_input, w_output, w_expand, w_reduce, lay):
+    c_input, c_output, c_expand, c_reduce = shard_parts(w_input, w_output, w_expand, w_reduce, lay)
+    attention = gather.chunk(jnp.concatenate([c_input, c_output], axis=1))
+    expand = gather.chunk(c_expand)
+    reduce = gather.chunk(c_reduce)
+    count = c_input.shape[1]
+    return (attention[:, :count], attention[:, count:], expand, reduce)
+
+
+def fetch_whole(w_input, w_output, w_expand, w_reduce, lay):
     parts = shard_parts(w_input, w_output, w_expand, w_reduce, lay)
-    joined = jnp.concatenate(parts, axis=1)
-    whole = lax.all_gather(joined, "sp", axis=0, tiled=True)
+    whole = lax.all_gather(jnp.concatenate(parts, axis=1), "sp", axis=0, tiled=True)
     return split_columns(whole, [part.shape[1] for part in parts])
 
 
-def reduce_weights(grads, lay):
-    joined = jnp.concatenate(grads, axis=1)
-    summed = lax.psum_scatter(joined, "sp", scatter_dimension=0, tiled=True)
-    return split_columns(summed, [grad.shape[1] for grad in grads])
+def sum_chips(grad):
+    return lax.psum_scatter(grad, "sp", scatter_dimension=0, tiled=True)
+
+
+def reduce_whole(grads):
+    g_attention, g_expand, g_reduce = grads
+    attention = sum_chips(g_attention)
+    count = g_attention.shape[1] * 3 // 4
+    return (attention[:, :count], attention[:, count:], sum_chips(g_expand), sum_chips(g_reduce))
+
+
+def reduce_weights(scatter, grads):
+    g_attention, g_expand, g_reduce = grads
+    reduce = scatter.chunk(g_reduce)
+    expand = scatter.chunk(g_expand)
+    attention = scatter.chunk(g_attention)
+    count = g_attention.shape[1] * 3 // 4
+    return (attention[:, :count], attention[:, count:], expand, reduce)
 
 
 def join_columns(parts, lay):
@@ -402,10 +566,12 @@
     clips = cores * clips_here
     clip_here = chip * frame_count // FRAMES
 
+    gather = Gather(lay)
+    scatter = Scatter(lay)
     spatial_weights = fetch_weights(
-        spatial_input, spatial_output, spatial_expand, spatial_reduce, lay
-    )
-    temporal_weights = fetch_weights(
+        gather, spatial_input, spatial_output, spatial_expand, spatial_reduce, lay
+    )
+    temporal_weights = fetch_whole(
         temporal_input, temporal_output, temporal_expand, temporal_reduce, lay
     )
 
@@ -502,13 +668,13 @@
     grad_between, temporal_dmod, temporal_split, temporal_whole, temporal_grads = block_backward(
         grad_after.astype(F32), temporal_kept, temporal_mod, temporal_weights, local_patches, lay
     )
-    temporal_sums = reduce_weights(temporal_grads, lay)
+    temporal_sums = reduce_whole(temporal_grads)
     own_grad = to_frames(grad_between.astype(BF16), frame_count, lay)
     grad_frames = cube_gather(own_grad, "dp", cores).reshape(-1, patches, width)
     input_grad_all, frame_dmod, spatial_split, spatial_whole, spatial_grads = block_backward(
         grad_frames.astype(F32), spatial_kept, frame_mod, spatial_weights, 1, lay
     )
-    spatial_sums = reduce_weights(spatial_grads, lay)
+    spatial_sums = reduce_weights(scatter, spatial_grads)
     input_grad = own_group(input_grad_all, lay)
 
     grad_positions = jnp.sum(input_grad, axis=0)

time: 1100 us -> 908 us (0.83)
  waiting for transfers between devices: 577 us -> 365 us
  starting transfers between devices: 40.2 us -> 107 us
  local copies, waits for them, and re-layouts: 180 us -> 132 us
  other arithmetic: 79.7 us -> 123 us
  blocking collectives: 36.9 us -> 0 us
    reduce_scatter x2 -> x3, waiting for transfers between devices: 254 us -> 36.8 us  [sum_chips(): return lax.psum_scatter(grad, 'sp', scatter_dimension=0, tiled=True)]
    all_gather x2 -> x1, waiting for transfers between devices: 215 us -> 0.01 us  [fetch_whole(): lax.all_gather(jnp.concatenate(parts, axis=1), 'sp', axis=0, tiled=True)]
    ppermute x34 -> x58, waiting for transfers between devices: 65.1 us -> 250 us  [flip(): return lax.ppermute(values, axis, [(i, i ^ bit) for i in range(size)])]
    ppermute x0 -> x18, waiting for transfers between devices: none -> 67.2 us  [turn(): lax.ppermute(values, 'sp', [(i, (i + 4 * offset) % count) for i in range(...]
    concatenate x4 -> x1, local copies, waits for them, and re-layouts: 57 us -> 2.76 us  [fetch_whole(): jnp.concatenate(parts, axis=1)]
    all_to_all x1 -> x0, blocking collectives: 36.9 us -> none  [to_frames(): return lax.all_to_all(own, 'sp', split_axis=0, concat_axis=1, tiled=True)]
    ppermute x0 -> x18, starting transfers between devices: none -> 34 us  [turn(): lax.ppermute(values, 'sp', [(i, (i + 4 * offset) % count) for i in range(...]
    ppermute x34 -> x58, starting transfers between devices: 20.7 us -> 52.5 us  [flip(): return lax.ppermute(values, axis, [(i, i ^ bit) for i in range(size)])]
  transfers between devices with their start and end apart: 41 -> 84, of which waited for: 22 -> 35; matrix products, arithmetic and copies ran while one was open for 29% -> 39% of each run, Pallas kernels for 0% -> 0%
where the time goes in v2:
time: 908 us; the launch traced here: 899 us
  waiting for transfers between devices  365 us (40%)
  matrix products  149 us (16%)
  local copies, waits for them, and re-layouts  132 us (15%)
  other arithmetic  123 us (14%)
  starting transfers between devices  107 us (12%)
  between operations  19.8 us (2%)
    ppermute x58, waiting for transfers between devices, flip(): return lax.ppermute(values, axis, [(i, i ^ bit) for i in range(size)])  250 us
    ppermute x18, waiting for transfers between devices, turn(): lax.ppermute(values, 'sp', [(i, (i + 4 * offset) % count) for i in range(...  67.2 us
    ppermute x58, starting transfers between devices, flip(): return lax.ppermute(values, axis, [(i, i ^ bit) for i in range(size)])  52.5 us
    dot_general x11, matrix products, contract_first(): lax.dot_general(left_rows, right_rows, (((0,), (0,)), ((), ())), preferre...  46.8 us
    dot_general x10, matrix products, project_rows(): lax.dot_general(left_rows, weight, (((left_rows.ndim - 1,), (1,)), ((), (...  44.5 us
    dot_general x12, matrix products, project(): lax.dot_general(left_rows, weight, (((left_rows.ndim - 1,), (0,)), ((), (...  44.3 us
    unnamed x374, local copies, waits for them, and re-layouts  37 us
    reduce_scatter x3, waiting for transfers between devices, sum_chips(): return lax.psum_scatter(grad, 'sp', scatter_dimension=0, tiled=True)  36.8 us
  transfers between devices with their start and end apart: 84, of which 35 were waited for; matrix products, arithmetic and copies ran while one was open for 39% of the time, Pallas kernels for 0%

profile of v2, /device:TPU:0, one launch (start us, length us, event | category | flops | bytes accessed | tf_op | source)
XLA Modules:
  0.0 898.8 jit_solution(10216719697729365855)
XLA Ops:
  51.0 15.2 %collective-permute-done.4 = f32[4,2880]{1,0:T(4,128)} collective-permute-done((f32[4,2880]{1,0:T(4,128)S(1)}, f32[4,2880]{1,0:T(4,128)}, u32[]{:S(2)}, u32[]{:S(2)}) %collective-permute-start.4) | collective-permute-done | bytes 46112 | tf_op jit(solution)/shard_map/ppermute | solution.py:72
  74.5 7.1 collective-permute-done.5
  108.8 36.1 %collective-permute-done.9.x_ref = bf16[4,72,2304]{2,1,0:T(8,128)(2,1)S(1)} collective-permute-done((bf16[4,72,2304]{2,1,0:T(8,128)(2,1)S(1)}, bf16[4,72,2304]{2,1,0:T(8,128)(2,1)S(1)}, u32[]{:S(2)}, u32[]{:S(2)}) %collective-permute-start.9) | collective-permute-done | bytes 1327136 | tf_op jit(solution)/shard_map/ppermute | solution.py:72
  149.8 13.0 %collective-permute-done.11.low_ref = bf16[4,72,1152]{2,1,0:T(8,128)(2,1)S(1)} collective-permute-done((bf16[4,72,1152]{2,1,0:T(8,128)(2,1)S(1)}, bf16[4,72,1152]{2,1,0:T(8,128)(2,1)S(1)}, u32[]{:S(2)}, u32[]{:S(2)}) %collective-permute-start.11) | collective-permute-done | bytes 663584 | tf_op jit(solution)/shard_map/ppermute | solution.py:72
  177.1 10.0 %collective-permute-done.21 = bf16[72,2304]{1,0:T(8,128)(2,1)S(1)} collective-permute-done((bf16[72,2304]{1,0:T(8,128)(2,1)S(1)}, bf16[72,2304]{1,0:T(8,128)(2,1)S(1)}, u32[]{:S(2)}, u32[]{:S(2)}) %collective-permute-start.21) | collective-permute-done | bytes 331808 | tf_op jit(solution)/shard_map/ppermute | solution.py:133
  190.9 22.1 %collective-permute-done.22 = bf16[72,2304]{1,0:T(8,128)(2,1)S(1)} collective-permute-done((bf16[72,2304]{1,0:T(8,128)(2,1)S(1)}, bf16[72,2304]{1,0:T(8,128)(2,1)S(1)}, u32[]{:S(2)}, u32[]{:S(2)}) %collective-permute-start.22) | collective-permute-done | bytes 331808 | tf_op jit(solution)/shard_map/ppermute | solution.py:133
  213.0 8.8 collective-permute-done.23
  235.5 54.2 %collective-permute-done.19.low_ref = bf16[4,72,1152]{2,1,0:T(8,128)(2,1)S(1)} collective-permute-done((bf16[4,72,1152]{2,1,0:T(8,128)(2,1)S(1)}, bf16[4,72,1152]{2,1,0:T(8,128)(2,1)S(1)}, u32[]{:S(2)}, u32[]{:S(2)}) %collective-permute-start.19) | collective-permute-done | bytes 663584 | tf_op jit(solution)/shard_map/ppermute | solution.py:72
  298.8 10.1 %collective-permute-done.26.low_ref = bf16[4,72,1152]{2,1,0:T(8,128)(2,1)S(1)} collective-permute-done((bf16[4,72,1152]{2,1,0:T(8,128)(2,1)S(1)}, bf16[4,72,1152]{2,1,0:T(8,128)(2,1)S(1)}, u32[]{:S(2)}, u32[]{:S(2)}) %collective-permute-start.26) | collective-permute-done | bytes 663584 | tf_op jit(solution)/shard_map/ppermute | solution.py:72
  341.3 6.0 reduce.34
  395.4 6.0 convolution_add_fusion
  409.0 8.2 convert_reduce_fusion
  417.2 7.1 fusion.48
  424.7 5.5 fusion.2
  430.2 9.3 %fusion.47 = bf16[2,256,1152]{2,1,0:T(8,128)(2,1)} fusion(bf16[1152,6912]{1,0:T(8,128)(2,1)} %all-gather.2.cloned.1.call-done, f32[2,256,2304]{2,1,0:T(8,128)} %copy-done.166), kind=kOutput, calls=%fused_computation.88 | convolution fusion | flops 2729115648 | bytes 11206656 | tf_op jit(solution)/shard_map/dot_general | solution.py:45
  444.1 5.9 convert_reduce_fusion.4
  474.0 7.0 all-to-all-start.3
  492.2 5.4 all-to-all-done.3
  502.0 10.2 %convolution_convert_fusion = bf16[1152,2304]{1,0:T(8,128)(2,1)} fusion(bf16[512,576]{0,1:T(8,128)(2,1)} %bitcast.670, bf16[512,2304]{0,1:T(8,128)(2,1)} %fusion.57, bf16[512,1152]{1,0:T(8,128)(2,1)} %bitcast.662, bf16[512,1152]{1,0:T(8,128)(2,1)} %fusion.66), kind=kOutput, calls=%fused_computation.10 | convolution fusion | flops 5457346560 | bytes 10616832 | tf_op jit(solution)/shard_map/dot_general | solution.py:54
  519.8 5.9 fusion.1
  525.8 10.5 %convert_reduce_fusion.1 = (f32[2304]{0:T(1024)S(1)}, bf16[2,256,2304]{2,1,0:T(8,128)(2,1)S(1)}) fusion(f32[2,256,2304]{2,1,0:T(8,128)} %copy-done.165, bf16[1152,2304,1]{1,0,2:T(8,128)(2,1)} %bitcast.591, bf16[1,256,1152]{2,1,0:T(8,128)(2,1)S(1)} %bitcast.624, bf16[1,256,1152]{2,1,0:T(8,128)(2,1)S(1)} %bitcast.623, f32[2,1152]{1,0:T(2,128)S(1)} %copy-done.113), kind=kOutput, calls=%fused_computation.53 | convolution fusion | flops 2746218240 | bytes 13584384 | tf_op jit(solution)/shard_map/dot_general | solution.py:36
  557.3 6.8 collective-permute-done.48
  591.5 6.8 convolution_convert_fusion.1
  613.6 9.8 %collective-permute-done.49 = bf16[4,72,1152]{2,1,0:T(8,128)(2,1)} collective-permute-done((bf16[4,72,1152]{2,1,0:T(8,128)(2,1)}, bf16[4,72,1152]{2,1,0:T(8,128)(2,1)}, u32[]{:S(2)}, u32[]{:S(2)}) %collective-permute-start.49) | collective-permute-done | bytes 663584 | tf_op jit(solution)/shard_map/ppermute | solution.py:72
  652.8 5.7 collective-permute-done.56
  667.2 16.8 %collective-permute-done.38 = f32[8,7488]{1,0:T(8,128)S(1)} collective-permute-done((f32[8,7488]{1,0:T(8,128)S(1)}, f32[8,7488]{1,0:T(8,128)S(1)}, u32[]{:S(2)}, u32[]{:S(2)}) %collective-permute-start.38) | collective-permute-done | bytes 239648 | tf_op jit(solution)/shard_map/ppermute | solution.py:72
  700.2 9.1 %collective-permute-start.41 = (f32[1,7488]{1,0:T(1,128)S(1)}, f32[1,7488]{1,0:T(1,128)S(1)}, u32[]{:S(2)}, u32[]{:S(2)}) collective-permute-start(f32[1,7488]{1,0:T(1,128)S(1)} %broadcast_select_fusion.23), channel_id=1, source_target_pairs={{0,1},{1,0},{2,3},{3,2},{4,5},{5,4},{6,7},{7,6},{8,9},{9,8},{10,11... | collective-permute-start | bytes 89864 | tf_op jit(solution)/shard_map/ppermute | solution.py:72
  718.7 17.6 %collective-permute-done.43 = f32[2,1152]{1,0:T(2,128)S(1)} collective-permute-done((f32[2,1152]{1,0:T(2,128)S(1)}, f32[2,1152]{1,0:T(2,128)S(1)}, u32[]{:S(2)}, u32[]{:S(2)}) %collective-permute-start.43) | collective-permute-done | bytes 9248 | tf_op jit(solution)/shard_map/ppermute | solution.py:72
  760.9 34.8 %collective-permute-done.59 = bf16[4,72,2304]{2,1,0:T(8,128)(2,1)} collective-permute-done((bf16[4,72,2304]{2,1,0:T(8,128)(2,1)}, bf16[4,72,2304]{2,1,0:T(8,128)(2,1)}, u32[]{:S(2)}, u32[]{:S(2)}) %collective-permute-start.59) | collective-permute-done | bytes 1327136 | tf_op jit(solution)/shard_map/ppermute | solution.py:72
  803.1 7.3 collective-permute-done.60
  810.4 13.3 %collective-permute-done.61 = bf16[72,2304]{1,0:T(8,128)(2,1)S(1)} collective-permute-done((bf16[72,2304]{1,0:T(8,128)(2,1)S(1)}, bf16[72,2304]{1,0:T(8,128)(2,1)S(1)}, u32[]{:S(2)}, u32[]{:S(2)}) %collective-permute-start.61) | collective-permute-done | bytes 331808 | tf_op jit(solution)/shard_map/ppermute | solution.py:133
  840.5 36.8 %reduce-scatter.4.cloned.1.call-done = bf16[72,2304]{1,0:T(8,128)(2,1)} async-done(((bf16[1152,2304]{1,0:T(8,128)(2,1)}), bf16[72,2304]{1,0:T(8,128)(2,1)}) %reduce-scatter.4.cloned.1.call-update) | async-done | bytes 331792 | tf_op jit(solution)/shard_map/reduce_scatter | solution.py:471
  (860 shorter events, 450.7 us)
Async XLA Ops:
  7.2 361.1 %all-gather.2.cloned.1.call-start = ((), (), s32[]{:S(2)}) async-start(), calls=%async_computation.7 | async-start | bytes 16920576 | tf_op jit(solution)/shard_map/all_gather | solution.py:466
  21.8 74.4 %collective-permute-start.6 = (bf16[72,2304]{1,0:T(8,128)(2,1)}, bf16[72,2304]{1,0:T(8,128)(2,1)}, u32[]{:S(2)}, u32[]{:S(2)}) collective-permute-start(bf16[72,2304]{1,0:T(8,128)(2,1)} %pad_maximum_fusion.10), channel_id=1, source_target_pairs={{0,4},{1,5},{2,6},{3,7},{4,8},{5,9},{6,10},{7,11},{8,12},{9,13},{1... | collective-permute-start | bytes 995336 | tf_op jit(solution)/shard_map/ppermute | solution.py:133
  24.8 71.4 %collective-permute-start.7 = (bf16[72,2304]{1,0:T(8,128)(2,1)}, bf16[72,2304]{1,0:T(8,128)(2,1)}, u32[]{:S(2)}, u32[]{:S(2)}) collective-permute-start(bf16[72,2304]{1,0:T(8,128)(2,1)} %pad_maximum_fusion.10), channel_id=1, source_target_pairs={{0,8},{1,9},{2,10},{3,11},{4,12},{5,13},{6,14},{7,15},{8,0},{9,1},... | collective-permute-start | bytes 995336 | tf_op jit(solution)/shard_map/ppermute | solution.py:133
  27.4 68.8 %collective-permute-start.8 = (bf16[72,2304]{1,0:T(8,128)(2,1)}, bf16[72,2304]{1,0:T(8,128)(2,1)}, u32[]{:S(2)}, u32[]{:S(2)}) collective-permute-start(bf16[72,2304]{1,0:T(8,128)(2,1)} %pad_maximum_fusion.10), channel_id=1, source_target_pairs={{0,12},{1,13},{2,14},{3,15},{4,0},{5,1},{6,2},{7,3},{8,4},{9,5},{1... | collective-permute-start | bytes 995336 | tf_op jit(solution)/shard_map/ppermute | solution.py:133
  31.4 71.6 %collective-permute-start = (bf16[1,1,256,1152]{3,2,1,0:T(8,128)(2,1)}, bf16[1,1,256,1152]{3,2,1,0:T(8,128)(2,1)}, u32[]{:S(2)}, u32[]{:S(2)}) collective-permute-start(bf16[1,1,256,1152]{3,2,1,0:T(8,128)(2,1)} %bitcast.663), channel_id=1, source_target_pairs={{0,16},{16,0},{1,17},{17,1},{2,18},{18,2},{3,19},{19,3},{4,20},{20... | collective-permute-start | bytes 1769480 | tf_op jit(solution)/shard_map/ppermute | solution.py:72
  97.8 47.1 %collective-permute-start.9 = (bf16[4,72,2304]{2,1,0:T(8,128)(2,1)S(1)}, bf16[4,72,2304]{2,1,0:T(8,128)(2,1)S(1)}, u32[]{:S(2)}, u32[]{:S(2)}) collective-permute-start(bf16[4,72,2304]{2,1,0:T(8,128)(2,1)S(1)} %pad_maximum_fusion.held_ref), channel_id=1, source_target_pairs={{0,1},{1,0},{2,3},{3,2},{4,5},{5,4},{6,7},{7,6},{8,9},{9,8},{10,11... | collective-permute-start | bytes 3981320 | tf_op jit(solution)/shard_map/ppermute | solution.py:72
  99.4 47.1 %collective-permute-start.10 = (bf16[4,72,2304]{2,1,0:T(8,128)(2,1)S(1)}, bf16[4,72,2304]{2,1,0:T(8,128)(2,1)S(1)}, u32[]{:S(2)}, u32[]{:S(2)}) collective-permute-start(bf16[4,72,2304]{2,1,0:T(8,128)(2,1)S(1)} %pad_maximum_fusion.held_ref), channel_id=1, source_target_pairs={{0,2},{1,3},{2,0},{3,1},{4,6},{5,7},{6,4},{7,5},{8,10},{9,11},{10,... | collective-permute-start | bytes 3981320 | tf_op jit(solution)/shard_map/ppermute | solution.py:72
  100.9 46.6 %collective-permute-start.14 = (bf16[72,2304]{1,0:T(8,128)(2,1)S(1)}, bf16[72,2304]{1,0:T(8,128)(2,1)S(1)}, u32[]{:S(2)}, u32[]{:S(2)}) collective-permute-start(bf16[72,2304]{1,0:T(8,128)(2,1)S(1)} %constant_dynamic-slice_fusion.13), channel_id=1, source_target_pairs={{0,4},{1,5},{2,6},{3,7},{4,8},{5,9},{6,10},{7,11},{8,12},{9,13},{1... | collective-permute-start | bytes 995336 | tf_op jit(solution)/shard_map/ppermute | solution.py:133
  100.9 46.6 %collective-permute-start.15 = (bf16[72,2304]{1,0:T(8,128)(2,1)S(1)}, bf16[72,2304]{1,0:T(8,128)(2,1)S(1)}, u32[]{:S(2)}, u32[]{:S(2)}) collective-permute-start(bf16[72,2304]{1,0:T(8,128)(2,1)S(1)} %constant_dynamic-slice_fusion.13), channel_id=1, source_target_pairs={{0,8},{1,9},{2,10},{3,11},{4,12},{5,13},{6,14},{7,15},{8,0},{9,1},... | collective-permute-start | bytes 995336 | tf_op jit(solution)/shard_map/ppermute | solution.py:133
  103.1 44.4 %collective-permute-start.16 = (bf16[72,2304]{1,0:T(8,128)(2,1)S(1)}, bf16[72,2304]{1,0:T(8,128)(2,1)S(1)}, u32[]{:S(2)}, u32[]{:S(2)}) collective-permute-start(bf16[72,2304]{1,0:T(8,128)(2,1)S(1)} %constant_dynamic-slice_fusion.13), channel_id=1, source_target_pairs={{0,12},{1,13},{2,14},{3,15},{4,0},{5,1},{6,2},{7,3},{8,4},{9,5},{1... | collective-permute-start | bytes 995336 | tf_op jit(solution)/shard_map/ppermute | solution.py:133
  147.7 75.4 %collective-permute-start.17 = (bf16[4,72,2304]{2,1,0:T(8,128)(2,1)S(1)}, bf16[4,72,2304]{2,1,0:T(8,128)(2,1)S(1)}, u32[]{:S(2)}, u32[]{:S(2)}) collective-permute-start(bf16[4,72,2304]{2,1,0:T(8,128)(2,1)S(1)} %pad_maximum_fusion.1.held_ref), channel_id=1, source_target_pairs={{0,1},{1,0},{2,3},{3,2},{4,5},{5,4},{6,7},{7,6},{8,9},{9,8},{10,11... | collective-permute-start | bytes 3981320 | tf_op jit(solution)/shard_map/ppermute | solution.py:72
  149.2 73.9 %collective-permute-start.18 = (bf16[4,72,2304]{2,1,0:T(8,128)(2,1)S(1)}, bf16[4,72,2304]{2,1,0:T(8,128)(2,1)S(1)}, u32[]{:S(2)}, u32[]{:S(2)}) collective-permute-start(bf16[4,72,2304]{2,1,0:T(8,128)(2,1)S(1)} %pad_maximum_fusion.1.held_ref), channel_id=1, source_target_pairs={{0,2},{1,3},{2,0},{3,1},{4,6},{5,7},{6,4},{7,5},{8,10},{9,11},{10,... | collective-permute-start | bytes 3981320 | tf_op jit(solution)/shard_map/ppermute | solution.py:72
  173.4 59.2 %collective-permute-start.13 = (bf16[2,256,1152]{2,1,0:T(8,128)(2,1)}, bf16[2,256,1152]{2,1,0:T(8,128)(2,1)}, u32[]{:S(2)}, u32[]{:S(2)}) collective-permute-start(bf16[2,256,1152]{2,1,0:T(8,128)(2,1)} %convolution_convert_fusion.5), channel_id=1, source_target_pairs={{0,16},{16,0},{1,17},{17,1},{2,18},{18,2},{3,19},{19,3},{4,20},{20... | collective-permute-start | bytes 3538952 | tf_op jit(solution)/shard_map/ppermute | solution.py:72
  173.4 39.6 %collective-permute-start.22 = (bf16[72,2304]{1,0:T(8,128)(2,1)S(1)}, bf16[72,2304]{1,0:T(8,128)(2,1)S(1)}, u32[]{:S(2)}, u32[]{:S(2)}) collective-permute-start(bf16[72,2304]{1,0:T(8,128)(2,1)S(1)} %constant_dynamic-slice_fusion.12), channel_id=1, source_target_pairs={{0,8},{1,9},{2,10},{3,11},{4,12},{5,13},{6,14},{7,15},{8,0},{9,1},... | collective-permute-start | bytes 995336 | tf_op jit(solution)/shard_map/ppermute | solution.py:133
  224.2 67.3 %collective-permute-start.24 = (bf16[4,72,2304]{2,1,0:T(8,128)(2,1)}, bf16[4,72,2304]{2,1,0:T(8,128)(2,1)}, u32[]{:S(2)}, u32[]{:S(2)}) collective-permute-start(bf16[4,72,2304]{2,1,0:T(8,128)(2,1)} %pad_maximum_fusion.2.held_ref), channel_id=1, source_target_pairs={{0,1},{1,0},{2,3},{3,2},{4,5},{5,4},{6,7},{7,6},{8,9},{9,8},{10,11... | collective-permute-start | bytes 3981320 | tf_op jit(solution)/shard_map/ppermute | solution.py:72
  225.9 67.9 %collective-permute-start.25 = (bf16[4,72,2304]{2,1,0:T(8,128)(2,1)}, bf16[4,72,2304]{2,1,0:T(8,128)(2,1)}, u32[]{:S(2)}, u32[]{:S(2)}) collective-permute-start(bf16[4,72,2304]{2,1,0:T(8,128)(2,1)} %pad_maximum_fusion.2.held_ref), channel_id=1, source_target_pairs={{0,2},{1,3},{2,0},{3,1},{4,6},{5,7},{6,4},{7,5},{8,10},{9,11},{10,... | collective-permute-start | bytes 3981320 | tf_op jit(solution)/shard_map/ppermute | solution.py:72
  229.2 60.5 %collective-permute-start.19 = (bf16[4,72,1152]{2,1,0:T(8,128)(2,1)S(1)}, bf16[4,72,1152]{2,1,0:T(8,128)(2,1)S(1)}, u32[]{:S(2)}, u32[]{:S(2)}) collective-permute-start(bf16[4,72,1152]{2,1,0:T(8,128)(2,1)S(1)} %slice.253), channel_id=1, source_target_pairs={{0,2},{1,3},{2,0},{3,1},{4,6},{5,7},{6,4},{7,5},{8,10},{9,11},{10,... | collective-permute-start | bytes 1990664 | tf_op jit(solution)/shard_map/ppermute | solution.py:72
  231.4 59.6 %collective-permute-start.20 = (bf16[4,72,1152]{2,1,0:T(8,128)(2,1)S(1)}, bf16[4,72,1152]{2,1,0:T(8,128)(2,1)S(1)}, u32[]{:S(2)}, u32[]{:S(2)}) collective-permute-start(bf16[4,72,1152]{2,1,0:T(8,128)(2,1)S(1)} %slice.254), channel_id=1, source_target_pairs={{0,1},{1,0},{2,3},{3,2},{4,5},{5,4},{6,7},{7,6},{8,9},{9,8},{10,11... | collective-permute-start | bytes 1990664 | tf_op jit(solution)/shard_map/ppermute | solution.py:72
  359.2 468.7 %reduce-scatter.8.cloned.1.call-start = ((), (), s32[]{:S(2)}) async-start(), calls=%async_computation.10 | async-start | bytes 5640192 | tf_op jit(solution)/shard_map/reduce_scatter | solution.py:471
  409.0 427.5 %reduce-scatter.6.cloned.1.call-start = ((), (), s32[]{:S(2)}) async-start(), calls=%async_computation.9 | async-start | bytes 5640192 | tf_op jit(solution)/shard_map/reduce_scatter | solution.py:471
  501.9 375.5 %reduce-scatter.4.cloned.1.call-start = ((), (), s32[]{:S(2)}) async-start(), calls=%async_computation.8 | async-start | bytes 5640192 | tf_op jit(solution)/shard_map/reduce_scatter | solution.py:471
  566.5 63.7 %collective-permute-start.52 = (bf16[4,72,2304]{2,1,0:T(8,128)(2,1)}, bf16[4,72,2304]{2,1,0:T(8,128)(2,1)}, u32[]{:S(2)}, u32[]{:S(2)}) collective-permute-start(bf16[4,72,2304]{2,1,0:T(8,128)(2,1)} %pad_maximum_fusion.4), channel_id=1, source_target_pairs={{0,2},{1,3},{2,0},{3,1},{4,6},{5,7},{6,4},{7,5},{8,10},{9,11},{10,... | collective-permute-start | bytes 3981320 | tf_op jit(solution)/shard_map/ppermute | solution.py:72
  570.7 59.6 %collective-permute-start.51 = (bf16[4,72,2304]{2,1,0:T(8,128)(2,1)}, bf16[4,72,2304]{2,1,0:T(8,128)(2,1)}, u32[]{:S(2)}, u32[]{:S(2)}) collective-permute-start(bf16[4,72,2304]{2,1,0:T(8,128)(2,1)} %pad_maximum_fusion.3), channel_id=1, source_target_pairs={{0,1},{1,0},{2,3},{3,2},{4,5},{5,4},{6,7},{7,6},{8,9},{9,8},{10,11... | collective-permute-start | bytes 3981320 | tf_op jit(solution)/shard_map/ppermute | solution.py:72
  572.2 51.1 %collective-permute-start.49 = (bf16[4,72,1152]{2,1,0:T(8,128)(2,1)}, bf16[4,72,1152]{2,1,0:T(8,128)(2,1)}, u32[]{:S(2)}, u32[]{:S(2)}) collective-permute-start(bf16[4,72,1152]{2,1,0:T(8,128)(2,1)} %get-tuple-element.42), channel_id=1, source_target_pairs={{0,2},{1,3},{2,0},{3,1},{4,6},{5,7},{6,4},{7,5},{8,10},{9,11},{10,... | collective-permute-start | bytes 1990664 | tf_op jit(solution)/shard_map/ppermute | solution.py:72
  572.9 54.6 %collective-permute-start.50 = (bf16[4,72,1152]{2,1,0:T(8,128)(2,1)}, bf16[4,72,1152]{2,1,0:T(8,128)(2,1)}, u32[]{:S(2)}, u32[]{:S(2)}) collective-permute-start(bf16[4,72,1152]{2,1,0:T(8,128)(2,1)} %get-tuple-element.43), channel_id=1, source_target_pairs={{0,1},{1,0},{2,3},{3,2},{4,5},{5,4},{6,7},{7,6},{8,9},{9,8},{10,11... | collective-permute-start | bytes 1990664 | tf_op jit(solution)/shard_map/ppermute | solution.py:72
  625.8 60.1 %collective-permute-start.65 = (bf16[4,72,2304]{2,1,0:T(8,128)(2,1)}, bf16[4,72,2304]{2,1,0:T(8,128)(2,1)}, u32[]{:S(2)}, u32[]{:S(2)}) collective-permute-start(bf16[4,72,2304]{2,1,0:T(8,128)(2,1)} %pad_maximum_fusion.7), channel_id=1, source_target_pairs={{0,1},{1,0},{2,3},{3,2},{4,5},{5,4},{6,7},{7,6},{8,9},{9,8},{10,11... | collective-permute-start | bytes 3981320 | tf_op jit(solution)/shard_map/ppermute | solution.py:72
  630.0 55.9 %collective-permute-start.66 = (bf16[4,72,2304]{2,1,0:T(8,128)(2,1)}, bf16[4,72,2304]{2,1,0:T(8,128)(2,1)}, u32[]{:S(2)}, u32[]{:S(2)}) collective-permute-start(bf16[4,72,2304]{2,1,0:T(8,128)(2,1)} %pad_maximum_fusion.8), channel_id=1, source_target_pairs={{0,2},{1,3},{2,0},{3,1},{4,6},{5,7},{6,4},{7,5},{8,10},{9,11},{10,... | collective-permute-start | bytes 3981320 | tf_op jit(solution)/shard_map/ppermute | solution.py:72
  652.6 39.6 %collective-permute-start.54 = (bf16[4,72,1152]{2,1,0:T(8,128)(2,1)}, bf16[4,72,1152]{2,1,0:T(8,128)(2,1)S(1)}, u32[]{:S(2)}, u32[]{:S(2)}) collective-permute-start(bf16[4,72,1152]{2,1,0:T(8,128)(2,1)} %get-tuple-element.45), channel_id=1, source_target_pairs={{0,1},{1,0},{2,3},{3,2},{4,5},{5,4},{6,7},{7,6},{8,9},{9,8},{10,11... | collective-permute-start | bytes 1990664 | tf_op jit(solution)/shard_map/ppermute | solution.py:72
  690.2 67.0 %collective-permute-start.67 = (bf16[72,2304]{1,0:T(8,128)(2,1)}, bf16[72,2304]{1,0:T(8,128)(2,1)S(1)}, u32[]{:S(2)}, u32[]{:S(2)}) collective-permute-start(bf16[72,2304]{1,0:T(8,128)(2,1)} %get-tuple-element.92), channel_id=1, source_target_pairs={{0,4},{1,5},{2,6},{3,7},{4,8},{5,9},{6,10},{7,11},{8,12},{9,13},{1... | collective-permute-start | bytes 995336 | tf_op jit(solution)/shard_map/ppermute | solution.py:133
  692.2 65.0 %collective-permute-start.68 = (bf16[72,2304]{1,0:T(8,128)(2,1)}, bf16[72,2304]{1,0:T(8,128)(2,1)}, u32[]{:S(2)}, u32[]{:S(2)}) collective-permute-start(bf16[72,2304]{1,0:T(8,128)(2,1)} %get-tuple-element.94), channel_id=1, source_target_pairs={{0,8},{1,9},{2,10},{3,11},{4,12},{5,13},{6,14},{7,15},{8,0},{9,1},... | collective-permute-start | bytes 995336 | tf_op jit(solution)/shard_map/ppermute | solution.py:133
  692.2 64.9 %collective-permute-start.69 = (bf16[72,2304]{1,0:T(8,128)(2,1)S(1)}, bf16[72,2304]{1,0:T(8,128)(2,1)}, u32[]{:S(2)}, u32[]{:S(2)}) collective-permute-start(bf16[72,2304]{1,0:T(8,128)(2,1)S(1)} %get-tuple-element.93), channel_id=1, source_target_pairs={{0,12},{1,13},{2,14},{3,15},{4,0},{5,1},{6,2},{7,3},{8,4},{9,5},{1... | collective-permute-start | bytes 995336 | tf_op jit(solution)/shard_map/ppermute | solution.py:133
  710.4 50.5 %collective-permute-start.58 = (bf16[4,72,2304]{2,1,0:T(8,128)(2,1)}, bf16[4,72,2304]{2,1,0:T(8,128)(2,1)}, u32[]{:S(2)}, u32[]{:S(2)}) collective-permute-start(bf16[4,72,2304]{2,1,0:T(8,128)(2,1)} %pad_maximum_fusion.5), channel_id=1, source_target_pairs={{0,1},{1,0},{2,3},{3,2},{4,5},{5,4},{6,7},{7,6},{8,9},{9,8},{10,11... | collective-permute-start | bytes 3981320 | tf_op jit(solution)/shard_map/ppermute | solution.py:72
  (223 other events, 2531.3 us)
Sparse Core Ops, SparseCore 0:
  17.0 284.1 all-gather.1
  409.1 144.8 reduce-scatter.7
  559.2 169.8 reduce-scatter.5
  734.3 142.9 reduce-scatter.3

commit v3 on v2

--- a/solution.py
+++ b/solution.py
@@ -200,7 +200,7 @@
         self.sides = []
         self.corners = []
 
-    def chunk(self, grad):
+    def chunk(self, grad, first=(), second=()):
         lay = self.lay
         depth = lay.chips // 4
         chip = lax.axis_index("sp")
@@ -226,6 +226,7 @@
             send_x, send_y = tie([send_x, send_y], self.layers[-2])
         got_x, got_y = hop(send_x, lay, 1), hop(send_y, lay, 2)
         own = at(y, x)
+        got_x, got_y, *first = tie([got_x, got_y] + list(first), [])
 
         def part(layer):
             return (
@@ -235,13 +236,65 @@
             )
 
         layers = [turn(part((z + k) % depth).astype(BF16), lay, k) for k in range(1, depth)]
+        tied = tie(list(layers) + list(second), [])
+        layers, second = tied[: depth - 1], tied[depth - 1 :]
         total = part(z)
         for got in layers:
             total = total + got.astype(F32)
         self.layers.append(layers)
         self.sides.append([got_x, got_y])
         self.corners.append([low_got, high_got])
-        return total
+        return (total, list(first), list(second))
+
+
+def tile_of(columns):
+    for tile in (384, 256, 128):
+        if columns % tile == 0:
+            return tile
+    return columns
+
+
+def fixed_spec(array):
+    return pl.BlockSpec(array.shape, lambda j: (0, 0))
+
+
+def weight_grad(left, right, offset, total, joined=None):
+    depth, rows = left.shape
+    columns = right.shape[1]
+    tile = tile_of(math.gcd(columns, offset) if offset else columns)
+    skip = offset // tile
+
+    def body(left_ref, right_ref, *refs):
+        out_ref, turned_ref = refs[-2:]
+
+        @pl.when(pl.program_id(0) == 0)
+        def _():
+            turned_ref[...] = left_ref[...].T
+
+        out_ref[...] = jnp.dot(
+            turned_ref[...], right_ref[...], preferred_element_type=F32
+        ).astype(BF16)
+
+    held = [] if joined is None else [joined]
+    return pl.pallas_call(
+        body,
+        grid=(columns // tile,),
+        in_specs=[fixed_spec(left), pl.BlockSpec((depth, tile), lambda j: (0, j))]
+        + [pl.BlockSpec(memory_space=pl.ANY)] * len(held),
+        out_specs=pl.BlockSpec((rows, tile), lambda j: (0, j + skip)),
+        out_shape=jax.ShapeDtypeStruct((rows, total), BF16),
+        scratch_shapes=[pltpu.VMEM((rows, depth), BF16)],
+        input_output_aliases={2: 0} if held else {},
+        compiler_params=pltpu.CompilerParams(
+            dimension_semantics=("arbitrary",), vmem_limit_bytes=40 << 20
+        ),
+        cost_estimate=pl.CostEstimate(
+            flops=2 * depth * rows * columns,
+            transcendentals=0,
+            bytes_accessed=2 * (depth * rows + depth * columns + rows * columns),
+        ),
+        name="weight_grad",
+    )(left, right, *held)
 
 
 def attention_scores(query, key, stride):
@@ -306,7 +359,7 @@
     return values.reshape(sequences, -1, lay.heads, HDIM)
 
 
-def block_forward(inputs, modulation, weights, biases, stride, lay):
+def block_forward(inputs, modulation, weights, biases, stride, lay, beside=None):
     w_input, w_output, w_expand, w_reduce = weights
     query_bias, value_bias, output_bias, expand_bias, reduce_bias = biases
     groups, count, width = inputs.shape
@@ -324,6 +377,8 @@
     attended = mixed.reshape(groups, count, share)
     branch = core_total(project_rows(attended, w_output), lay) + output_bias
     hidden = inputs + gate_att * branch
+    if beside is not None:
+        hidden = beside(hidden)
     normed_mlp, inverse_mlp = layer_norm(hidden)
     mlp_input = (normed_mlp * (1.0 + scale_mlp) + shift_mlp).astype(BF16)
     expanded = project(mlp_input, w_expand) + expand_bias
@@ -350,7 +405,7 @@
     return (output, kept)
 
 
-def block_backward(gradient, kept, modulation, weights, stride, lay):
+def block_backward(gradient, kept, modulation, weights, stride, lay, joint=False):
     w_input, w_output, w_expand, w_reduce = weights
     (
         normed_att,
@@ -376,11 +431,20 @@
     )
     grad_gate_mlp = jnp.sum(gradient * reduced, axis=1)
     grad_reduced = (gradient * gate_mlp).astype(BF16)
-    reduce_grad = contract_first(flat(grad_reduced), flat(activated)).astype(BF16)
+    columns = activated.shape[-1]
+    if joint:
+        reduce_grad = contract_first(flat(grad_reduced), flat(activated)).astype(BF16)
+        reduce_grad, grad_reduced = tie([reduce_grad, grad_reduced], [])
+    else:
+        reduce_grad = contract_first(flat(grad_reduced), flat(activated)).astype(BF16)
     grad_activated = project(grad_reduced, w_reduce)
     gelu_back = jax.vjp(partial(jax.nn.gelu, approximate=True), expanded)[1]
     grad_expanded = gelu_back(grad_activated)[0].astype(BF16)
-    expand_grad = contract_first(flat(mlp_input), flat(grad_expanded)).astype(BF16)
+    if joint:
+        joined = weight_grad(flat(mlp_input), flat(grad_expanded), 0, 2 * columns)
+        joined, grad_expanded = tie([joined, grad_expanded], [])
+    else:
+        expand_grad = contract_first(flat(mlp_input), flat(grad_expanded)).astype(BF16)
     grad_mlp_input = core_total(project_rows(grad_expanded, w_expand), lay)
     grad_scale_mlp = jnp.sum(grad_mlp_input * normed_mlp, axis=1)
     grad_shift_mlp = jnp.sum(grad_mlp_input, axis=1)
@@ -403,7 +467,10 @@
         ],
         axis=0,
     )
-    attention_grad = contract_first(left, right).astype(BF16)
+    if joint:
+        joined = weight_grad(left, right, columns, 2 * columns, joined)
+    else:
+        attention_grad = contract_first(left, right).astype(BF16)
     grad_attn_input = core_total(project_rows(grad_projected, w_input), lay)
     grad_scale_att = jnp.sum(grad_attn_input * normed_att, axis=1)
     grad_shift_att = jnp.sum(grad_attn_input, axis=1)
@@ -428,7 +495,7 @@
         grad_mod,
         split_biases,
         whole_biases,
-        (attention_grad, expand_grad, reduce_grad),
+        (reduce_grad, joined) if joint else (attention_grad, expand_grad, reduce_grad),
     )
 
 
@@ -467,27 +534,23 @@
     return split_columns(whole, [part.shape[1] for part in parts])
 
 
-def sum_chips(grad):
-    return lax.psum_scatter(grad, "sp", scatter_dimension=0, tiled=True)
-
-
-def reduce_whole(grads):
+def reduce_joint(grads):
+    g_reduce, g_joined = grads
+    reduce = lax.psum_scatter(g_reduce, "sp", scatter_dimension=0, tiled=True)
+    summed = lax.psum_scatter(g_joined, "sp", scatter_dimension=0, tiled=True)
+    expand, attention = jnp.split(summed, 2, axis=1)
+    return (attention, expand, reduce)
+
+
+def reduce_weights(scatter, grads, first, second):
     g_attention, g_expand, g_reduce = grads
-    attention = sum_chips(g_attention)
-    count = g_attention.shape[1] * 3 // 4
-    return (attention[:, :count], attention[:, count:], sum_chips(g_expand), sum_chips(g_reduce))
-
-
-def reduce_weights(scatter, grads):
-    g_attention, g_expand, g_reduce = grads
-    reduce = scatter.chunk(g_reduce)
-    expand = scatter.chunk(g_expand)
-    attention = scatter.chunk(g_attention)
-    count = g_attention.shape[1] * 3 // 4
-    return (attention[:, :count], attention[:, count:], expand, reduce)
-
-
-def join_columns(parts, lay):
+    reduce, _, _ = scatter.chunk(g_reduce)
+    expand, _, _ = scatter.chunk(g_expand)
+    attention, first, second = scatter.chunk(g_attention, first, second)
+    return ((attention, expand, reduce), first, second)
+
+
+def join_any(parts, lay):
     g_input, g_output, g_expand, g_reduce = [
         cube_gather(part.astype(BF16), "dp", lay.cores).astype(F32) for part in parts
     ]
@@ -501,10 +564,81 @@
     )
 
 
+def join_call(body, widths, own, other, name):
+    rows = own.shape[0]
+    return pl.pallas_call(
+        body,
+        out_shape=[jax.ShapeDtypeStruct((rows, width), F32) for width in widths],
+        in_specs=[pl.BlockSpec(memory_space=pltpu.VMEM)] * 2,
+        out_specs=[pl.BlockSpec(memory_space=pltpu.VMEM)] * len(widths),
+        compiler_params=pltpu.CompilerParams(vmem_limit_bytes=24 << 20),
+        cost_estimate=pl.CostEstimate(
+            flops=0, transcendentals=0, bytes_accessed=2 * rows * sum(widths) * 4
+        ),
+        name=name,
+    )(own, other)
+
+
+def in_order(write):
+    core = lax.axis_index("dp")
+    for first in (0, 1):
+        pl.when(core == first)(partial(write, first, 1 - first))
+
+
+def join_pair(own):
+    own = own.astype(BF16)
+    columns = own.shape[1]
+
+    def body(own_ref, other_ref, out_ref):
+        def write(low, high):
+            refs = (own_ref, other_ref)
+            out_ref[:, :columns] = refs[low][...].astype(F32)
+            out_ref[:, columns:] = refs[high][...].astype(F32)
+
+        in_order(write)
+
+    return join_call(body, [2 * columns], own, flip(own, "dp", 2, 1), "join_pair")[0]
+
+
+def join_attention(own):
+    own = own.astype(BF16)
+    share = own.shape[1] // 4
+
+    def body(own_ref, other_ref, in_ref, out_ref):
+        def write(low, high):
+            refs = (own_ref, other_ref)
+            for place, which in ((0, low), (1, high)):
+                values = refs[which][...].astype(F32)
+                for k in range(3):
+                    start = (2 * k + place) * share
+                    in_ref[:, start : start + share] = values[:, k * share : (k + 1) * share]
+                out_ref[:, place * share : (place + 1) * share] = values[:, 3 * share :]
+
+        in_order(write)
+
+    return join_call(body, [6 * share, 2 * share], own, flip(own, "dp", 2, 1), "join_attention")
+
+
+def join_columns(sums, lay):
+    attention, expand, reduce = sums
+    if lay.cores == 2:
+        g_input, g_output = join_attention(attention)
+        return (g_input, g_output, join_pair(expand), join_pair(reduce))
+    count = attention.shape[1] * 3 // 4
+    return join_any((attention[:, :count], attention[:, count:], expand, reduce), lay)
+
+
+def swap_chips(values):
+    return lax.all_to_all(values, "sp", split_axis=0, concat_axis=0, tiled=True)
+
+
 def to_positions(values, clips, lay):
-    moved = lax.all_to_all(values, "sp", split_axis=1, concat_axis=0, tiled=True)
-    moved = moved.reshape(clips, -1, values.shape[-1])
-    return cube_gather(moved, "dp", lay.cores).reshape(-1, moved.shape[1], moved.shape[2])
+    frames, patches, width = values.shape
+    parts = jnp.transpose(
+        values.reshape(frames, lay.chips, patches // lay.chips, width), (1, 0, 2, 3)
+    )
+    moved = swap_chips(parts.reshape(lay.chips, -1, width)).reshape(clips, -1, width)
+    return cube_gather(moved, "dp", lay.cores).reshape(-1, moved.shape[1], width)
 
 
 def own_group(values, lay):
@@ -514,8 +648,10 @@
 
 def to_frames(values, frames_here, lay):
     own = own_group(values, lay)
-    own = own.reshape(frames_here * lay.chips, -1, values.shape[-1])
-    return lax.all_to_all(own, "sp", split_axis=0, concat_axis=1, tiled=True)
+    width = own.shape[-1]
+    moved = swap_chips(own.reshape(lay.chips, -1, width))
+    parts = jnp.transpose(moved.reshape(lay.chips, frames_here, -1, width), (1, 0, 2, 3))
+    return parts.reshape(frames_here, -1, width)
 
 
 def place_split(values, lay):
@@ -654,27 +790,36 @@
     block_input = (all_frames + positions[:, None]).reshape(-1, patches, width)
     frame_mod = jnp.repeat(spatial_mod, frame_count, axis=0)
 
+    exchanged_after = []
+
+    def exchange_cotangent(hidden):
+        hidden, moving = tie([hidden, cotangent], [])
+        hidden, moved = tie([hidden, to_positions(moving, clips_here, lay)], [])
+        exchanged_after.append(moved)
+        return hidden
+
     spatial_out, spatial_kept = block_forward(
-        block_input, frame_mod, spatial_weights, spatial_biases, 1, lay
-    )
+        block_input, frame_mod, spatial_weights, spatial_biases, 1, lay, exchange_cotangent
+    )
+    grad_after = exchanged_after[0]
     own_out = own_group(spatial_out.astype(BF16), lay)
     between = to_positions(own_out, clips_here, lay)
     local_patches = patches // chips
     temporal_out, temporal_kept = block_forward(
         between.astype(F32), temporal_mod, temporal_weights, temporal_biases, local_patches, lay
     )
-    activations = to_frames(temporal_out.astype(BF16), frame_count, lay)
-    grad_after = to_positions(cotangent, clips_here, lay)
     grad_between, temporal_dmod, temporal_split, temporal_whole, temporal_grads = block_backward(
-        grad_after.astype(F32), temporal_kept, temporal_mod, temporal_weights, local_patches, lay
-    )
-    temporal_sums = reduce_whole(temporal_grads)
+        grad_after.astype(F32), temporal_kept, temporal_mod, temporal_weights, local_patches, lay, True
+    )
+    temporal_sums = reduce_joint(temporal_grads)
     own_grad = to_frames(grad_between.astype(BF16), frame_count, lay)
     grad_frames = cube_gather(own_grad, "dp", cores).reshape(-1, patches, width)
     input_grad_all, frame_dmod, spatial_split, spatial_whole, spatial_grads = block_backward(
         grad_frames.astype(F32), spatial_kept, frame_mod, spatial_weights, 1, lay
     )
-    spatial_sums = reduce_weights(scatter, spatial_grads)
+    reduce_sums, input_grad_all, temporal_low = tie([temporal_sums[2], input_grad_all, temporal_out.astype(BF16)], [])
+    temporal_sums = temporal_sums[:2] + (reduce_sums,)
+    activations = to_frames(temporal_low, frame_count, lay)
     input_grad = own_group(input_grad_all, lay)
 
     grad_positions = jnp.sum(input_grad, axis=0)
@@ -719,6 +864,9 @@
         temporal_rows[3],
     )
     summed = cube_scatter(jnp.concatenate(rows, axis=1), "sp", chips)
+    spatial_sums, ready_first, ready_second = reduce_weights(
+        scatter, spatial_grads, [], []
+    )
     sums = split_columns(summed, [row.shape[1] for row in rows])
 
     mod_low = sums[5].reshape(clips, -1).astype(BF16)

time: 908 us -> 878 us (0.967)
  waiting for transfers between devices: 365 us -> 322 us
  Pallas kernels: 3.27 us -> 34.7 us
  other arithmetic: 123 us -> 113 us
    ppermute x58 -> x56, waiting for transfers between devices: 250 us -> 171 us  [flip(): return lax.ppermute(values, axis, [(i, i ^ bit) for i in range(size)])]
    ppermute x18, waiting for transfers between devices: 67.2 us -> 134 us  [turn(): lax.ppermute(values, 'sp', [(i, (i + 4 * offset) % count) for i in range(...]
    reduce_scatter x3 -> x2, waiting for transfers between devices: 36.8 us -> 0.01 us  [the longest x1 0.01 us: reduce_joint(): reduce = lax.psum_scatter(g_reduce, 'sp', scatter_dimension=0, tiled=True)]
    pallas_call x0 -> x8, Pallas kernels: none -> 26.5 us  [the longest x2 16.4 us: weight_grad(): pl.pallas_call(body, grid=(columns // tile,), in_specs=[fixed_spec(left),...]
    reshape x12 -> x0, local copies, waits for them, and re-layouts: 16.6 us -> none  [the longest x4 9.58 us: join_columns(): jnp.transpose(thirds, (1, 2, 0, 3)).reshape(rows, -1)]
    concatenate x4 -> x7, local copies, waits for them, and re-layouts: 2.67 us -> 17.5 us  [block_backward(): jnp.concatenate([grad_query, grad_key, grad_value], axis=-1)]
    unnamed x12 -> x10, other arithmetic: 14.1 us -> 1.22 us
    dot_general x11 -> x9, matrix products: 46.8 us -> 35.3 us  [contract_first(): lax.dot_general(left_rows, right_rows, (((0,), (0,)), ((), ())), preferre...]
  transfers between devices with their start and end apart: 84 -> 81, of which waited for: 35 -> 33; matrix products, arithmetic and copies ran while one was open for 39% -> 37% of each run, Pallas kernels for 0% -> 4%
where the time goes in v3:
time: 878 us; the launch traced here: 870 us
  waiting for transfers between devices  322 us (37%)
  matrix products  145 us (17%)
  local copies, waits for them, and re-layouts  125 us (14%)
  other arithmetic  113 us (13%)
  starting transfers between devices  111 us (13%)
  Pallas kernels  34.7 us (4%)
  between operations  19.6 us (2%)
    ppermute x56, waiting for transfers between devices, flip(): return lax.ppermute(values, axis, [(i, i ^ bit) for i in range(size)])  171 us
    ppermute x18, waiting for transfers between devices, turn(): lax.ppermute(values, 'sp', [(i, (i + 4 * offset) % count) for i in range(...  134 us
    dot_general x10, matrix products, project_rows(): lax.dot_general(left_rows, weight, (((left_rows.ndim - 1,), (1,)), ((), (...  48.7 us
    ppermute x56, starting transfers between devices, flip(): return lax.ppermute(values, axis, [(i, i ^ bit) for i in range(size)])  46 us
    ppermute x18, starting transfers between devices, turn(): lax.ppermute(values, 'sp', [(i, (i + 4 * offset) % count) for i in range(...  44.2 us
    dot_general x12, matrix products, project(): lax.dot_general(left_rows, weight, (((left_rows.ndim - 1,), (0,)), ((), (...  43.9 us
    dot_general x9, matrix products, contract_first(): lax.dot_general(left_rows, right_rows, (((0,), (0,)), ((), ())), preferre...  35.3 us
    unnamed x348, local copies, waits for them, and re-layouts  31.6 us
  transfers between devices with their start and end apart: 81, of which 33 were waited for; matrix products, arithmetic and copies ran while one was open for 37% of the time, Pallas kernels for 4%

profile of v3, /device:TPU:0, one launch (start us, length us, event | category | flops | bytes accessed | tf_op | source)
XLA Modules:
  0.0 869.6 jit_solution(14161833331695949654)
XLA Ops:
  51.7 16.3 %collective-permute-done.4 = f32[4,2880]{1,0:T(4,128)} collective-permute-done((f32[4,2880]{1,0:T(4,128)S(1)}, f32[4,2880]{1,0:T(4,128)}, u32[]{:S(2)}, u32[]{:S(2)}) %collective-permute-start.4) | collective-permute-done | bytes 46112 | tf_op jit(solution)/shard_map/ppermute | solution.py:72
  105.8 22.0 %collective-permute-done.10.y_ref = bf16[4,72,2304]{2,1,0:T(8,128)(2,1)} collective-permute-done((bf16[4,72,2304]{2,1,0:T(8,128)(2,1)}, bf16[4,72,2304]{2,1,0:T(8,128)(2,1)}, u32[]{:S(2)}, u32[]{:S(2)}) %collective-permute-start.10) | collective-permute-done | bytes 1327136 | tf_op jit(solution)/shard_map/ppermute | solution.py:72
  130.4 12.4 %collective-permute-done.9.x_ref = bf16[4,72,2304]{2,1,0:T(8,128)(2,1)} collective-permute-done((bf16[4,72,2304]{2,1,0:T(8,128)(2,1)}, bf16[4,72,2304]{2,1,0:T(8,128)(2,1)}, u32[]{:S(2)}, u32[]{:S(2)}) %collective-permute-start.9) | collective-permute-done | bytes 1327136 | tf_op jit(solution)/shard_map/ppermute | solution.py:72
  146.3 8.8 %collective-permute-done.16 = bf16[72,2304]{1,0:T(8,128)(2,1)S(1)} collective-permute-done((bf16[72,2304]{1,0:T(8,128)(2,1)S(1)}, bf16[72,2304]{1,0:T(8,128)(2,1)S(1)}, u32[]{:S(2)}, u32[]{:S(2)}) %collective-permute-start.16) | collective-permute-done | bytes 331808 | tf_op jit(solution)/shard_map/ppermute | solution.py:133
  176.9 21.1 %collective-permute-done.24 = bf16[72,2304]{1,0:T(8,128)(2,1)S(1)} collective-permute-done((bf16[72,2304]{1,0:T(8,128)(2,1)S(1)}, bf16[72,2304]{1,0:T(8,128)(2,1)S(1)}, u32[]{:S(2)}, u32[]{:S(2)}) %collective-permute-start.24) | collective-permute-done | bytes 331808 | tf_op jit(solution)/shard_map/ppermute | solution.py:133
  198.0 8.4 collective-permute-start.22
  207.8 34.0 %collective-permute-done.23 = bf16[72,2304]{1,0:T(8,128)(2,1)} collective-permute-done((bf16[72,2304]{1,0:T(8,128)(2,1)S(1)}, bf16[72,2304]{1,0:T(8,128)(2,1)}, u32[]{:S(2)}, u32[]{:S(2)}) %collective-permute-start.23) | collective-permute-done | bytes 331808 | tf_op jit(solution)/shard_map/ppermute | solution.py:133
  248.2 6.3 all-to-all-start
  261.9 19.7 %collective-permute-done.26.y_ref = bf16[4,72,2304]{2,1,0:T(8,128)(2,1)} collective-permute-done((bf16[4,72,2304]{2,1,0:T(8,128)(2,1)}, bf16[4,72,2304]{2,1,0:T(8,128)(2,1)}, u32[]{:S(2)}, u32[]{:S(2)}) %collective-permute-start.26) | collective-permute-done | bytes 1327136 | tf_op jit(solution)/shard_map/ppermute | solution.py:72
  287.5 9.7 %collective-permute-done.21.high_ref = bf16[4,72,1152]{2,1,0:T(8,128)(2,1)} collective-permute-done((bf16[4,72,1152]{2,1,0:T(8,128)(2,1)}, bf16[4,72,1152]{2,1,0:T(8,128)(2,1)}, u32[]{:S(2)}, u32[]{:S(2)}) %collective-permute-start.21) | collective-permute-done | bytes 663584 | tf_op jit(solution)/shard_map/ppermute | solution.py:72
  302.4 7.1 collective-permute-done.28.high_ref
  321.2 6.2 convolution_add_fusion.1
  345.1 16.3 %all-to-all-done.1 = bf16[16,16,1152]{2,1,0:T(8,128)(2,1)S(1)} async-done(((bf16[16,16,1152]{2,1,0:T(8,128)(2,1)}), bf16[16,16,1152]{2,1,0:T(8,128)(2,1)S(1)}, u32[]{:S(2)}, u32[]{:S(2)}) %all-to-all-start.1) | async-done | bytes 589856 | tf_op jit(solution)/shard_map/all_to_all | solution.py:632
  386.8 6.1 convolution_add_fusion
  401.5 7.9 fusion.19
  409.4 5.8 weight_grad.2.refs_0_
  415.3 10.7 %fusion.41 = bf16[2,256,1152]{2,1,0:T(8,128)(2,1)} fusion(bf16[2,256,2304]{2,1,0:T(8,128)(2,1)S(1)} %fusion.19, bf16[1152,6912]{1,0:T(8,128)(2,1)} %all-gather.2.cloned.1.call-done), kind=kOutput, calls=%fused_computation.83 | convolution fusion | flops 2718498816 | bytes 8847360 | tf_op jit(solution)/shard_map/dot_general | solution.py:45
  426.1 7.6 fusion.40
  438.7 6.0 fusion.44
  453.0 6.0 fusion.38
  515.2 10.6 %weight_grad.3 = bf16[1152,4608]{1,0:T(8,128)(2,1)} custom-call(bf16[1024,1152]{1,0:T(8,128)(2,1)S(1)} %copy-done.3, bf16[1024,2304]{1,0:T(8,128)(2,1)S(1)} %copy-done.2, bf16[1152,4608]{1,0:T(8,128)(2,1)} %copy-done.1), custom_call_target="tpu_custom_call", output_to_operand_aliasing={{}: (2, {})} | custom-call | flops 5435817984 | bytes 12386304 | tf_op jit(solution)/shard_map/weight_grad/pallas_call | solution.py:279
  533.2 8.2 fusion.2
  567.3 15.3 %collective-permute-done.48 = bf16[4,72,1152]{2,1,0:T(8,128)(2,1)S(1)} collective-permute-done((bf16[4,72,1152]{2,1,0:T(8,128)(2,1)S(1)}, bf16[4,72,1152]{2,1,0:T(8,128)(2,1)S(1)}, u32[]{:S(2)}, u32[]{:S(2)}) %collective-permute-start.48) | collective-permute-done | bytes 663584 | tf_op jit(solution)/shard_map/ppermute | solution.py:72
  621.4 6.4 convolution_convert_fusion
  635.7 12.8 %collective-permute-done.51 = bf16[4,72,2304]{2,1,0:T(8,128)(2,1)} collective-permute-done((bf16[4,72,2304]{2,1,0:T(8,128)(2,1)}, bf16[4,72,2304]{2,1,0:T(8,128)(2,1)}, u32[]{:S(2)}, u32[]{:S(2)}) %collective-permute-start.51) | collective-permute-done | bytes 1327136 | tf_op jit(solution)/shard_map/ppermute | solution.py:72
  656.3 7.0 collective-permute-done.57
  664.7 15.9 %collective-permute-done.56 = bf16[72,2304]{1,0:T(8,128)(2,1)S(1)} collective-permute-done((bf16[72,2304]{1,0:T(8,128)(2,1)S(1)}, bf16[72,2304]{1,0:T(8,128)(2,1)S(1)}, u32[]{:S(2)}, u32[]{:S(2)}) %collective-permute-start.56) | collective-permute-done | bytes 331808 | tf_op jit(solution)/shard_map/ppermute | solution.py:133
  688.2 20.5 %collective-permute-done.53 = bf16[4,72,1152]{2,1,0:T(8,128)(2,1)S(1)} collective-permute-done((bf16[4,72,1152]{2,1,0:T(8,128)(2,1)S(1)}, bf16[4,72,1152]{2,1,0:T(8,128)(2,1)S(1)}, u32[]{:S(2)}, u32[]{:S(2)}) %collective-permute-start.53) | collective-permute-done | bytes 663584 | tf_op jit(solution)/shard_map/ppermute | solution.py:72
  708.9 8.0 collective-permute-done.54
  730.1 6.1 collective-permute-start.67
  743.1 20.3 %collective-permute-done.67 = bf16[72,2304]{1,0:T(8,128)(2,1)} collective-permute-done((bf16[72,2304]{1,0:T(8,128)(2,1)}, bf16[72,2304]{1,0:T(8,128)(2,1)}, u32[]{:S(2)}, u32[]{:S(2)}) %collective-permute-start.67) | collective-permute-done | bytes 331808 | tf_op jit(solution)/shard_map/ppermute | solution.py:133
  782.6 21.7 %collective-permute-done.61 = bf16[72,2304]{1,0:T(8,128)(2,1)} collective-permute-done((bf16[72,2304]{1,0:T(8,128)(2,1)}, bf16[72,2304]{1,0:T(8,128)(2,1)}, u32[]{:S(2)}, u32[]{:S(2)}) %collective-permute-start.61) | collective-permute-done | bytes 331808 | tf_op jit(solution)/shard_map/ppermute | solution.py:133
  (806 shorter events, 458.7 us)
Async XLA Ops:
  7.2 358.9 %all-gather.2.cloned.1.call-start = ((), (), s32[]{:S(2)}) async-start(), calls=%async_computation.6 | async-start | bytes 16920576 | tf_op jit(solution)/shard_map/all_gather | solution.py:533
  22.6 68.5 %collective-permute-start.7 = (bf16[72,2304]{1,0:T(8,128)(2,1)}, bf16[72,2304]{1,0:T(8,128)(2,1)}, u32[]{:S(2)}, u32[]{:S(2)}) collective-permute-start(bf16[72,2304]{1,0:T(8,128)(2,1)} %pad_maximum_fusion.11), channel_id=1, source_target_pairs={{0,8},{1,9},{2,10},{3,11},{4,12},{5,13},{6,14},{7,15},{8,0},{9,1},... | collective-permute-start | bytes 995336 | tf_op jit(solution)/shard_map/ppermute | solution.py:133
  26.6 64.4 %collective-permute-start.6 = (bf16[72,2304]{1,0:T(8,128)(2,1)}, bf16[72,2304]{1,0:T(8,128)(2,1)}, u32[]{:S(2)}, u32[]{:S(2)}) collective-permute-start(bf16[72,2304]{1,0:T(8,128)(2,1)} %pad_maximum_fusion.11), channel_id=1, source_target_pairs={{0,4},{1,5},{2,6},{3,7},{4,8},{5,9},{6,10},{7,11},{8,12},{9,13},{1... | collective-permute-start | bytes 995336 | tf_op jit(solution)/shard_map/ppermute | solution.py:133
  28.2 62.9 %collective-permute-start.8 = (bf16[72,2304]{1,0:T(8,128)(2,1)}, bf16[72,2304]{1,0:T(8,128)(2,1)}, u32[]{:S(2)}, u32[]{:S(2)}) collective-permute-start(bf16[72,2304]{1,0:T(8,128)(2,1)} %pad_maximum_fusion.11), channel_id=1, source_target_pairs={{0,12},{1,13},{2,14},{3,15},{4,0},{5,1},{6,2},{7,3},{8,4},{9,5},{1... | collective-permute-start | bytes 995336 | tf_op jit(solution)/shard_map/ppermute | solution.py:133
  33.1 67.9 %collective-permute-start = (bf16[1,1,256,1152]{3,2,1,0:T(8,128)(2,1)}, bf16[1,1,256,1152]{3,2,1,0:T(8,128)(2,1)}, u32[]{:S(2)}, u32[]{:S(2)}) collective-permute-start(bf16[1,1,256,1152]{3,2,1,0:T(8,128)(2,1)} %bitcast.548), channel_id=1, source_target_pairs={{0,16},{16,0},{1,17},{17,1},{2,18},{18,2},{3,19},{19,3},{4,20},{20... | collective-permute-start | bytes 1769480 | tf_op jit(solution)/shard_map/ppermute | solution.py:72
  95.1 47.8 %collective-permute-start.9 = (bf16[4,72,2304]{2,1,0:T(8,128)(2,1)}, bf16[4,72,2304]{2,1,0:T(8,128)(2,1)}, u32[]{:S(2)}, u32[]{:S(2)}) collective-permute-start(bf16[4,72,2304]{2,1,0:T(8,128)(2,1)} %pad_maximum_fusion.1.held_ref), channel_id=1, source_target_pairs={{0,1},{1,0},{2,3},{3,2},{4,5},{5,4},{6,7},{7,6},{8,9},{9,8},{10,11... | collective-permute-start | bytes 3981320 | tf_op jit(solution)/shard_map/ppermute | solution.py:72
  97.5 48.8 %collective-permute-start.17 = (bf16[72,2304]{1,0:T(8,128)(2,1)S(1)}, bf16[72,2304]{1,0:T(8,128)(2,1)S(1)}, u32[]{:S(2)}, u32[]{:S(2)}) collective-permute-start(bf16[72,2304]{1,0:T(8,128)(2,1)S(1)} %constant_dynamic-slice_fusion.11), channel_id=1, source_target_pairs={{0,12},{1,13},{2,14},{3,15},{4,0},{5,1},{6,2},{7,3},{8,4},{9,5},{1... | collective-permute-start | bytes 995336 | tf_op jit(solution)/shard_map/ppermute | solution.py:133
  101.0 54.1 %collective-permute-start.16 = (bf16[72,2304]{1,0:T(8,128)(2,1)S(1)}, bf16[72,2304]{1,0:T(8,128)(2,1)S(1)}, u32[]{:S(2)}, u32[]{:S(2)}) collective-permute-start(bf16[72,2304]{1,0:T(8,128)(2,1)S(1)} %constant_dynamic-slice_fusion.11), channel_id=1, source_target_pairs={{0,8},{1,9},{2,10},{3,11},{4,12},{5,13},{6,14},{7,15},{8,0},{9,1},... | collective-permute-start | bytes 995336 | tf_op jit(solution)/shard_map/ppermute | solution.py:133
  101.0 54.1 %collective-permute-start.15 = (bf16[72,2304]{1,0:T(8,128)(2,1)S(1)}, bf16[72,2304]{1,0:T(8,128)(2,1)S(1)}, u32[]{:S(2)}, u32[]{:S(2)}) collective-permute-start(bf16[72,2304]{1,0:T(8,128)(2,1)S(1)} %constant_dynamic-slice_fusion.11), channel_id=1, source_target_pairs={{0,4},{1,5},{2,6},{3,7},{4,8},{5,9},{6,10},{7,11},{8,12},{9,13},{1... | collective-permute-start | bytes 995336 | tf_op jit(solution)/shard_map/ppermute | solution.py:133
  156.4 87.8 %collective-permute-start.19 = (bf16[4,72,2304]{2,1,0:T(8,128)(2,1)}, bf16[4,72,2304]{2,1,0:T(8,128)(2,1)}, u32[]{:S(2)}, u32[]{:S(2)}) collective-permute-start(bf16[4,72,2304]{2,1,0:T(8,128)(2,1)} %pad_maximum_fusion.2.held_ref), channel_id=1, source_target_pairs={{0,2},{1,3},{2,0},{3,1},{4,6},{5,7},{6,4},{7,5},{8,10},{9,11},{10,... | collective-permute-start | bytes 3981320 | tf_op jit(solution)/shard_map/ppermute | solution.py:72
  157.6 86.5 %collective-permute-start.18 = (bf16[4,72,2304]{2,1,0:T(8,128)(2,1)}, bf16[4,72,2304]{2,1,0:T(8,128)(2,1)}, u32[]{:S(2)}, u32[]{:S(2)}) collective-permute-start(bf16[4,72,2304]{2,1,0:T(8,128)(2,1)} %pad_maximum_fusion.2.held_ref), channel_id=1, source_target_pairs={{0,1},{1,0},{2,3},{3,2},{4,5},{5,4},{6,7},{7,6},{8,9},{9,8},{10,11... | collective-permute-start | bytes 3981320 | tf_op jit(solution)/shard_map/ppermute | solution.py:72
  171.4 73.1 %collective-permute-start.13 = (bf16[2,256,1152]{2,1,0:T(8,128)(2,1)}, bf16[2,256,1152]{2,1,0:T(8,128)(2,1)}, u32[]{:S(2)}, u32[]{:S(2)}) collective-permute-start(bf16[2,256,1152]{2,1,0:T(8,128)(2,1)} %convolution_convert_fusion.4), channel_id=1, source_target_pairs={{0,16},{16,0},{1,17},{17,1},{2,18},{18,2},{3,19},{19,3},{4,20},{20... | collective-permute-start | bytes 3538952 | tf_op jit(solution)/shard_map/ppermute | solution.py:72
  176.9 65.0 %collective-permute-start.23 = (bf16[72,2304]{1,0:T(8,128)(2,1)S(1)}, bf16[72,2304]{1,0:T(8,128)(2,1)}, u32[]{:S(2)}, u32[]{:S(2)}) collective-permute-start(bf16[72,2304]{1,0:T(8,128)(2,1)S(1)} %constant_dynamic-slice_fusion.10), channel_id=1, source_target_pairs={{0,8},{1,9},{2,10},{3,11},{4,12},{5,13},{6,14},{7,15},{8,0},{9,1},... | collective-permute-start | bytes 995336 | tf_op jit(solution)/shard_map/ppermute | solution.py:133
  198.0 43.9 %collective-permute-start.22 = (bf16[72,2304]{1,0:T(8,128)(2,1)S(1)}, bf16[72,2304]{1,0:T(8,128)(2,1)}, u32[]{:S(2)}, u32[]{:S(2)}) collective-permute-start(bf16[72,2304]{1,0:T(8,128)(2,1)S(1)} %constant_dynamic-slice_fusion.10), channel_id=1, source_target_pairs={{0,4},{1,5},{2,6},{3,7},{4,8},{5,9},{6,10},{7,11},{8,12},{9,13},{1... | collective-permute-start | bytes 995336 | tf_op jit(solution)/shard_map/ppermute | solution.py:133
  244.2 37.5 %collective-permute-start.26 = (bf16[4,72,2304]{2,1,0:T(8,128)(2,1)}, bf16[4,72,2304]{2,1,0:T(8,128)(2,1)}, u32[]{:S(2)}, u32[]{:S(2)}) collective-permute-start(bf16[4,72,2304]{2,1,0:T(8,128)(2,1)} %pad_maximum_fusion.3.held_ref), channel_id=1, source_target_pairs={{0,2},{1,3},{2,0},{3,1},{4,6},{5,7},{6,4},{7,5},{8,10},{9,11},{10,... | collective-permute-start | bytes 3981320 | tf_op jit(solution)/shard_map/ppermute | solution.py:72
  244.2 39.7 %collective-permute-start.25 = (bf16[4,72,2304]{2,1,0:T(8,128)(2,1)}, bf16[4,72,2304]{2,1,0:T(8,128)(2,1)}, u32[]{:S(2)}, u32[]{:S(2)}) collective-permute-start(bf16[4,72,2304]{2,1,0:T(8,128)(2,1)} %pad_maximum_fusion.3.held_ref), channel_id=1, source_target_pairs={{0,1},{1,0},{2,3},{3,2},{4,5},{5,4},{6,7},{7,6},{8,9},{9,8},{10,11... | collective-permute-start | bytes 3981320 | tf_op jit(solution)/shard_map/ppermute | solution.py:72
  248.2 37.7 %all-to-all-start = ((bf16[16,16,1152]{2,1,0:T(8,128)(2,1)}), bf16[16,16,1152]{2,1,0:T(8,128)(2,1)}, u32[]{:S(2)}, u32[]{:S(2)}) async-start(bf16[16,16,1152]{2,1,0:T(8,128)(2,1)} %bitcast.26), calls=%async_computation | async-start | bytes 1179648 | tf_op jit(solution)/shard_map/all_to_all | solution.py:632
  256.5 40.7 %collective-permute-start.21 = (bf16[4,72,1152]{2,1,0:T(8,128)(2,1)}, bf16[4,72,1152]{2,1,0:T(8,128)(2,1)}, u32[]{:S(2)}, u32[]{:S(2)}) collective-permute-start(bf16[4,72,1152]{2,1,0:T(8,128)(2,1)} %slice.237), channel_id=1, source_target_pairs={{0,1},{1,0},{2,3},{3,2},{4,5},{5,4},{6,7},{7,6},{8,9},{9,8},{10,11... | collective-permute-start | bytes 1990664 | tf_op jit(solution)/shard_map/ppermute | solution.py:72
  344.8 423.7 %reduce-scatter.3.cloned.1.call-start = ((), (), s32[]{:S(2)}) async-start(), calls=%async_computation.7 | async-start | bytes 5640192 | tf_op jit(solution)/shard_map/reduce_scatter | solution.py:539
  481.3 371.9 %reduce-scatter.5.cloned.1.call-start = ((), (), s32[]{:S(2)}) async-start(), calls=%async_computation.8 | async-start | bytes 11280384 | tf_op jit(solution)/shard_map/reduce_scatter | solution.py:540
  583.9 50.5 %collective-permute-start.49 = (bf16[4,72,1152]{2,1,0:T(8,128)(2,1)}, bf16[4,72,1152]{2,1,0:T(8,128)(2,1)}, u32[]{:S(2)}, u32[]{:S(2)}) collective-permute-start(bf16[4,72,1152]{2,1,0:T(8,128)(2,1)} %get-tuple-element.81), channel_id=1, source_target_pairs={{0,2},{1,3},{2,0},{3,1},{4,6},{5,7},{6,4},{7,5},{8,10},{9,11},{10,... | collective-permute-start | bytes 1990664 | tf_op jit(solution)/shard_map/ppermute | solution.py:72
  585.4 45.7 %collective-permute-start.50 = (bf16[4,72,1152]{2,1,0:T(8,128)(2,1)}, bf16[4,72,1152]{2,1,0:T(8,128)(2,1)}, u32[]{:S(2)}, u32[]{:S(2)}) collective-permute-start(bf16[4,72,1152]{2,1,0:T(8,128)(2,1)} %get-tuple-element.82), channel_id=1, source_target_pairs={{0,1},{1,0},{2,3},{3,2},{4,5},{5,4},{6,7},{7,6},{8,9},{9,8},{10,11... | collective-permute-start | bytes 1990664 | tf_op jit(solution)/shard_map/ppermute | solution.py:72
  587.4 61.2 %collective-permute-start.51 = (bf16[4,72,2304]{2,1,0:T(8,128)(2,1)}, bf16[4,72,2304]{2,1,0:T(8,128)(2,1)}, u32[]{:S(2)}, u32[]{:S(2)}) collective-permute-start(bf16[4,72,2304]{2,1,0:T(8,128)(2,1)} %pad_maximum_fusion.4), channel_id=1, source_target_pairs={{0,1},{1,0},{2,3},{3,2},{4,5},{5,4},{6,7},{7,6},{8,9},{9,8},{10,11... | collective-permute-start | bytes 3981320 | tf_op jit(solution)/shard_map/ppermute | solution.py:72
  590.1 59.4 %collective-permute-start.52 = (bf16[4,72,2304]{2,1,0:T(8,128)(2,1)}, bf16[4,72,2304]{2,1,0:T(8,128)(2,1)}, u32[]{:S(2)}, u32[]{:S(2)}) collective-permute-start(bf16[4,72,2304]{2,1,0:T(8,128)(2,1)} %pad_maximum_fusion.5), channel_id=1, source_target_pairs={{0,2},{1,3},{2,0},{3,1},{4,6},{5,7},{6,4},{7,5},{8,10},{9,11},{10,... | collective-permute-start | bytes 3981320 | tf_op jit(solution)/shard_map/ppermute | solution.py:72
  619.7 62.8 %collective-permute-start.36 = (bf16[2,256,1152]{2,1,0:T(8,128)(2,1)S(1)}, bf16[2,256,1152]{2,1,0:T(8,128)(2,1)S(1)}, u32[]{:S(2)}, u32[]{:S(2)}) collective-permute-start(bf16[2,256,1152]{2,1,0:T(8,128)(2,1)S(1)} %fusion.39), channel_id=1, source_target_pairs={{0,16},{16,0},{1,17},{17,1},{2,18},{18,2},{3,19},{19,3},{4,20},{20... | collective-permute-start | bytes 3538952 | tf_op jit(solution)/shard_map/ppermute | solution.py:72
  632.9 88.1 %collective-permute-start.65 = (bf16[4,72,2304]{2,1,0:T(8,128)(2,1)S(1)}, bf16[4,72,2304]{2,1,0:T(8,128)(2,1)S(1)}, u32[]{:S(2)}, u32[]{:S(2)}) collective-permute-start(bf16[4,72,2304]{2,1,0:T(8,128)(2,1)S(1)} %pad_maximum_fusion.9), channel_id=1, source_target_pairs={{0,2},{1,3},{2,0},{3,1},{4,6},{5,7},{6,4},{7,5},{8,10},{9,11},{10,... | collective-permute-start | bytes 3981320 | tf_op jit(solution)/shard_map/ppermute | solution.py:72
  663.3 57.8 %collective-permute-start.64 = (bf16[4,72,2304]{2,1,0:T(8,128)(2,1)S(1)}, bf16[4,72,2304]{2,1,0:T(8,128)(2,1)S(1)}, u32[]{:S(2)}, u32[]{:S(2)}) collective-permute-start(bf16[4,72,2304]{2,1,0:T(8,128)(2,1)S(1)} %pad_maximum_fusion.8), channel_id=1, source_target_pairs={{0,1},{1,0},{2,3},{3,2},{4,5},{5,4},{6,7},{7,6},{8,9},{9,8},{10,11... | collective-permute-start | bytes 3981320 | tf_op jit(solution)/shard_map/ppermute | solution.py:72
  719.4 44.1 %collective-permute-start.58 = (bf16[4,72,2304]{2,1,0:T(8,128)(2,1)}, bf16[4,72,2304]{2,1,0:T(8,128)(2,1)}, u32[]{:S(2)}, u32[]{:S(2)}) collective-permute-start(bf16[4,72,2304]{2,1,0:T(8,128)(2,1)} %pad_maximum_fusion.6), channel_id=1, source_target_pairs={{0,1},{1,0},{2,3},{3,2},{4,5},{5,4},{6,7},{7,6},{8,9},{9,8},{10,11... | collective-permute-start | bytes 3981320 | tf_op jit(solution)/shard_map/ppermute | solution.py:72
  719.4 44.1 %collective-permute-start.59 = (bf16[4,72,2304]{2,1,0:T(8,128)(2,1)}, bf16[4,72,2304]{2,1,0:T(8,128)(2,1)}, u32[]{:S(2)}, u32[]{:S(2)}) collective-permute-start(bf16[4,72,2304]{2,1,0:T(8,128)(2,1)} %pad_maximum_fusion.7), channel_id=1, source_target_pairs={{0,2},{1,3},{2,0},{3,1},{4,6},{5,7},{6,4},{7,5},{8,10},{9,11},{10,... | collective-permute-start | bytes 3981320 | tf_op jit(solution)/shard_map/ppermute | solution.py:72
  743.1 69.8 %collective-permute-start.70 = (bf16[72,2304]{1,0:T(8,128)(2,1)S(1)}, bf16[72,2304]{1,0:T(8,128)(2,1)}, u32[]{:S(2)}, u32[]{:S(2)}) collective-permute-start(bf16[72,2304]{1,0:T(8,128)(2,1)S(1)} %fusion.126.own_ref), channel_id=1, source_target_pairs={{0,16},{16,0},{1,17},{17,1},{2,18},{18,2},{3,19},{19,3},{4,20},{20... | collective-permute-start | bytes 995336 | tf_op jit(solution)/shard_map/ppermute | solution.py:72
  766.4 37.9 %collective-permute-start.61 = (bf16[72,2304]{1,0:T(8,128)(2,1)}, bf16[72,2304]{1,0:T(8,128)(2,1)}, u32[]{:S(2)}, u32[]{:S(2)}) collective-permute-start(bf16[72,2304]{1,0:T(8,128)(2,1)} %get-tuple-element.150), channel_id=1, source_target_pairs={{0,8},{1,9},{2,10},{3,11},{4,12},{5,13},{6,14},{7,15},{8,0},{9,1},... | collective-permute-start | bytes 995336 | tf_op jit(solution)/shard_map/ppermute | solution.py:133
  766.4 37.9 %collective-permute-start.60 = (bf16[72,2304]{1,0:T(8,128)(2,1)}, bf16[72,2304]{1,0:T(8,128)(2,1)}, u32[]{:S(2)}, u32[]{:S(2)}) collective-permute-start(bf16[72,2304]{1,0:T(8,128)(2,1)} %get-tuple-element.151), channel_id=1, source_target_pairs={{0,4},{1,5},{2,6},{3,7},{4,8},{5,9},{6,10},{7,11},{8,12},{9,13},{1... | collective-permute-start | bytes 995336 | tf_op jit(solution)/shard_map/ppermute | solution.py:133
  (213 other events, 2334.4 us)
Sparse Core Ops, SparseCore 0:
  17.0 272.1 all-gather.1
  401.6 141.8 reduce-scatter.2
  549.4 225.7 reduce-scatter.4

commit v4 on v3

--- a/solution.py
+++ b/solution.py
@@ -102,9 +102,10 @@
 
 def cube_scatter(values, axis, size):
     rank = lax.axis_index(axis)
-    for bit in reversed(bits_of(size)):
+    for bit in bits_of(size):
         upper = (rank & bit) != 0
-        low, high = values[:bit], values[bit:]
+        pairs = values.reshape((-1, 2) + values.shape[1:])
+        low, high = pairs[:, 0], pairs[:, 1]
         away = jnp.where(upper, low, high)
         kept = jnp.where(upper, high, low)
         values = kept + flip(away, axis, size, bit)

time: 878 us -> 872 us (level)
  waiting for transfers between devices: 322 us -> 305 us
    concatenate x1 -> x11, local copies, waits for them, and re-layouts: 1.21 us -> 10.5 us  [per_device(): summed = cube_scatter(jnp.concatenate(rows, axis=1), 'sp', chips)]
    ppermute x56, waiting for transfers between devices: 171 us -> 162 us  [flip(): return lax.ppermute(values, axis, [(i, i ^ bit) for i in range(size)])]
    unnamed x348 -> x349, local copies, waits for them, and re-layouts: 31.6 us -> 32.6 us
  transfers between devices with their start and end apart: 81 -> 81, of which waited for: 33 -> 32; matrix products, arithmetic and copies ran while one was open for 37% -> 37% of each run, Pallas kernels for 4% -> 4%
where the time goes in v4:
time: 872 us; the launch traced here: 864 us
  waiting for transfers between devices  305 us (35%)
  matrix products  145 us (17%)
  local copies, waits for them, and re-layouts  129 us (15%)
  other arithmetic  115 us (13%)
  starting transfers between devices  113 us (13%)
  Pallas kernels  37.6 us (4%)
  between operations  19.3 us (2%)
    ppermute x56, waiting for transfers between devices, flip(): return lax.ppermute(values, axis, [(i, i ^ bit) for i in range(size)])  162 us
    ppermute x18, waiting for transfers between devices, turn(): lax.ppermute(values, 'sp', [(i, (i + 4 * offset) % count) for i in range(...  127 us
    dot_general x10, matrix products, project_rows(): lax.dot_general(left_rows, weight, (((left_rows.ndim - 1,), (1,)), ((), (...  48.7 us
    ppermute x18, starting transfers between devices, turn(): lax.ppermute(values, 'sp', [(i, (i + 4 * offset) % count) for i in range(...  45.8 us
    ppermute x56, starting transfers between devices, flip(): return lax.ppermute(values, axis, [(i, i ^ bit) for i in range(size)])  45 us
    dot_general x12, matrix products, project(): lax.dot_general(left_rows, weight, (((left_rows.ndim - 1,), (0,)), ((), (...  43.9 us
    dot_general x9, matrix products, contract_first(): lax.dot_general(left_rows, right_rows, (((0,), (0,)), ((), ())), preferre...  35.5 us
    unnamed x349, local copies, waits for them, and re-layouts  32.6 us
  transfers between devices with their start and end apart: 81, of which 32 were waited for; matrix products, arithmetic and copies ran while one was open for 37% of the time, Pallas kernels for 4%

profile of v4, /device:TPU:0, one launch (start us, length us, event | category | flops | bytes accessed | tf_op | source)
XLA Modules:
  0.0 863.6 jit_solution(8943037011237055666)
XLA Ops:
  51.8 16.3 %collective-permute-done.4 = f32[4,2880]{1,0:T(4,128)} collective-permute-done((f32[4,2880]{1,0:T(4,128)S(1)}, f32[4,2880]{1,0:T(4,128)}, u32[]{:S(2)}, u32[]{:S(2)}) %collective-permute-start.4) | collective-permute-done | bytes 46112 | tf_op jit(solution)/shard_map/ppermute | solution.py:72
  105.5 22.3 %collective-permute-done.10.y_ref = bf16[4,72,2304]{2,1,0:T(8,128)(2,1)} collective-permute-done((bf16[4,72,2304]{2,1,0:T(8,128)(2,1)}, bf16[4,72,2304]{2,1,0:T(8,128)(2,1)}, u32[]{:S(2)}, u32[]{:S(2)}) %collective-permute-start.10) | collective-permute-done | bytes 1327136 | tf_op jit(solution)/shard_map/ppermute | solution.py:72
  130.4 12.4 %collective-permute-done.9.x_ref = bf16[4,72,2304]{2,1,0:T(8,128)(2,1)} collective-permute-done((bf16[4,72,2304]{2,1,0:T(8,128)(2,1)}, bf16[4,72,2304]{2,1,0:T(8,128)(2,1)}, u32[]{:S(2)}, u32[]{:S(2)}) %collective-permute-start.9) | collective-permute-done | bytes 1327136 | tf_op jit(solution)/shard_map/ppermute | solution.py:72
  146.3 8.8 %collective-permute-done.16 = bf16[72,2304]{1,0:T(8,128)(2,1)S(1)} collective-permute-done((bf16[72,2304]{1,0:T(8,128)(2,1)S(1)}, bf16[72,2304]{1,0:T(8,128)(2,1)S(1)}, u32[]{:S(2)}, u32[]{:S(2)}) %collective-permute-start.16) | collective-permute-done | bytes 331808 | tf_op jit(solution)/shard_map/ppermute | solution.py:134
  176.9 21.1 %collective-permute-done.24 = bf16[72,2304]{1,0:T(8,128)(2,1)S(1)} collective-permute-done((bf16[72,2304]{1,0:T(8,128)(2,1)S(1)}, bf16[72,2304]{1,0:T(8,128)(2,1)S(1)}, u32[]{:S(2)}, u32[]{:S(2)}) %collective-permute-start.24) | collective-permute-done | bytes 331808 | tf_op jit(solution)/shard_map/ppermute | solution.py:134
  198.0 8.4 collective-permute-start.22
  207.9 34.0 %collective-permute-done.23 = bf16[72,2304]{1,0:T(8,128)(2,1)} collective-permute-done((bf16[72,2304]{1,0:T(8,128)(2,1)S(1)}, bf16[72,2304]{1,0:T(8,128)(2,1)}, u32[]{:S(2)}, u32[]{:S(2)}) %collective-permute-start.23) | collective-permute-done | bytes 331808 | tf_op jit(solution)/shard_map/ppermute | solution.py:134
  248.2 6.4 all-to-all-start
  262.0 19.7 %collective-permute-done.26.y_ref = bf16[4,72,2304]{2,1,0:T(8,128)(2,1)} collective-permute-done((bf16[4,72,2304]{2,1,0:T(8,128)(2,1)}, bf16[4,72,2304]{2,1,0:T(8,128)(2,1)}, u32[]{:S(2)}, u32[]{:S(2)}) %collective-permute-start.26) | collective-permute-done | bytes 1327136 | tf_op jit(solution)/shard_map/ppermute | solution.py:72
  287.5 9.7 %collective-permute-done.21.high_ref = bf16[4,72,1152]{2,1,0:T(8,128)(2,1)} collective-permute-done((bf16[4,72,1152]{2,1,0:T(8,128)(2,1)}, bf16[4,72,1152]{2,1,0:T(8,128)(2,1)}, u32[]{:S(2)}, u32[]{:S(2)}) %collective-permute-start.21) | collective-permute-done | bytes 663584 | tf_op jit(solution)/shard_map/ppermute | solution.py:72
  302.3 7.1 collective-permute-done.28.high_ref
  321.2 6.2 convolution_add_fusion.1
  345.3 16.1 %all-to-all-done.1 = bf16[16,16,1152]{2,1,0:T(8,128)(2,1)S(1)} async-done(((bf16[16,16,1152]{2,1,0:T(8,128)(2,1)}), bf16[16,16,1152]{2,1,0:T(8,128)(2,1)S(1)}, u32[]{:S(2)}, u32[]{:S(2)}) %all-to-all-start.1) | async-done | bytes 589856 | tf_op jit(solution)/shard_map/all_to_all | solution.py:633
  386.9 5.9 convolution_add_fusion
  401.3 7.9 fusion.19
  415.1 10.6 %fusion.41 = bf16[2,256,1152]{2,1,0:T(8,128)(2,1)} fusion(bf16[2,256,2304]{2,1,0:T(8,128)(2,1)S(1)} %fusion.19, bf16[1152,6912]{1,0:T(8,128)(2,1)} %all-gather.2.cloned.1.call-done), kind=kOutput, calls=%fused_computation.83 | convolution fusion | flops 2718498816 | bytes 8847360 | tf_op jit(solution)/shard_map/dot_general | solution.py:45
  425.9 7.6 fusion.40
  438.5 6.2 fusion.44
  453.0 6.0 fusion.38
  517.5 10.6 %weight_grad.3 = bf16[1152,4608]{1,0:T(8,128)(2,1)} custom-call(bf16[1024,1152]{1,0:T(8,128)(2,1)S(1)} %copy-done.3, bf16[1024,2304]{1,0:T(8,128)(2,1)S(1)} %copy-done.2, bf16[1152,4608]{1,0:T(8,128)(2,1)} %copy-done.1), custom_call_target="tpu_custom_call", output_to_operand_aliasing={{}: (2, {})} | custom-call | flops 5435817984 | bytes 12386304 | tf_op jit(solution)/shard_map/weight_grad/pallas_call | solution.py:280
  533.1 8.2 fusion.2
  567.4 15.3 %collective-permute-done.48 = bf16[4,72,1152]{2,1,0:T(8,128)(2,1)S(1)} collective-permute-done((bf16[4,72,1152]{2,1,0:T(8,128)(2,1)S(1)}, bf16[4,72,1152]{2,1,0:T(8,128)(2,1)S(1)}, u32[]{:S(2)}, u32[]{:S(2)}) %collective-permute-start.48) | collective-permute-done | bytes 663584 | tf_op jit(solution)/shard_map/ppermute | solution.py:72
  622.4 6.5 convolution_convert_fusion
  636.8 11.9 %collective-permute-done.51 = bf16[4,72,2304]{2,1,0:T(8,128)(2,1)} collective-permute-done((bf16[4,72,2304]{2,1,0:T(8,128)(2,1)}, bf16[4,72,2304]{2,1,0:T(8,128)(2,1)}, u32[]{:S(2)}, u32[]{:S(2)}) %collective-permute-start.51) | collective-permute-done | bytes 1327136 | tf_op jit(solution)/shard_map/ppermute | solution.py:72
  656.6 7.4 collective-permute-done.57
  664.6 17.7 %collective-permute-done.56 = bf16[72,2304]{1,0:T(8,128)(2,1)S(1)} collective-permute-done((bf16[72,2304]{1,0:T(8,128)(2,1)S(1)}, bf16[72,2304]{1,0:T(8,128)(2,1)S(1)}, u32[]{:S(2)}, u32[]{:S(2)}) %collective-permute-start.56) | collective-permute-done | bytes 331808 | tf_op jit(solution)/shard_map/ppermute | solution.py:134
  691.8 17.1 %collective-permute-done.53 = bf16[4,72,1152]{2,1,0:T(8,128)(2,1)S(1)} collective-permute-done((bf16[4,72,1152]{2,1,0:T(8,128)(2,1)S(1)}, bf16[4,72,1152]{2,1,0:T(8,128)(2,1)S(1)}, u32[]{:S(2)}, u32[]{:S(2)}) %collective-permute-start.53) | collective-permute-done | bytes 663584 | tf_op jit(solution)/shard_map/ppermute | solution.py:72
  709.1 7.6 collective-permute-done.54
  728.7 6.8 collective-permute-start.67
  736.7 5.9 collective-permute-done.68
  742.5 17.9 %collective-permute-done.67 = bf16[72,2304]{1,0:T(8,128)(2,1)} collective-permute-done((bf16[72,2304]{1,0:T(8,128)(2,1)}, bf16[72,2304]{1,0:T(8,128)(2,1)}, u32[]{:S(2)}, u32[]{:S(2)}) %collective-permute-start.67) | collective-permute-done | bytes 331808 | tf_op jit(solution)/shard_map/ppermute | solution.py:134
  781.6 14.4 %collective-permute-done.61 = bf16[72,2304]{1,0:T(8,128)(2,1)} collective-permute-done((bf16[72,2304]{1,0:T(8,128)(2,1)}, bf16[72,2304]{1,0:T(8,128)(2,1)}, u32[]{:S(2)}, u32[]{:S(2)}) %collective-permute-start.61) | collective-permute-done | bytes 331808 | tf_op jit(solution)/shard_map/ppermute | solution.py:134
  (811 shorter events, 464.6 us)
Async XLA Ops:
  7.2 358.9 %all-gather.2.cloned.1.call-start = ((), (), s32[]{:S(2)}) async-start(), calls=%async_computation.6 | async-start | bytes 16920576 | tf_op jit(solution)/shard_map/all_gather | solution.py:534
  22.6 68.5 %collective-permute-start.7 = (bf16[72,2304]{1,0:T(8,128)(2,1)}, bf16[72,2304]{1,0:T(8,128)(2,1)}, u32[]{:S(2)}, u32[]{:S(2)}) collective-permute-start(bf16[72,2304]{1,0:T(8,128)(2,1)} %pad_maximum_fusion.11), channel_id=1, source_target_pairs={{0,8},{1,9},{2,10},{3,11},{4,12},{5,13},{6,14},{7,15},{8,0},{9,1},... | collective-permute-start | bytes 995336 | tf_op jit(solution)/shard_map/ppermute | solution.py:134
  26.6 64.4 %collective-permute-start.6 = (bf16[72,2304]{1,0:T(8,128)(2,1)}, bf16[72,2304]{1,0:T(8,128)(2,1)}, u32[]{:S(2)}, u32[]{:S(2)}) collective-permute-start(bf16[72,2304]{1,0:T(8,128)(2,1)} %pad_maximum_fusion.11), channel_id=1, source_target_pairs={{0,4},{1,5},{2,6},{3,7},{4,8},{5,9},{6,10},{7,11},{8,12},{9,13},{1... | collective-permute-start | bytes 995336 | tf_op jit(solution)/shard_map/ppermute | solution.py:134
  28.2 62.9 %collective-permute-start.8 = (bf16[72,2304]{1,0:T(8,128)(2,1)}, bf16[72,2304]{1,0:T(8,128)(2,1)}, u32[]{:S(2)}, u32[]{:S(2)}) collective-permute-start(bf16[72,2304]{1,0:T(8,128)(2,1)} %pad_maximum_fusion.11), channel_id=1, source_target_pairs={{0,12},{1,13},{2,14},{3,15},{4,0},{5,1},{6,2},{7,3},{8,4},{9,5},{1... | collective-permute-start | bytes 995336 | tf_op jit(solution)/shard_map/ppermute | solution.py:134
  33.1 67.9 %collective-permute-start = (bf16[1,1,256,1152]{3,2,1,0:T(8,128)(2,1)}, bf16[1,1,256,1152]{3,2,1,0:T(8,128)(2,1)}, u32[]{:S(2)}, u32[]{:S(2)}) collective-permute-start(bf16[1,1,256,1152]{3,2,1,0:T(8,128)(2,1)} %bitcast.580), channel_id=1, source_target_pairs={{0,16},{16,0},{1,17},{17,1},{2,18},{18,2},{3,19},{19,3},{4,20},{20... | collective-permute-start | bytes 1769480 | tf_op jit(solution)/shard_map/ppermute | solution.py:72
  95.1 47.8 %collective-permute-start.9 = (bf16[4,72,2304]{2,1,0:T(8,128)(2,1)}, bf16[4,72,2304]{2,1,0:T(8,128)(2,1)}, u32[]{:S(2)}, u32[]{:S(2)}) collective-permute-start(bf16[4,72,2304]{2,1,0:T(8,128)(2,1)} %pad_maximum_fusion.1.held_ref), channel_id=1, source_target_pairs={{0,1},{1,0},{2,3},{3,2},{4,5},{5,4},{6,7},{7,6},{8,9},{9,8},{10,11... | collective-permute-start | bytes 3981320 | tf_op jit(solution)/shard_map/ppermute | solution.py:72
  97.5 48.8 %collective-permute-start.17 = (bf16[72,2304]{1,0:T(8,128)(2,1)S(1)}, bf16[72,2304]{1,0:T(8,128)(2,1)S(1)}, u32[]{:S(2)}, u32[]{:S(2)}) collective-permute-start(bf16[72,2304]{1,0:T(8,128)(2,1)S(1)} %constant_dynamic-slice_fusion.11), channel_id=1, source_target_pairs={{0,12},{1,13},{2,14},{3,15},{4,0},{5,1},{6,2},{7,3},{8,4},{9,5},{1... | collective-permute-start | bytes 995336 | tf_op jit(solution)/shard_map/ppermute | solution.py:134
  101.0 54.1 %collective-permute-start.16 = (bf16[72,2304]{1,0:T(8,128)(2,1)S(1)}, bf16[72,2304]{1,0:T(8,128)(2,1)S(1)}, u32[]{:S(2)}, u32[]{:S(2)}) collective-permute-start(bf16[72,2304]{1,0:T(8,128)(2,1)S(1)} %constant_dynamic-slice_fusion.11), channel_id=1, source_target_pairs={{0,8},{1,9},{2,10},{3,11},{4,12},{5,13},{6,14},{7,15},{8,0},{9,1},... | collective-permute-start | bytes 995336 | tf_op jit(solution)/shard_map/ppermute | solution.py:134
  101.0 54.1 %collective-permute-start.15 = (bf16[72,2304]{1,0:T(8,128)(2,1)S(1)}, bf16[72,2304]{1,0:T(8,128)(2,1)S(1)}, u32[]{:S(2)}, u32[]{:S(2)}) collective-permute-start(bf16[72,2304]{1,0:T(8,128)(2,1)S(1)} %constant_dynamic-slice_fusion.11), channel_id=1, source_target_pairs={{0,4},{1,5},{2,6},{3,7},{4,8},{5,9},{6,10},{7,11},{8,12},{9,13},{1... | collective-permute-start | bytes 995336 | tf_op jit(solution)/shard_map/ppermute | solution.py:134
  156.3 87.8 %collective-permute-start.19 = (bf16[4,72,2304]{2,1,0:T(8,128)(2,1)}, bf16[4,72,2304]{2,1,0:T(8,128)(2,1)}, u32[]{:S(2)}, u32[]{:S(2)}) collective-permute-start(bf16[4,72,2304]{2,1,0:T(8,128)(2,1)} %pad_maximum_fusion.2.held_ref), channel_id=1, source_target_pairs={{0,2},{1,3},{2,0},{3,1},{4,6},{5,7},{6,4},{7,5},{8,10},{9,11},{10,... | collective-permute-start | bytes 3981320 | tf_op jit(solution)/shard_map/ppermute | solution.py:72
  157.6 86.5 %collective-permute-start.18 = (bf16[4,72,2304]{2,1,0:T(8,128)(2,1)}, bf16[4,72,2304]{2,1,0:T(8,128)(2,1)}, u32[]{:S(2)}, u32[]{:S(2)}) collective-permute-start(bf16[4,72,2304]{2,1,0:T(8,128)(2,1)} %pad_maximum_fusion.2.held_ref), channel_id=1, source_target_pairs={{0,1},{1,0},{2,3},{3,2},{4,5},{5,4},{6,7},{7,6},{8,9},{9,8},{10,11... | collective-permute-start | bytes 3981320 | tf_op jit(solution)/shard_map/ppermute | solution.py:72
  171.5 73.1 %collective-permute-start.13 = (bf16[2,256,1152]{2,1,0:T(8,128)(2,1)}, bf16[2,256,1152]{2,1,0:T(8,128)(2,1)}, u32[]{:S(2)}, u32[]{:S(2)}) collective-permute-start(bf16[2,256,1152]{2,1,0:T(8,128)(2,1)} %convolution_convert_fusion.4), channel_id=1, source_target_pairs={{0,16},{16,0},{1,17},{17,1},{2,18},{18,2},{3,19},{19,3},{4,20},{20... | collective-permute-start | bytes 3538952 | tf_op jit(solution)/shard_map/ppermute | solution.py:72
  176.9 64.9 %collective-permute-start.23 = (bf16[72,2304]{1,0:T(8,128)(2,1)S(1)}, bf16[72,2304]{1,0:T(8,128)(2,1)}, u32[]{:S(2)}, u32[]{:S(2)}) collective-permute-start(bf16[72,2304]{1,0:T(8,128)(2,1)S(1)} %constant_dynamic-slice_fusion.10), channel_id=1, source_target_pairs={{0,8},{1,9},{2,10},{3,11},{4,12},{5,13},{6,14},{7,15},{8,0},{9,1},... | collective-permute-start | bytes 995336 | tf_op jit(solution)/shard_map/ppermute | solution.py:134
  198.0 43.9 %collective-permute-start.22 = (bf16[72,2304]{1,0:T(8,128)(2,1)S(1)}, bf16[72,2304]{1,0:T(8,128)(2,1)}, u32[]{:S(2)}, u32[]{:S(2)}) collective-permute-start(bf16[72,2304]{1,0:T(8,128)(2,1)S(1)} %constant_dynamic-slice_fusion.10), channel_id=1, source_target_pairs={{0,4},{1,5},{2,6},{3,7},{4,8},{5,9},{6,10},{7,11},{8,12},{9,13},{1... | collective-permute-start | bytes 995336 | tf_op jit(solution)/shard_map/ppermute | solution.py:134
  244.1 37.5 %collective-permute-start.26 = (bf16[4,72,2304]{2,1,0:T(8,128)(2,1)}, bf16[4,72,2304]{2,1,0:T(8,128)(2,1)}, u32[]{:S(2)}, u32[]{:S(2)}) collective-permute-start(bf16[4,72,2304]{2,1,0:T(8,128)(2,1)} %pad_maximum_fusion.3.held_ref), channel_id=1, source_target_pairs={{0,2},{1,3},{2,0},{3,1},{4,6},{5,7},{6,4},{7,5},{8,10},{9,11},{10,... | collective-permute-start | bytes 3981320 | tf_op jit(solution)/shard_map/ppermute | solution.py:72
  244.2 39.7 %collective-permute-start.25 = (bf16[4,72,2304]{2,1,0:T(8,128)(2,1)}, bf16[4,72,2304]{2,1,0:T(8,128)(2,1)}, u32[]{:S(2)}, u32[]{:S(2)}) collective-permute-start(bf16[4,72,2304]{2,1,0:T(8,128)(2,1)} %pad_maximum_fusion.3.held_ref), channel_id=1, source_target_pairs={{0,1},{1,0},{2,3},{3,2},{4,5},{5,4},{6,7},{7,6},{8,9},{9,8},{10,11... | collective-permute-start | bytes 3981320 | tf_op jit(solution)/shard_map/ppermute | solution.py:72
  248.2 37.7 %all-to-all-start = ((bf16[16,16,1152]{2,1,0:T(8,128)(2,1)}), bf16[16,16,1152]{2,1,0:T(8,128)(2,1)}, u32[]{:S(2)}, u32[]{:S(2)}) async-start(bf16[16,16,1152]{2,1,0:T(8,128)(2,1)} %bitcast.26), calls=%async_computation | async-start | bytes 1179648 | tf_op jit(solution)/shard_map/all_to_all | solution.py:633
  256.5 40.6 %collective-permute-start.21 = (bf16[4,72,1152]{2,1,0:T(8,128)(2,1)}, bf16[4,72,1152]{2,1,0:T(8,128)(2,1)}, u32[]{:S(2)}, u32[]{:S(2)}) collective-permute-start(bf16[4,72,1152]{2,1,0:T(8,128)(2,1)} %slice.237), channel_id=1, source_target_pairs={{0,1},{1,0},{2,3},{3,2},{4,5},{5,4},{6,7},{7,6},{8,9},{9,8},{10,11... | collective-permute-start | bytes 1990664 | tf_op jit(solution)/shard_map/ppermute | solution.py:72
  260.5 36.6 %collective-permute-start.20 = (bf16[4,72,1152]{2,1,0:T(8,128)(2,1)}, bf16[4,72,1152]{2,1,0:T(8,128)(2,1)}, u32[]{:S(2)}, u32[]{:S(2)}) collective-permute-start(bf16[4,72,1152]{2,1,0:T(8,128)(2,1)} %slice.236), channel_id=1, source_target_pairs={{0,2},{1,3},{2,0},{3,1},{4,6},{5,7},{6,4},{7,5},{8,10},{9,11},{10,... | collective-permute-start | bytes 1990664 | tf_op jit(solution)/shard_map/ppermute | solution.py:72
  344.8 423.2 %reduce-scatter.3.cloned.1.call-start = ((), (), s32[]{:S(2)}) async-start(), calls=%async_computation.7 | async-start | bytes 5640192 | tf_op jit(solution)/shard_map/reduce_scatter | solution.py:540
  490.6 356.9 %reduce-scatter.5.cloned.1.call-start = ((), (), s32[]{:S(2)}) async-start(), calls=%async_computation.8 | async-start | bytes 11280384 | tf_op jit(solution)/shard_map/reduce_scatter | solution.py:541
  584.0 51.5 %collective-permute-start.49 = (bf16[4,72,1152]{2,1,0:T(8,128)(2,1)}, bf16[4,72,1152]{2,1,0:T(8,128)(2,1)}, u32[]{:S(2)}, u32[]{:S(2)}) collective-permute-start(bf16[4,72,1152]{2,1,0:T(8,128)(2,1)} %get-tuple-element.81), channel_id=1, source_target_pairs={{0,2},{1,3},{2,0},{3,1},{4,6},{5,7},{6,4},{7,5},{8,10},{9,11},{10,... | collective-permute-start | bytes 1990664 | tf_op jit(solution)/shard_map/ppermute | solution.py:72
  585.5 46.2 %collective-permute-start.50 = (bf16[4,72,1152]{2,1,0:T(8,128)(2,1)}, bf16[4,72,1152]{2,1,0:T(8,128)(2,1)}, u32[]{:S(2)}, u32[]{:S(2)}) collective-permute-start(bf16[4,72,1152]{2,1,0:T(8,128)(2,1)} %get-tuple-element.82), channel_id=1, source_target_pairs={{0,1},{1,0},{2,3},{3,2},{4,5},{5,4},{6,7},{7,6},{8,9},{9,8},{10,11... | collective-permute-start | bytes 1990664 | tf_op jit(solution)/shard_map/ppermute | solution.py:72
  587.4 61.3 %collective-permute-start.51 = (bf16[4,72,2304]{2,1,0:T(8,128)(2,1)}, bf16[4,72,2304]{2,1,0:T(8,128)(2,1)}, u32[]{:S(2)}, u32[]{:S(2)}) collective-permute-start(bf16[4,72,2304]{2,1,0:T(8,128)(2,1)} %pad_maximum_fusion.4), channel_id=1, source_target_pairs={{0,1},{1,0},{2,3},{3,2},{4,5},{5,4},{6,7},{7,6},{8,9},{9,8},{10,11... | collective-permute-start | bytes 3981320 | tf_op jit(solution)/shard_map/ppermute | solution.py:72
  590.2 59.4 %collective-permute-start.52 = (bf16[4,72,2304]{2,1,0:T(8,128)(2,1)}, bf16[4,72,2304]{2,1,0:T(8,128)(2,1)}, u32[]{:S(2)}, u32[]{:S(2)}) collective-permute-start(bf16[4,72,2304]{2,1,0:T(8,128)(2,1)} %pad_maximum_fusion.5), channel_id=1, source_target_pairs={{0,2},{1,3},{2,0},{3,1},{4,6},{5,7},{6,4},{7,5},{8,10},{9,11},{10,... | collective-permute-start | bytes 3981320 | tf_op jit(solution)/shard_map/ppermute | solution.py:72
  620.6 65.1 %collective-permute-start.36 = (bf16[2,256,1152]{2,1,0:T(8,128)(2,1)S(1)}, bf16[2,256,1152]{2,1,0:T(8,128)(2,1)S(1)}, u32[]{:S(2)}, u32[]{:S(2)}) collective-permute-start(bf16[2,256,1152]{2,1,0:T(8,128)(2,1)S(1)} %fusion.39), channel_id=1, source_target_pairs={{0,16},{16,0},{1,17},{17,1},{2,18},{18,2},{3,19},{19,3},{4,20},{20... | collective-permute-start | bytes 3538952 | tf_op jit(solution)/shard_map/ppermute | solution.py:72
  634.1 87.0 %collective-permute-start.65 = (bf16[4,72,2304]{2,1,0:T(8,128)(2,1)S(1)}, bf16[4,72,2304]{2,1,0:T(8,128)(2,1)S(1)}, u32[]{:S(2)}, u32[]{:S(2)}) collective-permute-start(bf16[4,72,2304]{2,1,0:T(8,128)(2,1)S(1)} %pad_maximum_fusion.9), channel_id=1, source_target_pairs={{0,2},{1,3},{2,0},{3,1},{4,6},{5,7},{6,4},{7,5},{8,10},{9,11},{10,... | collective-permute-start | bytes 3981320 | tf_op jit(solution)/shard_map/ppermute | solution.py:72
  664.0 57.1 %collective-permute-start.64 = (bf16[4,72,2304]{2,1,0:T(8,128)(2,1)S(1)}, bf16[4,72,2304]{2,1,0:T(8,128)(2,1)S(1)}, u32[]{:S(2)}, u32[]{:S(2)}) collective-permute-start(bf16[4,72,2304]{2,1,0:T(8,128)(2,1)S(1)} %pad_maximum_fusion.8), channel_id=1, source_target_pairs={{0,1},{1,0},{2,3},{3,2},{4,5},{5,4},{6,7},{7,6},{8,9},{9,8},{10,11... | collective-permute-start | bytes 3981320 | tf_op jit(solution)/shard_map/ppermute | solution.py:72
  719.1 41.3 %collective-permute-start.58 = (bf16[4,72,2304]{2,1,0:T(8,128)(2,1)}, bf16[4,72,2304]{2,1,0:T(8,128)(2,1)}, u32[]{:S(2)}, u32[]{:S(2)}) collective-permute-start(bf16[4,72,2304]{2,1,0:T(8,128)(2,1)} %pad_maximum_fusion.6), channel_id=1, source_target_pairs={{0,1},{1,0},{2,3},{3,2},{4,5},{5,4},{6,7},{7,6},{8,9},{9,8},{10,11... | collective-permute-start | bytes 3981320 | tf_op jit(solution)/shard_map/ppermute | solution.py:72
  720.0 40.4 %collective-permute-start.59 = (bf16[4,72,2304]{2,1,0:T(8,128)(2,1)}, bf16[4,72,2304]{2,1,0:T(8,128)(2,1)}, u32[]{:S(2)}, u32[]{:S(2)}) collective-permute-start(bf16[4,72,2304]{2,1,0:T(8,128)(2,1)} %pad_maximum_fusion.7), channel_id=1, source_target_pairs={{0,2},{1,3},{2,0},{3,1},{4,6},{5,7},{6,4},{7,5},{8,10},{9,11},{10,... | collective-permute-start | bytes 3981320 | tf_op jit(solution)/shard_map/ppermute | solution.py:72
  742.5 60.9 %collective-permute-start.70 = (bf16[72,2304]{1,0:T(8,128)(2,1)S(1)}, bf16[72,2304]{1,0:T(8,128)(2,1)}, u32[]{:S(2)}, u32[]{:S(2)}) collective-permute-start(bf16[72,2304]{1,0:T(8,128)(2,1)S(1)} %fusion.126.own_ref), channel_id=1, source_target_pairs={{0,16},{16,0},{1,17},{17,1},{2,18},{18,2},{3,19},{19,3},{4,20},{20... | collective-permute-start | bytes 995336 | tf_op jit(solution)/shard_map/ppermute | solution.py:72
  812.1 38.5 %all-to-all-start.3 = ((bf16[16,16,1152]{2,1,0:T(8,128)(2,1)}), bf16[16,16,1152]{2,1,0:T(8,128)(2,1)}, u32[]{:S(2)}, u32[]{:S(2)}) async-start(bf16[16,16,1152]{2,1,0:T(8,128)(2,1)} %bitcast.567), calls=%async_computation.4 | async-start | bytes 1179648 | tf_op jit(solution)/shard_map/all_to_all | solution.py:633
  (212 other events, 2311.5 us)
Sparse Core Ops, SparseCore 0:
  17.0 272.0 all-gather.1
  401.4 141.0 reduce-scatter.2
  548.4 222.8 reduce-scatter.4
